TPU v7x, 128 devices: a whole 4x4x4 slice. The times are simulated.
128 devices in a mesh: row: 8 (over z, core), col: 16 (over x, y).
Axes of the slice: x: 4, y: 4, z: 4, core: 2. Of those that a mesh axis runs over, the one named last changes fastest.
Arguments:
- rate_terms: bfloat16 [6, 8192, 8192], P(None, 'row', 'col'), may hold values from -1 to 1
- populations: float32 [8192, 256], P(('row', 'col')), may hold values from 0.05 to 1
- temp_bins: int32 [256], replicated, may hold values from 0 to 63
- bin_coeffs: float32 [64, 6], replicated, may hold values from -1 to 1
Outputs:
- updated: float32 [8192, 256], P(('row', 'col'))
All inputs are finite; a program needn't handle non-finite values.
Results may differ from a plain program's by a relative error of at most 0.0011.
Values may be sent and summed in bfloat16 or wider, within the bound.
No kernel may reach another device: no remote copies, remote signals or barrier semaphores. Data moves between devices by JAX's collectives and lax.ppermute only.
A program may use at most 64 MiB of HBM per device.

v0:
```python
import math

import jax
import jax.numpy as jnp
from jax import lax
from jax.sharding import PartitionSpec as P

KRYLOV = 4
TAYLOR = 8


epsilon = 1e-06
step_size = 1.0


def body(rate_terms, populations, temp_bins, bin_coeffs):
    col_id = lax.axis_index("col")
    n_terms = rate_terms.shape[0]
    row_rows = rate_terms.shape[1]
    col_rows = rate_terms.shape[2]
    n_bins = bin_coeffs.shape[0]
    n_cells = populations.shape[1]
    onehot = (temp_bins[:, None] == jnp.arange(n_bins, dtype=jnp.int32)[None, :]).astype(
        jnp.float32
    )
    weights = jnp.dot(onehot, bin_coeffs, precision=lax.Precision.HIGHEST)
    weights_t = weights.T
    stacked = rate_terms.reshape(n_terms * row_rows, col_rows)

    def apply_rates(vector):
        rounded = vector.astype(jnp.bfloat16)
        gathered = lax.all_gather(rounded, ("row", "col"), axis=0, tiled=True)
        operand = lax.dynamic_slice_in_dim(gathered, col_id * col_rows, col_rows, 0)
        products = jnp.dot(stacked, operand, preferred_element_type=jnp.float32).reshape(
            n_terms, row_rows, n_cells
        )
        partial_value = jnp.sum(products * weights_t[:, None, :], axis=0)
        return lax.psum_scatter(partial_value, "col", scatter_dimension=0, tiled=True)

    def norm_of(vector):
        squares = lax.psum(jnp.sum(vector * vector, axis=0), ("row", "col"))
        return jnp.sqrt(squares + epsilon)

    force = apply_rates(populations)
    scale_norm = norm_of(force)
    basis = [force / scale_norm[None, :]]
    zero_row = jnp.zeros((n_cells,), jnp.float32)
    hessen = [[zero_row for j in range(KRYLOV)] for i in range(KRYLOV)]
    for j in range(KRYLOV):
        fresh = apply_rates(basis[j])
        for i in range(j + 1):
            correlation = lax.psum(jnp.sum(basis[i] * fresh, axis=0), ("row", "col"))
            fresh = fresh - correlation[None, :] * basis[i]
            hessen[i][j] = correlation
        if j < KRYLOV - 1:
            length = norm_of(fresh)
            hessen[j + 1][j] = length
            basis.append(fresh / length[None, :])
    hmat = jnp.stack([jnp.stack(line) for line in hessen]) * step_size
    first_unit = jnp.zeros((KRYLOV, n_cells), jnp.float32).at[0].set(1.0)
    coeffs = first_unit / float(math.factorial(TAYLOR + 1))
    for k in range(TAYLOR - 1, -1, -1):
        coeffs = jnp.sum(hmat * coeffs[None, :, :], axis=1) + first_unit / float(
            math.factorial(k + 1)
        )
    update = jnp.zeros(populations.shape, jnp.float32)
    for i in range(KRYLOV):
        update = update + coeffs[i][None, :] * basis[i]
    return populations + step_size * scale_norm[None, :] * update


def solution(mesh):
    placed = (P(None, "row", "col"), P(("row", "col"), None), P(), P())
    return jax.shard_map(
        body, mesh=mesh, in_specs=placed, out_specs=P(("row", "col"), None), check_vma=False
    )
```

profile of v0, /device:TPU:0, one launch (start us, length us, event | category | flops | bytes accessed | tf_op | source)
XLA Modules:
  0.0 1695.8 jit_solution(16298154041316169169)
XLA Ops:
  9.0 70.6 %all-gather.6.cloned.1.call-done = bf16[8192,256]{1,0:T(8,128)(2,1)} async-done(((bf16[64,256]{1,0:T(8,128)(2,1)}), bf16[8192,256]{1,0:T(8,128)(2,1)}) %all-gather.6.cloned.1.call-update) | async-done | bytes 4194320 | tf_op jit(solution)/shard_map/all_gather | solution.py:32
  79.5 7.4 convolution_bitcast_fusion.4
  86.9 6.5 copy.11
  97.9 71.6 %reduce-scatter.6.cloned.1.call-done = f32[64,256]{1,0:T(8,128)} async-done(((f32[1024,256]{1,0:T(8,128)}), f32[64,256]{1,0:T(8,128)}) %reduce-scatter.6.cloned.1.call-update) | async-done | bytes 65552 | tf_op jit(solution)/shard_map/reduce_scatter | solution.py:38
  170.3 64.9 %psum.98 = f32[256]{0:T(256)S(1)} all-reduce(f32[256]{0:T(256)S(1)} %multiply_reduce_fusion.18), channel_id=1, replica_groups=mesh['row'=8,'col'=16] {'row','col'}, use_global_device_ids=true, to_apply=%region_3.0 | all-reduce | flops 256 | bytes 2048 | tf_op jit(solution)/shard_map/psum | solution.py:41
  236.8 62.6 %all-gather.8.cloned.1.call-done = bf16[8192,256]{1,0:T(8,128)(2,1)} async-done(((bf16[64,256]{1,0:T(8,128)(2,1)}), bf16[8192,256]{1,0:T(8,128)(2,1)}) %all-gather.8.cloned.1.call-update) | async-done | bytes 4194320 | tf_op jit(solution)/shard_map/all_gather | solution.py:32
  299.4 7.4 convolution_bitcast_fusion.3
  306.8 6.5 copy.12
  317.8 71.6 %reduce-scatter.8.cloned.1.call-done = f32[64,256]{1,0:T(8,128)} async-done(((f32[1024,256]{1,0:T(8,128)}), f32[64,256]{1,0:T(8,128)}) %reduce-scatter.8.cloned.1.call-update) | async-done | bytes 65552 | tf_op jit(solution)/shard_map/reduce_scatter | solution.py:38
  390.2 64.9 %psum.99 = f32[256]{0:T(256)S(1)} all-reduce(f32[256]{0:T(256)S(1)} %multiply_reduce_fusion.17), channel_id=1, replica_groups=mesh['row'=8,'col'=16] {'row','col'}, use_global_device_ids=true, to_apply=%region_7.0 | all-reduce | flops 256 | bytes 2048 | tf_op jit(solution)/shard_map/psum | solution.py:52
  456.0 62.0 %psum.100 = f32[256]{0:T(256)S(1)} all-reduce(f32[256]{0:T(256)S(1)} %multiply_reduce_fusion.16), channel_id=1, replica_groups=mesh['row'=8,'col'=16] {'row','col'}, use_global_device_ids=true, to_apply=%region_9.0 | all-reduce | flops 256 | bytes 2048 | tf_op jit(solution)/shard_map/psum | solution.py:41
  519.7 63.6 %all-gather.10.cloned.1.call-done = bf16[8192,256]{1,0:T(8,128)(2,1)} async-done(((bf16[64,256]{1,0:T(8,128)(2,1)}), bf16[8192,256]{1,0:T(8,128)(2,1)}) %all-gather.10.cloned.1.call-update) | async-done | bytes 4194320 | tf_op jit(solution)/shard_map/all_gather | solution.py:32
  583.3 7.4 convolution_bitcast_fusion.2
  601.7 71.6 %reduce-scatter.10.cloned.1.call-done = f32[64,256]{1,0:T(8,128)} async-done(((f32[1024,256]{1,0:T(8,128)}), f32[64,256]{1,0:T(8,128)}) %reduce-scatter.10.cloned.1.call-update) | async-done | bytes 65552 | tf_op jit(solution)/shard_map/reduce_scatter | solution.py:38
  674.2 64.9 %psum.101 = f32[256]{0:T(256)S(1)} all-reduce(f32[256]{0:T(256)S(1)} %multiply_reduce_fusion.15), channel_id=1, replica_groups=mesh['row'=8,'col'=16] {'row','col'}, use_global_device_ids=true, to_apply=%region_13.0 | all-reduce | flops 256 | bytes 2048 | tf_op jit(solution)/shard_map/psum | solution.py:52
  739.9 62.0 %psum.102 = f32[256]{0:T(256)S(1)} all-reduce(f32[256]{0:T(256)S(1)} %multiply_reduce_fusion.14), channel_id=1, replica_groups=mesh['row'=8,'col'=16] {'row','col'}, use_global_device_ids=true, to_apply=%region_15.0 | all-reduce | flops 256 | bytes 2048 | tf_op jit(solution)/shard_map/psum | solution.py:52
  802.8 64.5 %psum.103 = f32[256]{0:T(256)S(1)} all-reduce(f32[256]{0:T(256)S(1)} %get-tuple-element.21), channel_id=1, replica_groups=mesh['row'=8,'col'=16] {'row','col'}, use_global_device_ids=true, to_apply=%region_17.0 | all-reduce | flops 256 | bytes 2048 | tf_op jit(solution)/shard_map/psum | solution.py:41
  868.0 62.7 %all-gather.12.cloned.1.call-done = bf16[8192,256]{1,0:T(8,128)(2,1)} async-done(((bf16[64,256]{1,0:T(8,128)(2,1)}), bf16[8192,256]{1,0:T(8,128)(2,1)}) %all-gather.12.cloned.1.call-update) | async-done | bytes 4194320 | tf_op jit(solution)/shard_map/all_gather | solution.py:32
  930.7 7.4 convolution_bitcast_fusion.1
  949.1 71.6 %reduce-scatter.12.cloned.1.call-done = f32[64,256]{1,0:T(8,128)} async-done(((f32[1024,256]{1,0:T(8,128)}), f32[64,256]{1,0:T(8,128)}) %reduce-scatter.12.cloned.1.call-update) | async-done | bytes 65552 | tf_op jit(solution)/shard_map/reduce_scatter | solution.py:38
  1021.5 64.9 %psum.104 = f32[256]{0:T(256)S(1)} all-reduce(f32[256]{0:T(256)S(1)} %multiply_reduce_fusion.12), channel_id=1, replica_groups=mesh['row'=8,'col'=16] {'row','col'}, use_global_device_ids=true, to_apply=%region_21.0 | all-reduce | flops 256 | bytes 2048 | tf_op jit(solution)/shard_map/psum | solution.py:52
  1087.3 62.0 %psum.105 = f32[256]{0:T(256)S(1)} all-reduce(f32[256]{0:T(256)S(1)} %multiply_reduce_fusion.11), channel_id=1, replica_groups=mesh['row'=8,'col'=16] {'row','col'}, use_global_device_ids=true, to_apply=%region_23.0 | all-reduce | flops 256 | bytes 2048 | tf_op jit(solution)/shard_map/psum | solution.py:52
  1150.2 64.8 %psum.106 = f32[256]{0:T(256)S(1)} all-reduce(f32[256]{0:T(256)S(1)} %get-tuple-element.19), channel_id=1, replica_groups=mesh['row'=8,'col'=16] {'row','col'}, use_global_device_ids=true, to_apply=%region_25.0 | all-reduce | flops 256 | bytes 2048 | tf_op jit(solution)/shard_map/psum | solution.py:52
  1215.0 62.0 %psum.107 = f32[256]{0:T(256)S(1)} all-reduce(f32[256]{0:T(256)S(1)} %multiply_reduce_fusion.9), channel_id=1, replica_groups=mesh['row'=8,'col'=16] {'row','col'}, use_global_device_ids=true, to_apply=%region_27.0 | all-reduce | flops 256 | bytes 2048 | tf_op jit(solution)/shard_map/psum | solution.py:41
  1277.7 63.9 %all-gather.14.cloned.1.call-done = bf16[8192,256]{1,0:T(8,128)(2,1)} async-done(((bf16[64,256]{1,0:T(8,128)(2,1)}), bf16[8192,256]{1,0:T(8,128)(2,1)}) %all-gather.14.cloned.1.call-update) | async-done | bytes 4194320 | tf_op jit(solution)/shard_map/all_gather | solution.py:32
  1341.5 7.4 convolution_bitcast_fusion
  1349.0 6.5 copy.15
  1360.0 71.6 %reduce-scatter.14.cloned.1.call-done = f32[64,256]{1,0:T(8,128)} async-done(((f32[1024,256]{1,0:T(8,128)}), f32[64,256]{1,0:T(8,128)}) %reduce-scatter.14.cloned.1.call-update) | async-done | bytes 65552 | tf_op jit(solution)/shard_map/reduce_scatter | solution.py:38
  1432.5 64.9 %psum.108 = f32[256]{0:T(256)S(1)} all-reduce(f32[256]{0:T(256)S(1)} %multiply_reduce_fusion.8), channel_id=1, replica_groups=mesh['row'=8,'col'=16] {'row','col'}, use_global_device_ids=true, to_apply=%region_31.0 | all-reduce | flops 256 | bytes 2048 | tf_op jit(solution)/shard_map/psum | solution.py:52
  1498.2 62.0 %psum.109 = f32[256]{0:T(256)S(1)} all-reduce(f32[256]{0:T(256)S(1)} %multiply_reduce_fusion.7), channel_id=1, replica_groups=mesh['row'=8,'col'=16] {'row','col'}, use_global_device_ids=true, to_apply=%region_33.0 | all-reduce | flops 256 | bytes 2048 | tf_op jit(solution)/shard_map/psum | solution.py:52
  1561.1 64.5 %psum.110 = f32[256]{0:T(256)S(1)} all-reduce(f32[256]{0:T(256)S(1)} %get-tuple-element.17), channel_id=1, replica_groups=mesh['row'=8,'col'=16] {'row','col'}, use_global_device_ids=true, to_apply=%region_35.0 | all-reduce | flops 256 | bytes 2048 | tf_op jit(solution)/shard_map/psum | solution.py:52
  1625.7 62.0 %psum.111 = f32[1,256]{1,0:T(1,128)S(1)} all-reduce(f32[1,256]{1,0:T(1,128)S(1)} %bitcast.72), channel_id=1, replica_groups=mesh['row'=8,'col'=16] {'row','col'}, use_global_device_ids=true, to_apply=%region_37.0 | all-reduce | flops 256 | bytes 2048 | tf_op jit(solution)/shard_map/psum | solution.py:52
  (101 shorter events, 54.0 us)
Async XLA Ops:
  6.5 1.6 copy-start
  6.5 73.0 %all-gather.6.cloned.1.call-start = ((), (), s32[]{:S(2)}) async-start(), calls=%async_computation.5 | async-start | bytes 4227072 | tf_op jit(solution)/shard_map/all_gather | solution.py:32
  8.0 161.4 %reduce-scatter.6.cloned.1.call-start = ((), (), s32[]{:S(2)}) async-start(), calls=%async_computation.6 | async-start | bytes 1114112 | tf_op jit(solution)/shard_map/reduce_scatter | solution.py:38
  97.9 201.5 %all-gather.8.cloned.1.call-start = ((), (), s32[]{:S(2)}) async-start(), calls=%async_computation.7 | async-start | bytes 4227072 | tf_op jit(solution)/shard_map/all_gather | solution.py:32
  236.7 152.6 %reduce-scatter.8.cloned.1.call-start = ((), (), s32[]{:S(2)}) async-start(), calls=%async_computation.8 | async-start | bytes 1114112 | tf_op jit(solution)/shard_map/reduce_scatter | solution.py:38
  313.3 76.0 %copy-start.2 = (f32[64,256]{1,0:T(8,128)S(1)}, f32[64,256]{1,0:T(8,128)}, u32[]{:S(2)}) copy-start(f32[64,256]{1,0:T(8,128)} %reduce-scatter.6.cloned.1.call-done) | copy-start | bytes 196612
  317.7 265.6 %all-gather.10.cloned.1.call-start = ((), (), s32[]{:S(2)}) async-start(), calls=%async_computation.9 | async-start | bytes 4227072 | tf_op jit(solution)/shard_map/all_gather | solution.py:32
  519.5 153.8 %reduce-scatter.10.cloned.1.call-start = ((), (), s32[]{:S(2)}) async-start(), calls=%async_computation.10 | async-start | bytes 1114112 | tf_op jit(solution)/shard_map/reduce_scatter | solution.py:38
  597.3 141.8 %copy-start.3 = (f32[64,256]{1,0:T(8,128)S(1)}, f32[64,256]{1,0:T(8,128)}, u32[]{:S(2)}) copy-start(f32[64,256]{1,0:T(8,128)} %reduce-scatter.8.cloned.1.call-done) | copy-start | bytes 196612
  601.7 329.1 %all-gather.12.cloned.1.call-start = ((), (), s32[]{:S(2)}) async-start(), calls=%async_computation.11 | async-start | bytes 4227072 | tf_op jit(solution)/shard_map/all_gather | solution.py:32
  868.0 152.7 %reduce-scatter.12.cloned.1.call-start = ((), (), s32[]{:S(2)}) async-start(), calls=%async_computation.12 | async-start | bytes 1114112 | tf_op jit(solution)/shard_map/reduce_scatter | solution.py:38
  949.0 392.5 %all-gather.14.cloned.1.call-start = ((), (), s32[]{:S(2)}) async-start(), calls=%async_computation.13 | async-start | bytes 4227072 | tf_op jit(solution)/shard_map/all_gather | solution.py:32
  1277.6 154.0 %reduce-scatter.14.cloned.1.call-start = ((), (), s32[]{:S(2)}) async-start(), calls=%async_computation.14 | async-start | bytes 1114112 | tf_op jit(solution)/shard_map/reduce_scatter | solution.py:38
  1349.0 340.0 %copy-start.1 = (f32[64,6]{0,1:T(8,128)S(1)}, f32[64,6]{0,1:T(8,128)}, u32[]{:S(2)}) copy-start(f32[64,6]{0,1:T(8,128)} %param.9) | copy-start | bytes 4612
  1355.5 332.4 %copy-start.12 = (f32[4,256]{1,0:T(4,128)S(1)}, f32[4,256]{1,0:T(4,128)}, u32[]{:S(2)}) copy-start(f32[4,256]{1,0:T(4,128)} %constant.71.clone.1) | copy-start | bytes 12292
  1355.5 332.4 %copy-start.11 = (f32[4,256]{1,0:T(4,128)S(1)}, f32[4,256]{1,0:T(4,128)}, u32[]{:S(2)}) copy-start(f32[4,256]{1,0:T(4,128)} %constant.72.clone.1) | copy-start | bytes 12292
  1355.5 332.5 %copy-start.10 = (f32[4,256]{1,0:T(4,128)S(1)}, f32[4,256]{1,0:T(4,128)}, u32[]{:S(2)}) copy-start(f32[4,256]{1,0:T(4,128)} %constant.73.clone.1) | copy-start | bytes 12292
  1355.5 332.5 %copy-start.9 = (f32[4,256]{1,0:T(4,128)S(1)}, f32[4,256]{1,0:T(4,128)}, u32[]{:S(2)}) copy-start(f32[4,256]{1,0:T(4,128)} %constant.74.clone.1) | copy-start | bytes 12292
  1355.5 332.6 %copy-start.8 = (f32[4,256]{1,0:T(4,128)S(1)}, f32[4,256]{1,0:T(4,128)}, u32[]{:S(2)}) copy-start(f32[4,256]{1,0:T(4,128)} %constant.75.clone.1) | copy-start | bytes 12292
  1355.5 332.6 %copy-start.7 = (f32[4,256]{1,0:T(4,128)S(1)}, f32[4,256]{1,0:T(4,128)}, u32[]{:S(2)}) copy-start(f32[4,256]{1,0:T(4,128)} %constant.76.clone.1) | copy-start | bytes 12292
  1355.5 332.6 %copy-start.6 = (f32[4,256]{1,0:T(4,128)S(1)}, f32[4,256]{1,0:T(4,128)}, u32[]{:S(2)}) copy-start(f32[4,256]{1,0:T(4,128)} %constant.77.clone.1) | copy-start | bytes 12292
  1355.5 332.7 %copy-start.5 = (f32[4,256]{1,0:T(4,128)S(1)}, f32[4,256]{1,0:T(4,128)}, u32[]{:S(2)}) copy-start(f32[4,256]{1,0:T(4,128)} %constant.78.clone.1) | copy-start | bytes 12292
  1355.6 332.7 %copy-start.4 = (f32[64,256]{1,0:T(8,128)S(1)}, f32[64,256]{1,0:T(8,128)}, u32[]{:S(2)}) copy-start(f32[64,256]{1,0:T(8,128)} %param.7) | copy-start | bytes 196612
Sparse Core Ops, SparseCore 0:
  10.5 69.0 all-gather.5
  98.0 71.4 reduce-scatter.5
  236.8 62.5 all-gather.7
  317.8 71.4 reduce-scatter.7
  519.6 63.6 all-gather.9
  601.8 71.4 reduce-scatter.9
  868.1 62.5 all-gather.11
  949.2 71.4 reduce-scatter.11
  1277.8 63.7 all-gather.13
  1360.1 71.4 reduce-scatter.13
where the time goes:
time: 1700 us
  blocking collectives  890 us (52%)
  waiting for transfers between devices  681 us (40%)
  other arithmetic  39.3 us (2%)
  matrix products  37.9 us (2%)
  local copies, waits for them, and re-layouts  32.7 us (2%)
    psum x10, blocking collectives, body(): correlation = lax.psum(jnp.sum(basis[i] * fresh, axis=0), ('row', 'col'))  637 us
    reduce_scatter x5, waiting for transfers between devices, apply_rates(): lax.psum_scatter(partial_value, 'col', scatter_dimension=0, tiled=True)  358 us
    all_gather x5, waiting for transfers between devices, apply_rates(): gathered = lax.all_gather(rounded, ('row', 'col'), axis=0, tiled=True)  323 us
    psum x4, blocking collectives, norm_of(): squares = lax.psum(jnp.sum(vector * vector, axis=0), ('row', 'col'))  253 us
    dot_general x5, matrix products, apply_rates(): jnp.dot(stacked, operand, preferred_element_type=jnp.float32)  37 us
  transfers between devices with their start and end apart: 10, of which 10 were waited for; matrix products, arithmetic and copies ran while one was open for 0% of the time, Pallas kernels for 0%

commit v1 on v0

v1 whole, which is shorter than its diff:
```python
import math

import jax
import jax.numpy as jnp
from jax import lax
from jax.experimental import pallas as pl
from jax.experimental.pallas import tpu as pltpu
from jax.sharding import Mesh, PartitionSpec as P

KRYLOV = 4
TAYLOR = 8
TERMS = 6

epsilon = 1e-06
step_size = 1.0

NZ, NK, NX, NY = 4, 2, 4, 4
ALL = ("z", "k", "x", "y")
SUB = 64
HALF = NX * SUB
COLS = NK * HALF
EXTRA = 8


def device(z, k, x, y):
    return ((z * NK + k) * NX + x) * NY + y


TO_INNER = [
    (device(z, k, x, y), device(z, x % 2, y, 2 * k + x // 2))
    for z in range(NZ)
    for k in range(NK)
    for x in range(NX)
    for y in range(NY)
]
TO_OUTER = [(b, a) for a, b in TO_INNER]
SWAP = [(0, 1), (1, 0)]


def solve(gram, count):
    g = lambda m, n: gram[(min(m, n), max(m, n))]
    scale = jnp.sqrt(g(1, 1) + epsilon)
    combos = {1: {1: 1.0 / scale}}
    hess = {(1, 0): scale}
    for j in range(1, count):
        d = {j + 1: None}
        for m in range(1, j + 1):
            d[m] = 0.0
        for i in range(1, j + 1):
            h = 0.0
            for m, c in combos[i].items():
                h = h + c * g(m, j + 1)
            hess[(i, j)] = h
            for m, c in combos[i].items():
                d[m] = d[m] - h * c
        square = g(j + 1, j + 1)
        for m in range(1, j + 1):
            inner = 2.0 * g(m, j + 1)
            for n in range(1, j + 1):
                inner = inner + d[n] * g(m, n)
            square = square + d[m] * inner
        length = jnp.sqrt(jnp.maximum(square, 0.0) + epsilon)
        hess[(j + 1, j)] = length
        inv = 1.0 / length
        combos[j + 1] = {m: (inv if m == j + 1 else d[m] * inv) for m in d}
    return combos, hess


def matmul_kernel(n_fields, exact, k_ref, kept_ref, got_ref, w_ref, *refs):
    own_refs, other_refs = refs[:n_fields], refs[n_fields : 2 * n_fields]
    out_ref, x_ref = refs[2 * n_fields :][:2]
    step = pl.program_id(0)
    core = k_ref[0]
    cells = w_ref.shape[1]

    if not exact:
        gram_ref = refs[2 * n_fields + 2]

    @pl.when(step == 0)
    def _():
        for ref, at in ((own_refs[-1], core * HALF), (other_refs[-1], (1 - core) * HALF)):
            for x in range(NX):
                rows = pl.ds(pl.multiple_of(at + x * SUB, SUB), SUB)
                x_ref[rows, pl.ds(0, cells)] = ref[x, pl.ds(0, SUB), :]
                if not exact:
                    x_ref[rows, pl.ds(cells, cells)] = ref[x, pl.ds(SUB, SUB), :]
        if not exact:
            gram_ref[...] = jnp.zeros_like(gram_ref)
            for m in range(n_fields):
                total = jnp.zeros((8, cells), jnp.float32)
                for a_ref, b_ref in ((own_refs[m], own_refs[-1]), (other_refs[m], other_refs[-1])):
                    for x in range(NX):
                        wide = lambda r: (
                            r[x, pl.ds(0, SUB), :].astype(jnp.float32)
                            + r[x, pl.ds(SUB, SUB), :].astype(jnp.float32)
                        )
                        product = wide(a_ref) * wide(b_ref)
                        total = total + jnp.sum(product.reshape(SUB // 8, 8, cells), axis=0)
                gram_ref[pl.ds(m, 1), :] = jnp.sum(total, axis=0, keepdims=True)

    def part(rates):
        total = None
        for j in range(TERMS):
            product = jnp.dot(rates[j, 0], x_ref[...], preferred_element_type=jnp.float32)
            if not exact:
                product = product[:, :cells] + product[:, cells:]
            product = w_ref[pl.ds(j, 1), :] * product
            total = product if total is None else total + product
        for x in range(NX):
            out_ref[x, 0, pl.ds(0, SUB), :] = total[x * SUB : (x + 1) * SUB, :]
            if not exact:
                out_ref[x, 0, pl.ds(SUB, EXTRA), :] = gram_ref[...]

    @pl.when(step < 2)
    def _():
        part(kept_ref)

    @pl.when(step >= 2)
    def _():
        part(got_ref)


def apply_rates(core, kept, got, weights, fields, exact):
    cells = weights.shape[1]
    rows = SUB if exact else SUB + EXTRA
    whole = lambda a: pl.BlockSpec(a.shape, lambda g, k: (0,) * a.ndim)
    own, other = [f[0] for f in fields], [f[1] for f in fields]
    block = (TERMS, 1, HALF, COLS)
    scratch = [pltpu.VMEM((COLS, cells if exact else 2 * cells), jnp.bfloat16)]
    if not exact:
        scratch.append(pltpu.VMEM((EXTRA, cells), jnp.float32))

    def kernel(*refs):
        matmul_kernel(len(fields), exact, *refs)

    out = pl.pallas_call(
        kernel,
        out_shape=jax.ShapeDtypeStruct((NX, NY, rows, cells), jnp.float32),
        grid_spec=pltpu.PrefetchScalarGridSpec(
            num_scalar_prefetch=1,
            grid=(NY,),
            in_specs=[
                pl.BlockSpec(block, lambda g, k: (0, 2 * jnp.minimum(g, 1) + k[0], 0, 0)),
                pl.BlockSpec(block, lambda g, k: (0, jnp.maximum(g - 2, 0), 0, 0)),
                whole(weights),
                *[whole(a) for a in own],
                *[whole(a) for a in other],
            ],
            out_specs=pl.BlockSpec(
                (NX, 1, rows, cells), lambda g, k: (0, (g + 2 * k[0]) % NY, 0, 0)
            ),
            scratch_shapes=scratch,
        ),
        name="rates",
    )(core, kept, got, weights, *own, *other)
    return out.reshape(NX * NY, rows, cells)


def combine_kernel(j, got_ref, gram_ref, *refs):
    q_refs, outs = refs[:j], refs[j:]
    cells = got_ref.shape[2]
    total = got_ref[0]
    for b in range(1, NX * NY):
        total = total + got_ref[b]
    fresh = total[:SUB]
    gram_out = outs[-1]
    gram = {}
    if j > 0:
        gram_out[...] = gram_ref[...]
        for m in range(1, j + 1):
            for n in range(m, j):
                gram[(m, n)] = gram_ref[pl.ds(4 * (m - 1) + n - 1, 1), :]
            row = total[SUB + m - 1 : SUB + m]
            gram[(m, j)] = row
            gram_out[pl.ds(4 * (m - 1) + j - 1, 1), :] = row
        _, hess = solve(gram, j)
        for i in range(1, j):
            fresh = fresh - hess[(i, j - 1)] * q_refs[i][...]
        fresh = fresh * (1.0 / hess[(j, j - 1)])
    else:
        gram_out[...] = jnp.zeros_like(gram_out)
    if j < KRYLOV:
        q_out, send_out = outs[0], outs[1]
        q_out[...] = fresh
        high = fresh.astype(jnp.bfloat16)
        low = (fresh - high.astype(jnp.float32)).astype(jnp.bfloat16)
        for b in range(NZ * NX):
            send_out[b, pl.ds(0, SUB), :] = high
            send_out[b, pl.ds(SUB, SUB), :] = low
    else:
        dots = outs[0]
        lanes = dots.shape[1]
        for m in range(1, KRYLOV + 1):
            row = jnp.sum(q_refs[m - 1][...] * fresh, axis=0, keepdims=True)
            dots[pl.ds(m - 1, 1), :] = row[:, :lanes]
            dots[pl.ds(KRYLOV + m - 1, 1), :] = row[:, lanes:]


def combine(j, got, gram, fields):
    cells = got.shape[2]

    def kernel(*refs):
        combine_kernel(j, *refs)

    if j < KRYLOV:
        outs = (
            jax.ShapeDtypeStruct((SUB, cells), jnp.float32),
            jax.ShapeDtypeStruct((NZ * NX, 2 * SUB, cells), jnp.bfloat16),
        )
    else:
        outs = (jax.ShapeDtypeStruct((2 * KRYLOV, cells // 2), jnp.float32),)
    return pl.pallas_call(
        kernel,
        out_shape=(*outs, jax.ShapeDtypeStruct(gram.shape, jnp.float32)),
        name=f"combine{j}",
    )(got, gram, *fields)


def finish_kernel(p_ref, q_ref, gram_ref, dots_ref, out_ref):
    gram = {}
    for m in range(1, KRYLOV + 1):
        for n in range(m, KRYLOV + 1):
            gram[(m, n)] = gram_ref[pl.ds(4 * (m - 1) + n - 1, 1), :]
    dots = jnp.sum(dots_ref[...], axis=0)
    last = {
        m: jnp.concatenate([dots[m - 1 : m], dots[KRYLOV + m - 1 : KRYLOV + m]], axis=1)
        for m in range(1, KRYLOV + 1)
    }
    combos, hess = solve(gram, KRYLOV)
    for i in range(1, KRYLOV + 1):
        h = 0.0
        for m, c in combos[i].items():
            h = h + c * last[m]
        hess[(i, KRYLOV)] = h
    zero = jnp.zeros_like(gram[(1, 1)])
    unit = [zero + 1.0] + [zero] * (KRYLOV - 1)
    coeffs = [u / float(math.factorial(TAYLOR + 1)) for u in unit]
    for k in range(TAYLOR - 1, -1, -1):
        fresh = []
        for i in range(1, KRYLOV + 1):
            value = unit[i - 1] / float(math.factorial(k + 1))
            for j in range(max(i - 1, 1), KRYLOV + 1):
                value = value + step_size * hess[(i, j)] * coeffs[j - 1]
            fresh.append(value)
        coeffs = fresh
    out = p_ref[...]
    for m in range(1, KRYLOV + 1):
        factor = 0.0
        for i in range(m, KRYLOV + 1):
            factor = factor + coeffs[i - 1] * combos[i][m]
        out = out + step_size * hess[(1, 0)] * factor * q_ref[m - 1]
    out_ref[...] = out


def body(rate_terms, populations, temp_bins, bin_coeffs):
    core = lax.axis_index("k")
    n_bins = bin_coeffs.shape[0]
    cells = populations.shape[1]
    exchange = lambda v, axes: lax.all_to_all(v, axes, 0, 0, tiled=True)

    rates = rate_terms.reshape(TERMS, 2 * NK, HALF, COLS)
    away = lax.dynamic_index_in_dim(
        rate_terms.reshape(TERMS, 2, NK, HALF, COLS), 1 - core, 2, keepdims=False
    )
    got_rates = lax.ppermute(away, "k", SWAP)

    onehot = (temp_bins[:, None] == jnp.arange(n_bins, dtype=jnp.int32)[None, :]).astype(
        jnp.float32
    )
    weights = jnp.dot(onehot, bin_coeffs, precision=lax.Precision.HIGHEST)
    weights = jnp.pad(weights.T, ((0, 2), (0, 0)))
    core_id = core.astype(jnp.int32).reshape(1)

    def spread(blocks):
        met = exchange(blocks, ("z", "x"))
        own = lax.dynamic_slice_in_dim(met, lax.axis_index("x") * NX, NX, 0)
        return own, lax.ppermute(own, "k", SWAP)

    piece = lax.ppermute(populations.astype(jnp.bfloat16), ALL, TO_INNER)
    field = spread(jnp.broadcast_to(piece[None], (NZ * NX, SUB, cells)))
    met = exchange(apply_rates(core_id, rates, got_rates, weights, [field], True), ("x", "y"))
    gram = jnp.zeros((16, cells), jnp.float32)
    q, sent, gram = combine(0, met, gram, [])
    pieces, fields = [q], []
    for j in range(1, KRYLOV + 1):
        fields.append(spread(sent))
        if j == KRYLOV:
            outer = lax.ppermute(jnp.stack(pieces), ALL, TO_OUTER)
        met = exchange(
            apply_rates(core_id, rates, got_rates, weights, fields, False), ("x", "y")
        )
        if j < KRYLOV:
            q, sent, gram = combine(j, met, gram, pieces)
            pieces.append(q)
        else:
            dots, gram = combine(j, met, gram, pieces)
    dots = dots + lax.ppermute(dots, "k", SWAP)
    dots = exchange(jnp.broadcast_to(dots[None], (NZ * NX * NY, *dots.shape)), ("z", "x", "y"))
    return pl.pallas_call(
        finish_kernel,
        out_shape=jax.ShapeDtypeStruct(populations.shape, jnp.float32),
        name="finish",
    )(populations, outer, gram, dots)


def solution(mesh):
    named = Mesh(mesh.devices.reshape(NZ, NK, NX, NY), ALL)
    placed = (P(None, ("z", "k"), ("x", "y")), P(ALL, None), P(), P())
    return jax.shard_map(
        body, mesh=named, in_specs=placed, out_specs=P(ALL, None), check_vma=False
    )
```

time: 1700 us -> 319 us (0.19)
  blocking collectives: 890 us -> 196 us
  waiting for transfers between devices: 681 us -> 29.2 us
  Pallas kernels: 0 us -> 51.4 us
  other arithmetic: 39.3 us -> 0.7 us
  matrix products: 37.9 us -> 0.19 us
  starting transfers between devices: 0.56 us -> 27.3 us
  local copies, waits for them, and re-layouts: 32.7 us -> 12.8 us
    psum x14 -> x0, blocking collectives: 890 us -> none  [the longest x10 637 us: body(): correlation = lax.psum(jnp.sum(basis[i] * fresh, axis=0), ('row', 'col'))]
    reduce_scatter x5 -> x0, waiting for transfers between devices: 358 us -> none  [apply_rates(): lax.psum_scatter(partial_value, 'col', scatter_dimension=0, tiled=True)]
    all_gather x5 -> x0, waiting for transfers between devices: 323 us -> none  [apply_rates(): gathered = lax.all_gather(rounded, ('row', 'col'), axis=0, tiled=True)]
    all_to_all x0 -> x9, blocking collectives: none -> 196 us  [body(): exchange = lambda v, axes: lax.all_to_all(v, axes, 0, 0, tiled=True)]
    pallas_call x0 -> x11, Pallas kernels: none -> 51.4 us  [the longest x5 37.6 us: apply_rates(): pl.pallas_call(kernel, out_shape=jax.ShapeDtypeStruct((NX, NY, rows, cell...]
    dot_general x5 -> x0, matrix products: 37 us -> none  [apply_rates(): jnp.dot(stacked, operand, preferred_element_type=jnp.float32)]
    reduce_sum x27 -> x0, other arithmetic: 32.7 us -> none  [the longest x5 21.9 us: apply_rates(): partial_value = jnp.sum(products * weights_t[:, None, :], axis=0)]
    dot_general x5 -> x0, local copies, waits for them, and re-layouts: 32.6 us -> none  [apply_rates(): jnp.dot(stacked, operand, preferred_element_type=jnp.float32)]
  transfers between devices with their start and end apart: 10 -> 11, of which waited for: 10 -> 8; matrix products, arithmetic and copies ran while one was open for 0% -> 1% of each run, Pallas kernels for 0% -> 0%
where the time goes in v1:
time: 319 us; the launch traced here: 318 us
  blocking collectives  196 us (61%)
  Pallas kernels  51.4 us (16%)
  waiting for transfers between devices  29.2 us (9%)
  starting transfers between devices  27.3 us (9%)
  local copies, waits for them, and re-layouts  12.8 us (4%)
    all_to_all x9, blocking collectives, body(): exchange = lambda v, axes: lax.all_to_all(v, axes, 0, 0, tiled=True)  196 us
    pallas_call x5, Pallas kernels, apply_rates(): pl.pallas_call(kernel, out_shape=jax.ShapeDtypeStruct((NX, NY, rows, cell...  37.6 us
    all_to_all x2, starting transfers between devices, body(): exchange = lambda v, axes: lax.all_to_all(v, axes, 0, 0, tiled=True)  25.3 us
    all_to_all x2, waiting for transfers between devices, body(): exchange = lambda v, axes: lax.all_to_all(v, axes, 0, 0, tiled=True)  22 us
    pallas_call x5, Pallas kernels, combine(): pl.pallas_call(kernel, out_shape=(*outs, jax.ShapeDtypeStruct(gram.shape,...  12 us
    ppermute x5, waiting for transfers between devices, spread(): return (own, lax.ppermute(own, 'k', SWAP))  6.54 us
  transfers between devices with their start and end apart: 11, of which 8 were waited for; matrix products, arithmetic and copies ran while one was open for 1% of the time, Pallas kernels for 0%

profile of v1, /device:TPU:0, one launch (start us, length us, event | category | flops | bytes accessed | tf_op | source)
XLA Modules:
  0.0 317.6 jit_solution(5249859218865990519)
XLA Ops:
  0.0 3.8 %dynamic-slice_bitcast_fusion = bf16[6,2,256,512]{3,2,1,0:T(8,128)(2,1)} fusion(bf16[6,2,2,256,512]{4,3,2,1,0:T(8,128)(2,1)} %bitcast.19, s32[]{:T(128)S(6)} %select_n.6), kind=kLoop, calls=%fused_computation | loop fusion | bytes 6291460 | tf_op jit(solution)/shard_map/jit(dynamic_index_in_dim)/squeeze | solution.py:262
  4.5 0.9 broadcast_in_dim.6
  5.3 17.2 %all-to-all-start = ((bf16[16,64,256]{2,1,0:T(8,128)(2,1)}), bf16[16,64,256]{2,1,0:T(8,128)(2,1)}, u32[]{:S(2)}, u32[]{:S(2)}) async-start(bf16[16,64,256]{2,1,0:T(8,128)(2,1)} %broadcast_in_dim.6), calls=%async_computation | async-start | bytes 1048576 | tf_op jit(solution)/shard_map/all_to_all | solution.py:259
  22.6 11.4 %all-to-all-done = bf16[16,64,256]{2,1,0:T(8,128)(2,1)} async-done(((bf16[16,64,256]{2,1,0:T(8,128)(2,1)}), bf16[16,64,256]{2,1,0:T(8,128)(2,1)}, u32[]{:S(2)}, u32[]{:S(2)}) %all-to-all-start) | async-done | bytes 524320 | tf_op jit(solution)/shard_map/all_to_all | solution.py:259
  33.9 0.9 constant_dynamic-slice_fusion.4.refs_4_
  36.9 1.0 copy-done.1
  38.0 6.0 %rates.5 = f32[4,4,64,256]{3,2,1,0:T(8,128)} custom-call(s32[1]{0:T(128)} %bitcast.refs_0_, bf16[6,4,256,512]{3,2,1,0:T(8,128)(2,1)} %bitcast.20, bf16[6,2,256,512]{3,2,1,0:T(8,128)(2,1)} %copy-done.1, f32[8,256]{1,0:T(8,128)} %pad.4.refs_3_, bf16[4,64,256]{2,1,0:T(8,128)(2,1)} %copy-done.13, bf16[4,64,256]{2,1,0:T(8,128)(2,1)} %copy-done.18), custom_call_target="tpu_custom_call" | custom-call | tf_op jit(solution)/shard_map/rates/pallas_call | solution.py:136
  44.0 22.0 %all_to_all.55.refs_0_ = f32[16,64,256]{2,1,0:T(8,128)} all-to-all(f32[16,64,256]{2,1,0:T(8,128)} %bitcast.29), channel_id=1, replica_groups=mesh['z'=4,'k'=2,'x'=4,'y'=4] {'x','y'}, dimensions={0} | all-to-all | bytes 2097152 | tf_op jit(solution)/shard_map/all_to_all | solution.py:259
  66.6 2.4 combine0.1
  69.0 19.8 %all_to_all.56 = bf16[16,128,256]{2,1,0:T(8,128)(2,1)S(1)} all-to-all(bf16[16,128,256]{2,1,0:T(8,128)(2,1)} %get-tuple-element.20), channel_id=1, replica_groups=mesh['z'=4,'k'=2,'x'=4,'y'=4] {'z','x'}, dimensions={0} | all-to-all | bytes 2097152 | tf_op jit(solution)/shard_map/all_to_all | solution.py:259
  88.9 1.5 collective-permute-done.3.refs_5_.refs_6_.refs_7_.refs_8_
  91.1 7.4 %rates.6 = f32[4,4,72,256]{3,2,1,0:T(8,128)} custom-call(s32[1]{0:T(128)} %bitcast.refs_0_, bf16[6,4,256,512]{3,2,1,0:T(8,128)(2,1)} %bitcast.21, bf16[6,2,256,512]{3,2,1,0:T(8,128)(2,1)} %copy-done.1, f32[8,256]{1,0:T(8,128)} %pad.4.refs_3_, bf16[4,128,256]{2,1,0:T(8,128)(2,1)} %copy-done.2, bf16[4,128,256]{2,1,0:T(8,128)(2,1)} %copy-done.3), custom_call_target="tpu_custom_call" | custom-call | tf_op jit(solution)/shard_map/rates/pallas_call | solution.py:136
  98.6 23.3 %all_to_all.57.refs_0_ = f32[16,72,256]{2,1,0:T(8,128)} all-to-all(f32[16,72,256]{2,1,0:T(8,128)} %bitcast.25), channel_id=1, replica_groups=mesh['z'=4,'k'=2,'x'=4,'y'=4] {'x','y'}, dimensions={0} | all-to-all | bytes 2359296 | tf_op jit(solution)/shard_map/all_to_all | solution.py:259
  121.9 2.5 combine1.1
  124.3 20.3 %all_to_all.58 = bf16[16,128,256]{2,1,0:T(8,128)(2,1)S(1)} all-to-all(bf16[16,128,256]{2,1,0:T(8,128)(2,1)} %get-tuple-element.23), channel_id=1, replica_groups=mesh['z'=4,'k'=2,'x'=4,'y'=4] {'z','x'}, dimensions={0} | all-to-all | bytes 2097152 | tf_op jit(solution)/shard_map/all_to_all | solution.py:259
  144.7 1.5 collective-permute-done.4.refs_7_.refs_8_.refs_9_
  146.9 7.7 %rates.7 = f32[4,4,72,256]{3,2,1,0:T(8,128)} custom-call(s32[1]{0:T(128)} %bitcast.refs_0_, bf16[6,4,256,512]{3,2,1,0:T(8,128)(2,1)} %bitcast.22, bf16[6,2,256,512]{3,2,1,0:T(8,128)(2,1)} %copy-done.1, f32[8,256]{1,0:T(8,128)} %pad.4.refs_3_, bf16[4,128,256]{2,1,0:T(8,128)(2,1)} %copy-done.2, bf16[4,128,256]{2,1,0:T(8,128)(2,1)} %copy-done.4, ...), custom_call_target="tpu_custom_call" | custom-call | tf_op jit(solution)/shard_map/rates/pallas_call | solution.py:136
  154.7 23.3 %all_to_all.59.refs_0_ = f32[16,72,256]{2,1,0:T(8,128)} all-to-all(f32[16,72,256]{2,1,0:T(8,128)} %bitcast.26), channel_id=1, replica_groups=mesh['z'=4,'k'=2,'x'=4,'y'=4] {'x','y'}, dimensions={0} | all-to-all | bytes 2359296 | tf_op jit(solution)/shard_map/all_to_all | solution.py:259
  178.0 2.5 combine2.1
  180.4 20.3 %all_to_all.60 = bf16[16,128,256]{2,1,0:T(8,128)(2,1)S(1)} all-to-all(bf16[16,128,256]{2,1,0:T(8,128)(2,1)} %get-tuple-element.26), channel_id=1, replica_groups=mesh['z'=4,'k'=2,'x'=4,'y'=4] {'z','x'}, dimensions={0} | all-to-all | bytes 2097152 | tf_op jit(solution)/shard_map/all_to_all | solution.py:259
  200.8 1.5 collective-permute-done.5.refs_9_.refs_10_
  203.1 8.1 %rates.8 = f32[4,4,72,256]{3,2,1,0:T(8,128)} custom-call(s32[1]{0:T(128)} %bitcast.refs_0_, bf16[6,4,256,512]{3,2,1,0:T(8,128)(2,1)} %bitcast.23, bf16[6,2,256,512]{3,2,1,0:T(8,128)(2,1)} %copy-done.1, f32[8,256]{1,0:T(8,128)} %pad.4.refs_3_, bf16[4,128,256]{2,1,0:T(8,128)(2,1)} %copy-done.2, bf16[4,128,256]{2,1,0:T(8,128)(2,1)} %copy-done.4, ...), custom_call_target="tpu_custom_call" | custom-call | tf_op jit(solution)/shard_map/rates/pallas_call | solution.py:136
  211.1 23.3 %all_to_all.61.refs_0_ = f32[16,72,256]{2,1,0:T(8,128)} all-to-all(f32[16,72,256]{2,1,0:T(8,128)} %bitcast.28), channel_id=1, replica_groups=mesh['z'=4,'k'=2,'x'=4,'y'=4] {'x','y'}, dimensions={0} | all-to-all | bytes 2359296 | tf_op jit(solution)/shard_map/all_to_all | solution.py:259
  234.4 2.5 combine3.1
  236.9 20.3 %all_to_all.62 = bf16[16,128,256]{2,1,0:T(8,128)(2,1)S(1)} all-to-all(bf16[16,128,256]{2,1,0:T(8,128)(2,1)} %get-tuple-element.29), channel_id=1, replica_groups=mesh['z'=4,'k'=2,'x'=4,'y'=4] {'z','x'}, dimensions={0} | all-to-all | bytes 2097152 | tf_op jit(solution)/shard_map/all_to_all | solution.py:259
  257.5 1.5 collective-permute-done.7.refs_11_
  259.7 8.3 %rates.9 = f32[4,4,72,256]{3,2,1,0:T(8,128)} custom-call(s32[1]{0:T(128)} %bitcast.refs_0_, bf16[6,4,256,512]{3,2,1,0:T(8,128)(2,1)} %bitcast.24, bf16[6,2,256,512]{3,2,1,0:T(8,128)(2,1)} %copy-done.1, f32[8,256]{1,0:T(8,128)} %pad.4.refs_3_, bf16[4,128,256]{2,1,0:T(8,128)(2,1)} %copy-done.2, bf16[4,128,256]{2,1,0:T(8,128)(2,1)} %copy-done.4, ...), custom_call_target="tpu_custom_call" | custom-call | tf_op jit(solution)/shard_map/rates/pallas_call | solution.py:136
  268.0 23.3 %all_to_all.63.refs_0_ = f32[16,72,256]{2,1,0:T(8,128)} all-to-all(f32[16,72,256]{2,1,0:T(8,128)} %bitcast.27), channel_id=1, replica_groups=mesh['z'=4,'k'=2,'x'=4,'y'=4] {'x','y'}, dimensions={0} | all-to-all | bytes 2359296 | tf_op jit(solution)/shard_map/all_to_all | solution.py:259
  291.3 2.1 combine4.1
  296.2 8.1 %all-to-all-start.10 = ((f32[64,8,128]{2,1,0:T(8,128)}), f32[64,8,128]{2,1,0:T(8,128)S(1)}, u32[]{:S(2)}, u32[]{:S(2)}) async-start(f32[64,8,128]{2,1,0:T(8,128)} %broadcast_in_dim.8), calls=%async_computation.10 | async-start | bytes 524288 | tf_op jit(solution)/shard_map/all_to_all | solution.py:259
  304.3 10.7 %all-to-all-done.10.dots_ref = f32[64,8,128]{2,1,0:T(8,128)S(1)} async-done(((f32[64,8,128]{2,1,0:T(8,128)}), f32[64,8,128]{2,1,0:T(8,128)S(1)}, u32[]{:S(2)}, u32[]{:S(2)}) %all-to-all-start.10) | async-done | bytes 262176 | tf_op jit(solution)/shard_map/all_to_all | solution.py:259
  315.7 1.9 finish.1
  (64 shorter events, 10.2 us)
Async XLA Ops:
  0.0 35.0 %copy-start = (f32[64,6]{0,1:T(8,128)S(1)}, f32[64,6]{0,1:T(8,128)}, u32[]{:S(2)}) copy-start(f32[64,6]{0,1:T(8,128)} %param.7) | copy-start | bytes 4612
  0.0 3.8 %copy-start.17 = (f32[64,256]{1,0:T(8,128)S(1)}, f32[64,256]{1,0:T(8,128)}, u32[]{:S(2)}) copy-start(f32[64,256]{1,0:T(8,128)} %p_ref.1) | copy-start | bytes 196612
  3.8 31.2 %copy-start.19 = (s32[256]{0:T(256)S(1)}, s32[256]{0:T(256)}, u32[]{:S(2)}) copy-start(s32[256]{0:T(256)} %param.6) | copy-start | bytes 3076
  3.8 32.5 %collective-permute-start = (bf16[6,2,256,512]{3,2,1,0:T(8,128)(2,1)}, bf16[6,2,256,512]{3,2,1,0:T(8,128)(2,1)S(1)}, u32[]{:S(2)}, u32[]{:S(2)}) collective-permute-start(bf16[6,2,256,512]{3,2,1,0:T(8,128)(2,1)} %dynamic-slice_bitcast_fusion), channel_id=1, source_target_pairs={{0,16},{16,0},{1,17},{17,1},{2,18},{18,2},{3,19},{19,3},{4,20},{20... | collective-permute-start | bytes 9437192 | tf_op jit(solution)/shard_map/ppermute | solution.py:265
  3.8 0.7 collective-permute-start.1
  5.3 28.6 %all-to-all-start = ((bf16[16,64,256]{2,1,0:T(8,128)(2,1)}), bf16[16,64,256]{2,1,0:T(8,128)(2,1)}, u32[]{:S(2)}, u32[]{:S(2)}) async-start(bf16[16,64,256]{2,1,0:T(8,128)(2,1)} %broadcast_in_dim.6), calls=%async_computation | async-start | bytes 1048576 | tf_op jit(solution)/shard_map/all_to_all | solution.py:259
  34.9 1.4 copy-start.13
  34.9 1.4 collective-permute-start.2
  36.3 0.6 copy-start.18
  36.3 1.7 copy-start.1
  88.8 1.6 copy-start.2
  88.8 1.6 collective-permute-start.3
  90.4 0.7 copy-start.3
  144.6 1.6 copy-start.4
  144.6 1.6 collective-permute-start.4
  146.2 0.7 copy-start.5
  200.7 1.6 copy-start.6
  200.7 1.6 collective-permute-start.5
  202.4 0.7 copy-start.8
  257.2 1.8 copy-start.9
  257.2 1.8 collective-permute-start.7
  259.0 0.7 copy-start.14
  291.3 2.1 copy-start.7
  291.3 2.1 copy-start.11
  291.3 2.1 copy-start.12
  291.3 2.1 copy-start.16
  293.5 1.4 collective-permute-start.8
  293.5 10.8 %collective-permute-start.6 = (f32[4,64,256]{2,1,0:T(8,128)S(1)}, f32[4,64,256]{2,1,0:T(8,128)S(1)}, u32[]{:S(2)}, u32[]{:S(2)}) collective-permute-start(f32[4,64,256]{2,1,0:T(8,128)S(1)} %pad_maximum_fusion), channel_id=1, source_target_pairs={{0,0},{4,1},{8,2},{12,3},{16,4},{20,5},{24,6},{28,7},{1,8},{5,9},{... | collective-permute-start | bytes 786440 | tf_op jit(solution)/shard_map/ppermute | solution.py:288
  296.2 18.8 %all-to-all-start.10 = ((f32[64,8,128]{2,1,0:T(8,128)}), f32[64,8,128]{2,1,0:T(8,128)S(1)}, u32[]{:S(2)}, u32[]{:S(2)}) async-start(f32[64,8,128]{2,1,0:T(8,128)} %broadcast_in_dim.8), calls=%async_computation.10 | async-start | bytes 524288 | tf_op jit(solution)/shard_map/all_to_all | solution.py:259
  304.3 10.7 %copy-start.15 = (f32[4,64,256]{2,1,0:T(8,128)}, f32[4,64,256]{2,1,0:T(8,128)S(1)}, u32[]{:S(2)}) copy-start(f32[4,64,256]{2,1,0:T(8,128)S(1)} %collective-permute-done.6.q_ref) | copy-start | bytes 786436
  315.0 0.7 copy-start.10

commit v2 on v1

--- a/solution.py
+++ b/solution.py
@@ -19,7 +19,8 @@
 SUB = 64
 HALF = NX * SUB
 COLS = NK * HALF
-EXTRA = 8
+EXTRA = 16
+WIRE = jnp.float16
 
 
 def device(z, k, x, y):
@@ -27,7 +28,7 @@
 
 
 TO_INNER = [
-    (device(z, k, x, y), device(z, x % 2, y, 2 * k + x // 2))
+    (device(z, k, x, y), device(z, (k + x) % 2, y, 2 * k + x // 2))
     for z in range(NZ)
     for k in range(NK)
     for x in range(NX)
@@ -35,6 +36,19 @@
 ]
 TO_OUTER = [(b, a) for a, b in TO_INNER]
 SWAP = [(0, 1), (1, 0)]
+SPREAD = [
+    [
+        ((z * NK + k) * NX + x, (((x + 2 * k + t) % NZ) * NK + k) * NX + z)
+        for z in range(NZ)
+        for k in range(NK)
+        for x in range(NX)
+    ]
+    for t in range(2)
+]
+
+
+def exponent(value):
+    return jnp.floor(jnp.log2(jnp.maximum(jnp.abs(value), 1e-30)))
 
 
 def solve(gram, count):
@@ -66,37 +80,41 @@
     return combos, hess
 
 
-def matmul_kernel(n_fields, exact, k_ref, kept_ref, got_ref, w_ref, *refs):
+def matmul_kernel(n_fields, exact, at_ref, kept_ref, got_ref, w_ref, *refs):
     own_refs, other_refs = refs[:n_fields], refs[n_fields : 2 * n_fields]
-    out_ref, x_ref = refs[2 * n_fields :][:2]
+    out_ref, x_ref, extra_ref = refs[2 * n_fields :]
     step = pl.program_id(0)
-    core = k_ref[0]
+    core, place, side = at_ref[0], at_ref[1], at_ref[2]
     cells = w_ref.shape[1]
-
-    if not exact:
-        gram_ref = refs[2 * n_fields + 2]
 
     @pl.when(step == 0)
     def _():
-        for ref, at in ((own_refs[-1], core * HALF), (other_refs[-1], (1 - core) * HALF)):
-            for x in range(NX):
-                rows = pl.ds(pl.multiple_of(at + x * SUB, SUB), SUB)
-                x_ref[rows, pl.ds(0, cells)] = ref[x, pl.ds(0, SUB), :]
-                if not exact:
-                    x_ref[rows, pl.ds(cells, cells)] = ref[x, pl.ds(SUB, SUB), :]
+        for ref, k in ((own_refs[-1], core), (other_refs[-1], 1 - core)):
+            for t in range(2):
+                x = (place + 2 * NZ - 2 * k - t) % NX
+                for o in range(2):
+                    half = (k + o + side) % 2
+                    rows = pl.ds(pl.multiple_of(half * HALF + x * SUB, SUB), SUB)
+                    value = ref[t, o]
+                    high = value.astype(jnp.bfloat16)
+                    x_ref[rows, pl.ds(0, cells)] = high
+                    if not exact:
+                        low = (value - high.astype(jnp.float32)).astype(jnp.bfloat16)
+                        x_ref[rows, pl.ds(cells, cells)] = low
+        extra_ref[...] = jnp.zeros_like(extra_ref)
         if not exact:
-            gram_ref[...] = jnp.zeros_like(gram_ref)
             for m in range(n_fields):
                 total = jnp.zeros((8, cells), jnp.float32)
                 for a_ref, b_ref in ((own_refs[m], own_refs[-1]), (other_refs[m], other_refs[-1])):
-                    for x in range(NX):
-                        wide = lambda r: (
-                            r[x, pl.ds(0, SUB), :].astype(jnp.float32)
-                            + r[x, pl.ds(SUB, SUB), :].astype(jnp.float32)
-                        )
-                        product = wide(a_ref) * wide(b_ref)
-                        total = total + jnp.sum(product.reshape(SUB // 8, 8, cells), axis=0)
-                gram_ref[pl.ds(m, 1), :] = jnp.sum(total, axis=0, keepdims=True)
+                    product = a_ref[...] * b_ref[...]
+                    total = total + jnp.sum(product.reshape(HALF // 8, 8, cells), axis=0)
+                total = jnp.sum(total, axis=0, keepdims=True)
+                power = exponent(total)
+                total = total * jnp.exp2(-power)
+                high = total.astype(jnp.bfloat16).astype(jnp.float32)
+                extra_ref[pl.ds(3 * m + 1, 1), :] = power
+                extra_ref[pl.ds(3 * m + 2, 1), :] = high
+                extra_ref[pl.ds(3 * m + 3, 1), :] = (total - high) * 256.0
 
     def part(rates):
         total = None
@@ -107,9 +125,11 @@
             product = w_ref[pl.ds(j, 1), :] * product
             total = product if total is None else total + product
         for x in range(NX):
-            out_ref[x, 0, pl.ds(0, SUB), :] = total[x * SUB : (x + 1) * SUB, :]
-            if not exact:
-                out_ref[x, 0, pl.ds(SUB, EXTRA), :] = gram_ref[...]
+            block = total[x * SUB : (x + 1) * SUB, :]
+            power = exponent(jnp.max(jnp.abs(block), axis=0, keepdims=True))
+            out_ref[x, 0, pl.ds(0, SUB), :] = block * jnp.exp2(-power)
+            out_ref[x, 0, pl.ds(SUB, EXTRA), :] = extra_ref[...]
+            out_ref[x, 0, pl.ds(SUB, 1), :] = power
 
     @pl.when(step < 2)
     def _():
@@ -120,15 +140,12 @@
         part(got_ref)
 
 
-def apply_rates(core, kept, got, weights, fields, exact):
+def apply_rates(at, kept, got, weights, fields, exact):
     cells = weights.shape[1]
-    rows = SUB if exact else SUB + EXTRA
-    whole = lambda a: pl.BlockSpec(a.shape, lambda g, k: (0,) * a.ndim)
+    rows = SUB + EXTRA
+    whole = lambda a: pl.BlockSpec(a.shape, lambda g, at: (0,) * a.ndim)
     own, other = [f[0] for f in fields], [f[1] for f in fields]
     block = (TERMS, 1, HALF, COLS)
-    scratch = [pltpu.VMEM((COLS, cells if exact else 2 * cells), jnp.bfloat16)]
-    if not exact:
-        scratch.append(pltpu.VMEM((EXTRA, cells), jnp.float32))
 
     def kernel(*refs):
         matmul_kernel(len(fields), exact, *refs)
@@ -140,29 +157,37 @@
             num_scalar_prefetch=1,
             grid=(NY,),
             in_specs=[
-                pl.BlockSpec(block, lambda g, k: (0, 2 * jnp.minimum(g, 1) + k[0], 0, 0)),
-                pl.BlockSpec(block, lambda g, k: (0, jnp.maximum(g - 2, 0), 0, 0)),
+                pl.BlockSpec(block, lambda g, at: (0, 2 * jnp.minimum(g, 1), 0, 0)),
+                pl.BlockSpec(block, lambda g, at: (0, jnp.maximum(g - 2, 0), 0, 0)),
                 whole(weights),
                 *[whole(a) for a in own],
                 *[whole(a) for a in other],
             ],
             out_specs=pl.BlockSpec(
-                (NX, 1, rows, cells), lambda g, k: (0, (g + 2 * k[0]) % NY, 0, 0)
+                (NX, 1, rows, cells), lambda g, at: (0, (g + 2 * at[0]) % NY, 0, 0)
             ),
-            scratch_shapes=scratch,
+            scratch_shapes=[
+                pltpu.VMEM((COLS, cells if exact else 2 * cells), jnp.bfloat16),
+                pltpu.VMEM((EXTRA, cells), jnp.float32),
+            ],
         ),
         name="rates",
-    )(core, kept, got, weights, *own, *other)
+    )(at, kept, got, weights, *own, *other)
     return out.reshape(NX * NY, rows, cells)
 
 
 def combine_kernel(j, got_ref, gram_ref, *refs):
     q_refs, outs = refs[:j], refs[j:]
     cells = got_ref.shape[2]
-    total = got_ref[0]
-    for b in range(1, NX * NY):
-        total = total + got_ref[b]
-    fresh = total[:SUB]
+    fresh, inner = None, [None] * j
+    for b in range(NX * NY):
+        extra = got_ref[b, pl.ds(SUB, EXTRA), :]
+        value = got_ref[b, pl.ds(0, SUB), :] * jnp.exp2(extra[:1])
+        fresh = value if fresh is None else fresh + value
+        for m in range(j):
+            value = extra[3 * m + 2 : 3 * m + 3] + extra[3 * m + 3 : 3 * m + 4] * (1.0 / 256.0)
+            value = value * jnp.exp2(extra[3 * m + 1 : 3 * m + 2])
+            inner[m] = value if inner[m] is None else inner[m] + value
     gram_out = outs[-1]
     gram = {}
     if j > 0:
@@ -170,7 +195,7 @@
         for m in range(1, j + 1):
             for n in range(m, j):
                 gram[(m, n)] = gram_ref[pl.ds(4 * (m - 1) + n - 1, 1), :]
-            row = total[SUB + m - 1 : SUB + m]
+            row = inner[m - 1]
             gram[(m, j)] = row
             gram_out[pl.ds(4 * (m - 1) + j - 1, 1), :] = row
         _, hess = solve(gram, j)
@@ -180,13 +205,7 @@
     else:
         gram_out[...] = jnp.zeros_like(gram_out)
     if j < KRYLOV:
-        q_out, send_out = outs[0], outs[1]
-        q_out[...] = fresh
-        high = fresh.astype(jnp.bfloat16)
-        low = (fresh - high.astype(jnp.float32)).astype(jnp.bfloat16)
-        for b in range(NZ * NX):
-            send_out[b, pl.ds(0, SUB), :] = high
-            send_out[b, pl.ds(SUB, SUB), :] = low
+        outs[0][...] = fresh
     else:
         dots = outs[0]
         lanes = dots.shape[1]
@@ -203,10 +222,7 @@
         combine_kernel(j, *refs)
 
     if j < KRYLOV:
-        outs = (
-            jax.ShapeDtypeStruct((SUB, cells), jnp.float32),
-            jax.ShapeDtypeStruct((NZ * NX, 2 * SUB, cells), jnp.bfloat16),
-        )
+        outs = (jax.ShapeDtypeStruct((SUB, cells), jnp.float32),)
     else:
         outs = (jax.ShapeDtypeStruct((2 * KRYLOV, cells // 2), jnp.float32),)
     return pl.pallas_call(
@@ -259,9 +275,7 @@
     exchange = lambda v, axes: lax.all_to_all(v, axes, 0, 0, tiled=True)
 
     rates = rate_terms.reshape(TERMS, 2 * NK, HALF, COLS)
-    away = lax.dynamic_index_in_dim(
-        rate_terms.reshape(TERMS, 2, NK, HALF, COLS), 1 - core, 2, keepdims=False
-    )
+    away = rate_terms.reshape(TERMS, 2, NK, HALF, COLS)[:, :, 1]
     got_rates = lax.ppermute(away, "k", SWAP)
 
     onehot = (temp_bins[:, None] == jnp.arange(n_bins, dtype=jnp.int32)[None, :]).astype(
@@ -269,28 +283,29 @@
     )
     weights = jnp.dot(onehot, bin_coeffs, precision=lax.Precision.HIGHEST)
     weights = jnp.pad(weights.T, ((0, 2), (0, 0)))
-    core_id = core.astype(jnp.int32).reshape(1)
-
-    def spread(blocks):
-        met = exchange(blocks, ("z", "x"))
-        own = lax.dynamic_slice_in_dim(met, lax.axis_index("x") * NX, NX, 0)
-        return own, lax.ppermute(own, "k", SWAP)
+    at = jnp.stack([core, lax.axis_index("z"), lax.axis_index("y") // 2]).astype(jnp.int32)
+
+    def spread(piece):
+        both = jnp.stack([piece, lax.ppermute(piece, "k", SWAP)])
+        own = jnp.stack([lax.ppermute(both, ("z", "k", "x"), pairs) for pairs in SPREAD])
+        other = lax.ppermute(own, "k", SWAP)
+        return own.astype(jnp.float32), other.astype(jnp.float32)
+
+    def reduce(partial):
+        return exchange(partial.astype(WIRE), ("x", "y")).astype(jnp.float32)
 
     piece = lax.ppermute(populations.astype(jnp.bfloat16), ALL, TO_INNER)
-    field = spread(jnp.broadcast_to(piece[None], (NZ * NX, SUB, cells)))
-    met = exchange(apply_rates(core_id, rates, got_rates, weights, [field], True), ("x", "y"))
+    met = reduce(apply_rates(at, rates, got_rates, weights, [spread(piece)], True))
     gram = jnp.zeros((16, cells), jnp.float32)
-    q, sent, gram = combine(0, met, gram, [])
+    q, gram = combine(0, met, gram, [])
     pieces, fields = [q], []
     for j in range(1, KRYLOV + 1):
-        fields.append(spread(sent))
+        fields.append(spread(q.astype(WIRE)))
         if j == KRYLOV:
             outer = lax.ppermute(jnp.stack(pieces), ALL, TO_OUTER)
-        met = exchange(
-            apply_rates(core_id, rates, got_rates, weights, fields, False), ("x", "y")
-        )
+        met = reduce(apply_rates(at, rates, got_rates, weights, fields, False))
         if j < KRYLOV:
-            q, sent, gram = combine(j, met, gram, pieces)
+            q, gram = combine(j, met, gram, pieces)
             pieces.append(q)
         else:
             dots, gram = combine(j, met, gram, pieces)

time: 319 us -> 278 us (0.87)
  blocking collectives: 196 us -> 90.4 us
  waiting for transfers between devices: 29.2 us -> 58 us
  other arithmetic: 0.7 us -> 28.7 us
  starting transfers between devices: 27.3 us -> 37.5 us
  local copies, waits for them, and re-layouts: 12.8 us -> 8.16 us
    all_to_all x9 -> x5, blocking collectives: 196 us -> 90.4 us  [body(): exchange = lambda v, axes: lax.all_to_all(v, axes, 0, 0, tiled=True)]
    ppermute x5 -> x20, waiting for transfers between devices: 6.54 us -> 46.4 us  [the longest x10 38.8 us: spread(): lax.ppermute(both, ('z', 'k', 'x'), pairs)]
    ppermute x5 -> x20, starting transfers between devices: 0.61 us -> 27.3 us  [the longest x10 18.3 us: spread(): lax.ppermute(both, ('z', 'k', 'x'), pairs)]
    convert_element_type x0 -> x19, other arithmetic: none -> 20.2 us  [the longest x10 13.2 us: reduce(): return exchange(partial.astype(WIRE), ('x', 'y')).astype(jnp.float32)]
    all_to_all x2 -> x1, starting transfers between devices: 25.3 us -> 8.88 us  [body(): exchange = lambda v, axes: lax.all_to_all(v, axes, 0, 0, tiled=True)]
    all_to_all x2 -> x1, waiting for transfers between devices: 22 us -> 11 us  [body(): exchange = lambda v, axes: lax.all_to_all(v, axes, 0, 0, tiled=True)]
    another operation x0 -> x15, other arithmetic: none -> 7.72 us  [the longest x5 3.7 us: spread(): jnp.stack([lax.ppermute(both, ('z', 'k', 'x'), pairs) for pairs in SPREAD])]
    pallas_call x5, Pallas kernels: 37.6 us -> 41.3 us  [apply_rates(): pl.pallas_call(kernel, out_shape=jax.ShapeDtypeStruct((NX, NY, rows, cell...]
  transfers between devices with their start and end apart: 11 -> 25, of which waited for: 8 -> 16; matrix products, arithmetic and copies ran while one was open for 1% -> 3% of each run, Pallas kernels for 0% -> 0%
where the time goes in v2:
time: 278 us; the launch traced here: 277 us
  blocking collectives  90.4 us (33%)
  waiting for transfers between devices  58 us (21%)
  Pallas kernels  53.7 us (19%)
  starting transfers between devices  37.5 us (13%)
  other arithmetic  28.7 us (10%)
  local copies, waits for them, and re-layouts  8.16 us (3%)
    all_to_all x5, blocking collectives, body(): exchange = lambda v, axes: lax.all_to_all(v, axes, 0, 0, tiled=True)  90.4 us
    pallas_call x5, Pallas kernels, apply_rates(): pl.pallas_call(kernel, out_shape=jax.ShapeDtypeStruct((NX, NY, rows, cell...  41.3 us
    ppermute x10, waiting for transfers between devices, spread(): lax.ppermute(both, ('z', 'k', 'x'), pairs)  38.8 us
    ppermute x10, starting transfers between devices, spread(): lax.ppermute(both, ('z', 'k', 'x'), pairs)  18.3 us
    convert_element_type x10, other arithmetic, reduce(): return exchange(partial.astype(WIRE), ('x', 'y')).astype(jnp.float32)  13.2 us
    all_to_all x1, waiting for transfers between devices, body(): exchange = lambda v, axes: lax.all_to_all(v, axes, 0, 0, tiled=True)  11 us
    pallas_call x5, Pallas kernels, combine(): pl.pallas_call(kernel, out_shape=(*outs, jax.ShapeDtypeStruct(gram.shape,...  10.5 us
    all_to_all x1, starting transfers between devices, body(): exchange = lambda v, axes: lax.all_to_all(v, axes, 0, 0, tiled=True)  8.88 us
  transfers between devices with their start and end apart: 25, of which 16 were waited for; matrix products, arithmetic and copies ran while one was open for 3% of the time, Pallas kernels for 0%

profile of v2, /device:TPU:0, one launch (start us, length us, event | category | flops | bytes accessed | tf_op | source)
XLA Modules:
  0.0 276.9 jit_solution(2916427065663319430)
XLA Ops:
  0.0 3.8 %slice_bitcast_fusion = bf16[6,2,256,512]{3,2,1,0:T(8,128)(2,1)} fusion(bf16[6,2,2,256,512]{4,3,2,1,0:T(8,128)(2,1)} %bitcast.45), kind=kLoop, calls=%fused_computation | loop fusion | bytes 6291456 | tf_op jit(solution)/shard_map/squeeze | solution.py:278
  4.5 5.8 %collective-permute-start.2 = (bf16[64,256]{1,0:T(8,128)(2,1)S(1)}, bf16[64,256]{1,0:T(8,128)(2,1)S(1)}, u32[]{:S(2)}, u32[]{:S(2)}) collective-permute-start(bf16[64,256]{1,0:T(8,128)(2,1)S(1)} %collective-permute-done.1), channel_id=1, source_target_pairs={{0,16},{16,0},{1,17},{17,1},{2,18},{18,2},{3,19},{19,3},{4,20},{20... | collective-permute-start | bytes 98312 | tf_op jit(solution)/shard_map/ppermute | solution.py:289
  11.1 1.9 collective-permute-start.4
  13.7 8.8 %collective-permute-done.4 = bf16[2,64,256]{2,1,0:T(8,128)(2,1)S(1)} collective-permute-done((bf16[2,64,256]{2,1,0:T(8,128)(2,1)S(1)}, bf16[2,64,256]{2,1,0:T(8,128)(2,1)S(1)}, u32[]{:S(2)}, u32[]{:S(2)}) %collective-permute-start.4) | collective-permute-done | bytes 65568 | tf_op jit(solution)/shard_map/ppermute | solution.py:290
  23.3 3.2 %collective-permute-start.5 = (bf16[2,2,64,256]{3,2,1,0:T(8,128)(2,1)S(1)}, bf16[2,2,64,256]{3,2,1,0:T(8,128)(2,1)S(1)}, u32[]{:S(2)}, u32[]{:S(2)}) collective-permute-start(bf16[2,2,64,256]{3,2,1,0:T(8,128)(2,1)S(1)} %get-tuple-element.33), channel_id=1, source_target_pairs={{0,16},{16,0},{1,17},{17,1},{2,18},{18,2},{3,19},{19,3},{4,20},{20... | collective-permute-start | bytes 393224 | tf_op jit(solution)/shard_map/ppermute | solution.py:291
  28.7 1.7 copy-done.1
  30.3 7.0 %rates.5 = f32[4,4,80,256]{3,2,1,0:T(8,128)} custom-call(s32[3]{0:T(128)} %pad_add_fusion.refs_0_, bf16[6,4,256,512]{3,2,1,0:T(8,128)(2,1)} %bitcast.46, bf16[6,2,256,512]{3,2,1,0:T(8,128)(2,1)} %copy-done.1, f32[8,256]{1,0:T(8,128)} %pad.4.refs_3_, f32[2,2,64,256]{3,2,1,0:T(8,128)} %get-tuple-element.34.refs_4_, f32[2,2,64,256]{3,2,1,0:T(8,128)} %convert_element_type.95.refs_5_), custom_call_target="tpu_custom_call" | custom-call | tf_op jit(solution)/shard_map/rates/pallas_call | solution.py:153
  38.7 22.1 %all_to_all.30 = f16[16,80,256]{2,1,0:T(8,128)(2,1)S(1)} all-to-all(f16[16,80,256]{2,1,0:T(8,128)(2,1)S(1)} %bitcast.52), channel_id=1, replica_groups=mesh['z'=4,'k'=2,'x'=4,'y'=4] {'x','y'}, dimensions={0} | all-to-all | bytes 1310720 | tf_op jit(solution)/shard_map/all_to_all | solution.py:275
  62.6 2.0 combine0.1
  67.4 3.3 %collective-permute-start.8 = (f16[2,64,256]{2,1,0:T(8,128)(2,1)S(1)}, f16[2,64,256]{2,1,0:T(8,128)(2,1)S(1)}, u32[]{:S(2)}, u32[]{:S(2)}) collective-permute-start(f16[2,64,256]{2,1,0:T(8,128)(2,1)S(1)} %pad_maximum_fusion.7), channel_id=1, source_target_pairs={{0,32},{4,64},{8,96},{12,0},{16,112},{20,16},{24,48},{28,80},{32,3... | collective-permute-start | bytes 196616 | tf_op jit(solution)/shard_map/ppermute | solution.py:290
  70.7 6.4 %collective-permute-done.8 = f16[2,64,256]{2,1,0:T(8,128)(2,1)S(1)} collective-permute-done((f16[2,64,256]{2,1,0:T(8,128)(2,1)S(1)}, f16[2,64,256]{2,1,0:T(8,128)(2,1)S(1)}, u32[]{:S(2)}, u32[]{:S(2)}) %collective-permute-start.8) | collective-permute-done | bytes 65568 | tf_op jit(solution)/shard_map/ppermute | solution.py:290
  79.9 8.3 %rates.6 = f32[4,4,80,256]{3,2,1,0:T(8,128)} custom-call(s32[3]{0:T(128)} %pad_add_fusion.refs_0_, bf16[6,4,256,512]{3,2,1,0:T(8,128)(2,1)} %bitcast.47, bf16[6,2,256,512]{3,2,1,0:T(8,128)(2,1)} %copy-done.1, f32[8,256]{1,0:T(8,128)} %pad.4.refs_3_, f32[2,2,64,256]{3,2,1,0:T(8,128)} %get-tuple-element.32.refs_4_, ...), custom_call_target="tpu_custom_call" | custom-call | tf_op jit(solution)/shard_map/rates/pallas_call | solution.py:153
  89.6 17.7 %all_to_all.31 = f16[16,80,256]{2,1,0:T(8,128)(2,1)S(1)} all-to-all(f16[16,80,256]{2,1,0:T(8,128)(2,1)S(1)} %bitcast.53), channel_id=1, replica_groups=mesh['z'=4,'k'=2,'x'=4,'y'=4] {'x','y'}, dimensions={0} | all-to-all | bytes 1310720 | tf_op jit(solution)/shard_map/all_to_all | solution.py:275
  108.6 2.1 combine1.1
  113.4 3.3 %collective-permute-start.12 = (f16[2,64,256]{2,1,0:T(8,128)(2,1)S(1)}, f16[2,64,256]{2,1,0:T(8,128)(2,1)S(1)}, u32[]{:S(2)}, u32[]{:S(2)}) collective-permute-start(f16[2,64,256]{2,1,0:T(8,128)(2,1)S(1)} %pad_maximum_fusion.8), channel_id=1, source_target_pairs={{0,32},{4,64},{8,96},{12,0},{16,112},{20,16},{24,48},{28,80},{32,3... | collective-permute-start | bytes 196616 | tf_op jit(solution)/shard_map/ppermute | solution.py:290
  116.6 7.8 %collective-permute-done.12 = f16[2,64,256]{2,1,0:T(8,128)(2,1)S(1)} collective-permute-done((f16[2,64,256]{2,1,0:T(8,128)(2,1)S(1)}, f16[2,64,256]{2,1,0:T(8,128)(2,1)S(1)}, u32[]{:S(2)}, u32[]{:S(2)}) %collective-permute-start.12) | collective-permute-done | bytes 65568 | tf_op jit(solution)/shard_map/ppermute | solution.py:290
  127.3 8.5 %rates.7 = f32[4,4,80,256]{3,2,1,0:T(8,128)} custom-call(s32[3]{0:T(128)} %pad_add_fusion.refs_0_, bf16[6,4,256,512]{3,2,1,0:T(8,128)(2,1)} %bitcast.48, bf16[6,2,256,512]{3,2,1,0:T(8,128)(2,1)} %copy-done.1, f32[8,256]{1,0:T(8,128)} %pad.4.refs_3_, f32[2,2,64,256]{3,2,1,0:T(8,128)} %get-tuple-element.32.refs_4_, ...), custom_call_target="tpu_custom_call" | custom-call | tf_op jit(solution)/shard_map/rates/pallas_call | solution.py:153
  137.2 16.8 %all_to_all.32 = f16[16,80,256]{2,1,0:T(8,128)(2,1)S(1)} all-to-all(f16[16,80,256]{2,1,0:T(8,128)(2,1)S(1)} %bitcast.54), channel_id=1, replica_groups=mesh['z'=4,'k'=2,'x'=4,'y'=4] {'x','y'}, dimensions={0} | all-to-all | bytes 1310720 | tf_op jit(solution)/shard_map/all_to_all | solution.py:275
  155.3 2.1 combine2.1
  160.1 3.3 %collective-permute-start.16 = (f16[2,64,256]{2,1,0:T(8,128)(2,1)S(1)}, f16[2,64,256]{2,1,0:T(8,128)(2,1)S(1)}, u32[]{:S(2)}, u32[]{:S(2)}) collective-permute-start(f16[2,64,256]{2,1,0:T(8,128)(2,1)S(1)} %pad_maximum_fusion.9), channel_id=1, source_target_pairs={{0,32},{4,64},{8,96},{12,0},{16,112},{20,16},{24,48},{28,80},{32,3... | collective-permute-start | bytes 196616 | tf_op jit(solution)/shard_map/ppermute | solution.py:290
  163.3 7.8 %collective-permute-done.16 = f16[2,64,256]{2,1,0:T(8,128)(2,1)S(1)} collective-permute-done((f16[2,64,256]{2,1,0:T(8,128)(2,1)S(1)}, f16[2,64,256]{2,1,0:T(8,128)(2,1)S(1)}, u32[]{:S(2)}, u32[]{:S(2)}) %collective-permute-start.16) | collective-permute-done | bytes 65568 | tf_op jit(solution)/shard_map/ppermute | solution.py:290
  174.0 8.7 %rates.8 = f32[4,4,80,256]{3,2,1,0:T(8,128)} custom-call(s32[3]{0:T(128)} %pad_add_fusion.refs_0_, bf16[6,4,256,512]{3,2,1,0:T(8,128)(2,1)} %bitcast.49, bf16[6,2,256,512]{3,2,1,0:T(8,128)(2,1)} %copy-done.1, f32[8,256]{1,0:T(8,128)} %pad.4.refs_3_, f32[2,2,64,256]{3,2,1,0:T(8,128)} %get-tuple-element.32.refs_4_, ...), custom_call_target="tpu_custom_call" | custom-call | tf_op jit(solution)/shard_map/rates/pallas_call | solution.py:153
  184.1 17.1 %all_to_all.33 = f16[16,80,256]{2,1,0:T(8,128)(2,1)S(1)} all-to-all(f16[16,80,256]{2,1,0:T(8,128)(2,1)S(1)} %bitcast.55), channel_id=1, replica_groups=mesh['z'=4,'k'=2,'x'=4,'y'=4] {'x','y'}, dimensions={0} | all-to-all | bytes 1310720 | tf_op jit(solution)/shard_map/all_to_all | solution.py:275
  202.4 2.2 combine3.1
  207.3 3.3 %collective-permute-start.21 = (f16[2,64,256]{2,1,0:T(8,128)(2,1)S(1)}, f16[2,64,256]{2,1,0:T(8,128)(2,1)S(1)}, u32[]{:S(2)}, u32[]{:S(2)}) collective-permute-start(f16[2,64,256]{2,1,0:T(8,128)(2,1)S(1)} %pad_maximum_fusion.10), channel_id=1, source_target_pairs={{0,32},{4,64},{8,96},{12,0},{16,112},{20,16},{24,48},{28,80},{32,3... | collective-permute-start | bytes 196616 | tf_op jit(solution)/shard_map/ppermute | solution.py:290
  210.6 7.8 %collective-permute-done.21 = f16[2,64,256]{2,1,0:T(8,128)(2,1)S(1)} collective-permute-done((f16[2,64,256]{2,1,0:T(8,128)(2,1)S(1)}, f16[2,64,256]{2,1,0:T(8,128)(2,1)S(1)}, u32[]{:S(2)}, u32[]{:S(2)}) %collective-permute-start.21) | collective-permute-done | bytes 65568 | tf_op jit(solution)/shard_map/ppermute | solution.py:290
  221.3 8.9 %rates.9 = f32[4,4,80,256]{3,2,1,0:T(8,128)} custom-call(s32[3]{0:T(128)} %pad_add_fusion.refs_0_, bf16[6,4,256,512]{3,2,1,0:T(8,128)(2,1)} %bitcast.50, bf16[6,2,256,512]{3,2,1,0:T(8,128)(2,1)} %copy-done.1, f32[8,256]{1,0:T(8,128)} %pad.4.refs_3_, f32[2,2,64,256]{3,2,1,0:T(8,128)} %get-tuple-element.32.refs_4_, ...), custom_call_target="tpu_custom_call" | custom-call | tf_op jit(solution)/shard_map/rates/pallas_call | solution.py:153
  231.6 16.7 %all_to_all.34 = f16[16,80,256]{2,1,0:T(8,128)(2,1)S(1)} all-to-all(f16[16,80,256]{2,1,0:T(8,128)(2,1)S(1)} %bitcast.56), channel_id=1, replica_groups=mesh['z'=4,'k'=2,'x'=4,'y'=4] {'x','y'}, dimensions={0} | all-to-all | bytes 1310720 | tf_op jit(solution)/shard_map/all_to_all | solution.py:275
  249.5 2.2 combine4.1
  254.5 8.9 %all-to-all-start.5 = ((f32[64,8,128]{2,1,0:T(8,128)}), f32[64,8,128]{2,1,0:T(8,128)S(1)}, u32[]{:S(2)}, u32[]{:S(2)}) async-start(f32[64,8,128]{2,1,0:T(8,128)} %broadcast_in_dim.5), calls=%async_computation.5 | async-start | bytes 524288 | tf_op jit(solution)/shard_map/all_to_all | solution.py:275
  263.4 11.0 %all-to-all-done.5.dots_ref = f32[64,8,128]{2,1,0:T(8,128)S(1)} async-done(((f32[64,8,128]{2,1,0:T(8,128)}), f32[64,8,128]{2,1,0:T(8,128)S(1)}, u32[]{:S(2)}, u32[]{:S(2)}) %all-to-all-start.5) | async-done | bytes 262176 | tf_op jit(solution)/shard_map/all_to_all | solution.py:275
  275.1 1.9 finish.1
  (96 shorter events, 44.6 us)
Async XLA Ops:
  0.0 26.5 %copy-start = (f32[64,6]{0,1:T(8,128)S(1)}, f32[64,6]{0,1:T(8,128)}, u32[]{:S(2)}) copy-start(f32[64,6]{0,1:T(8,128)} %param.7) | copy-start | bytes 4612
  0.0 3.8 %copy-start.8 = (f32[64,256]{1,0:T(8,128)S(1)}, f32[64,256]{1,0:T(8,128)}, u32[]{:S(2)}) copy-start(f32[64,256]{1,0:T(8,128)} %p_ref.1) | copy-start | bytes 196612
  0.0 26.5 %copy-start.9 = (s32[256]{0:T(256)S(1)}, s32[256]{0:T(256)}, u32[]{:S(2)}) copy-start(s32[256]{0:T(256)} %param.6) | copy-start | bytes 3076
  3.8 24.9 %collective-permute-start = (bf16[6,2,256,512]{3,2,1,0:T(8,128)(2,1)}, bf16[6,2,256,512]{3,2,1,0:T(8,128)(2,1)S(1)}, u32[]{:S(2)}, u32[]{:S(2)}) collective-permute-start(bf16[6,2,256,512]{3,2,1,0:T(8,128)(2,1)} %slice_bitcast_fusion), channel_id=1, source_target_pairs={{0,16},{16,0},{1,17},{17,1},{2,18},{18,2},{3,19},{19,3},{4,20},{20... | collective-permute-start | bytes 9437192 | tf_op jit(solution)/shard_map/ppermute | solution.py:279
  3.8 0.7 collective-permute-start.1
  4.5 6.6 %collective-permute-start.2 = (bf16[64,256]{1,0:T(8,128)(2,1)S(1)}, bf16[64,256]{1,0:T(8,128)(2,1)S(1)}, u32[]{:S(2)}, u32[]{:S(2)}) collective-permute-start(bf16[64,256]{1,0:T(8,128)(2,1)S(1)} %collective-permute-done.1), channel_id=1, source_target_pairs={{0,16},{16,0},{1,17},{17,1},{2,18},{18,2},{3,19},{19,3},{4,20},{20... | collective-permute-start | bytes 98312 | tf_op jit(solution)/shard_map/ppermute | solution.py:289
  11.1 11.4 %collective-permute-start.4 = (bf16[2,64,256]{2,1,0:T(8,128)(2,1)S(1)}, bf16[2,64,256]{2,1,0:T(8,128)(2,1)S(1)}, u32[]{:S(2)}, u32[]{:S(2)}) collective-permute-start(bf16[2,64,256]{2,1,0:T(8,128)(2,1)S(1)} %pad_maximum_fusion.6), channel_id=1, source_target_pairs={{0,32},{4,64},{8,96},{12,0},{16,112},{20,16},{24,48},{28,80},{32,3... | collective-permute-start | bytes 196616 | tf_op jit(solution)/shard_map/ppermute | solution.py:290
  13.1 9.5 %collective-permute-start.3 = (bf16[2,64,256]{2,1,0:T(8,128)(2,1)S(1)}, bf16[2,64,256]{2,1,0:T(8,128)(2,1)S(1)}, u32[]{:S(2)}, u32[]{:S(2)}) collective-permute-start(bf16[2,64,256]{2,1,0:T(8,128)(2,1)S(1)} %pad_maximum_fusion.6), channel_id=1, source_target_pairs={{0,0},{4,32},{8,64},{12,96},{16,80},{20,112},{24,16},{28,48},{32,4... | collective-permute-start | bytes 196616 | tf_op jit(solution)/shard_map/ppermute | solution.py:290
  23.3 4.6 %collective-permute-start.5 = (bf16[2,2,64,256]{3,2,1,0:T(8,128)(2,1)S(1)}, bf16[2,2,64,256]{3,2,1,0:T(8,128)(2,1)S(1)}, u32[]{:S(2)}, u32[]{:S(2)}) collective-permute-start(bf16[2,2,64,256]{3,2,1,0:T(8,128)(2,1)S(1)} %get-tuple-element.33), channel_id=1, source_target_pairs={{0,16},{16,0},{1,17},{17,1},{2,18},{18,2},{3,19},{19,3},{4,20},{20... | collective-permute-start | bytes 393224 | tf_op jit(solution)/shard_map/ppermute | solution.py:291
  65.5 1.2 collective-permute-start.6
  66.7 3.9 %collective-permute-start.7 = (f16[2,64,256]{2,1,0:T(8,128)(2,1)S(1)}, f16[2,64,256]{2,1,0:T(8,128)(2,1)S(1)}, u32[]{:S(2)}, u32[]{:S(2)}) collective-permute-start(f16[2,64,256]{2,1,0:T(8,128)(2,1)S(1)} %pad_maximum_fusion.7), channel_id=1, source_target_pairs={{0,0},{4,32},{8,64},{12,96},{16,80},{20,112},{24,16},{28,48},{32,4... | collective-permute-start | bytes 196616 | tf_op jit(solution)/shard_map/ppermute | solution.py:290
  67.4 9.7 %collective-permute-start.8 = (f16[2,64,256]{2,1,0:T(8,128)(2,1)S(1)}, f16[2,64,256]{2,1,0:T(8,128)(2,1)S(1)}, u32[]{:S(2)}, u32[]{:S(2)}) collective-permute-start(f16[2,64,256]{2,1,0:T(8,128)(2,1)S(1)} %pad_maximum_fusion.7), channel_id=1, source_target_pairs={{0,32},{4,64},{8,96},{12,0},{16,112},{20,16},{24,48},{28,80},{32,3... | collective-permute-start | bytes 196616 | tf_op jit(solution)/shard_map/ppermute | solution.py:290
  77.9 1.3 collective-permute-start.9
  111.5 1.2 collective-permute-start.10
  112.7 3.9 %collective-permute-start.11 = (f16[2,64,256]{2,1,0:T(8,128)(2,1)S(1)}, f16[2,64,256]{2,1,0:T(8,128)(2,1)S(1)}, u32[]{:S(2)}, u32[]{:S(2)}) collective-permute-start(f16[2,64,256]{2,1,0:T(8,128)(2,1)S(1)} %pad_maximum_fusion.8), channel_id=1, source_target_pairs={{0,0},{4,32},{8,64},{12,96},{16,80},{20,112},{24,16},{28,48},{32,4... | collective-permute-start | bytes 196616 | tf_op jit(solution)/shard_map/ppermute | solution.py:290
  113.4 11.1 %collective-permute-start.12 = (f16[2,64,256]{2,1,0:T(8,128)(2,1)S(1)}, f16[2,64,256]{2,1,0:T(8,128)(2,1)S(1)}, u32[]{:S(2)}, u32[]{:S(2)}) collective-permute-start(f16[2,64,256]{2,1,0:T(8,128)(2,1)S(1)} %pad_maximum_fusion.8), channel_id=1, source_target_pairs={{0,32},{4,64},{8,96},{12,0},{16,112},{20,16},{24,48},{28,80},{32,3... | collective-permute-start | bytes 196616 | tf_op jit(solution)/shard_map/ppermute | solution.py:290
  125.2 1.3 collective-permute-start.13
  158.2 1.2 collective-permute-start.14
  159.4 3.9 %collective-permute-start.15 = (f16[2,64,256]{2,1,0:T(8,128)(2,1)S(1)}, f16[2,64,256]{2,1,0:T(8,128)(2,1)S(1)}, u32[]{:S(2)}, u32[]{:S(2)}) collective-permute-start(f16[2,64,256]{2,1,0:T(8,128)(2,1)S(1)} %pad_maximum_fusion.9), channel_id=1, source_target_pairs={{0,0},{4,32},{8,64},{12,96},{16,80},{20,112},{24,16},{28,48},{32,4... | collective-permute-start | bytes 196616 | tf_op jit(solution)/shard_map/ppermute | solution.py:290
  160.1 11.1 %collective-permute-start.16 = (f16[2,64,256]{2,1,0:T(8,128)(2,1)S(1)}, f16[2,64,256]{2,1,0:T(8,128)(2,1)S(1)}, u32[]{:S(2)}, u32[]{:S(2)}) collective-permute-start(f16[2,64,256]{2,1,0:T(8,128)(2,1)S(1)} %pad_maximum_fusion.9), channel_id=1, source_target_pairs={{0,32},{4,64},{8,96},{12,0},{16,112},{20,16},{24,48},{28,80},{32,3... | collective-permute-start | bytes 196616 | tf_op jit(solution)/shard_map/ppermute | solution.py:290
  171.9 1.3 collective-permute-start.17
  205.4 1.2 collective-permute-start.19
  206.7 3.9 %collective-permute-start.20 = (f16[2,64,256]{2,1,0:T(8,128)(2,1)S(1)}, f16[2,64,256]{2,1,0:T(8,128)(2,1)S(1)}, u32[]{:S(2)}, u32[]{:S(2)}) collective-permute-start(f16[2,64,256]{2,1,0:T(8,128)(2,1)S(1)} %pad_maximum_fusion.10), channel_id=1, source_target_pairs={{0,0},{4,32},{8,64},{12,96},{16,80},{20,112},{24,16},{28,48},{32,4... | collective-permute-start | bytes 196616 | tf_op jit(solution)/shard_map/ppermute | solution.py:290
  207.3 11.1 %collective-permute-start.21 = (f16[2,64,256]{2,1,0:T(8,128)(2,1)S(1)}, f16[2,64,256]{2,1,0:T(8,128)(2,1)S(1)}, u32[]{:S(2)}, u32[]{:S(2)}) collective-permute-start(f16[2,64,256]{2,1,0:T(8,128)(2,1)S(1)} %pad_maximum_fusion.10), channel_id=1, source_target_pairs={{0,32},{4,64},{8,96},{12,0},{16,112},{20,16},{24,48},{28,80},{32,3... | collective-permute-start | bytes 196616 | tf_op jit(solution)/shard_map/ppermute | solution.py:290
  219.2 1.3 collective-permute-start.22
  248.3 3.4 %copy-start.3 = (f32[64,256]{1,0:T(8,128)S(1)}, f32[64,256]{1,0:T(8,128)}, u32[]{:S(2)}) copy-start(f32[64,256]{1,0:T(8,128)} %get-tuple-element.17.refs_3_) | copy-start | bytes 196612
  248.3 3.5 %copy-start.4 = (f32[64,256]{1,0:T(8,128)S(1)}, f32[64,256]{1,0:T(8,128)}, u32[]{:S(2)}) copy-start(f32[64,256]{1,0:T(8,128)} %get-tuple-element.19.refs_4_) | copy-start | bytes 196612
  248.3 3.5 %copy-start.6 = (f32[64,256]{1,0:T(8,128)S(1)}, f32[64,256]{1,0:T(8,128)}, u32[]{:S(2)}) copy-start(f32[64,256]{1,0:T(8,128)} %get-tuple-element.21.refs_5_) | copy-start | bytes 196612
  251.7 1.4 collective-permute-start.23
  251.8 11.6 %collective-permute-start.18 = (f32[4,64,256]{2,1,0:T(8,128)S(1)}, f32[4,64,256]{2,1,0:T(8,128)S(1)}, u32[]{:S(2)}, u32[]{:S(2)}) collective-permute-start(f32[4,64,256]{2,1,0:T(8,128)S(1)} %pad_maximum_fusion), channel_id=1, source_target_pairs={{0,0},{4,1},{8,2},{12,3},{16,4},{20,5},{24,6},{28,7},{1,8},{5,9},{... | collective-permute-start | bytes 786440 | tf_op jit(solution)/shard_map/ppermute | solution.py:305
  254.5 19.9 %all-to-all-start.5 = ((f32[64,8,128]{2,1,0:T(8,128)}), f32[64,8,128]{2,1,0:T(8,128)S(1)}, u32[]{:S(2)}, u32[]{:S(2)}) async-start(f32[64,8,128]{2,1,0:T(8,128)} %broadcast_in_dim.5), calls=%async_computation.5 | async-start | bytes 524288 | tf_op jit(solution)/shard_map/all_to_all | solution.py:275
  263.4 11.0 %copy-start.7 = (f32[4,64,256]{2,1,0:T(8,128)}, f32[4,64,256]{2,1,0:T(8,128)S(1)}, u32[]{:S(2)}) copy-start(f32[4,64,256]{2,1,0:T(8,128)S(1)} %collective-permute-done.18.q_ref) | copy-start | bytes 786436
  (3 other events, 5.8 us)

commit v3 on v2

--- a/solution.py
+++ b/solution.py
@@ -80,46 +80,60 @@
     return combos, hess
 
 
+def call(kernel, name, outs, *operands, scratch=()):
+    vmem = pl.BlockSpec(memory_space=pltpu.VMEM)
+    return pl.pallas_call(
+        kernel,
+        out_shape=outs,
+        in_specs=[
+            pl.BlockSpec(memory_space=pltpu.SMEM) if a.dtype == jnp.int32 else vmem for a in operands
+        ],
+        out_specs=jax.tree.map(lambda _: vmem, outs),
+        scratch_shapes=scratch,
+        compiler_params=pltpu.CompilerParams(vmem_limit_bytes=16 << 20),
+        name=name,
+    )(*operands)
+
+
 def matmul_kernel(n_fields, exact, at_ref, kept_ref, got_ref, w_ref, *refs):
     own_refs, other_refs = refs[:n_fields], refs[n_fields : 2 * n_fields]
     out_ref, x_ref, extra_ref = refs[2 * n_fields :]
-    step = pl.program_id(0)
     core, place, side = at_ref[0], at_ref[1], at_ref[2]
     cells = w_ref.shape[1]
 
-    @pl.when(step == 0)
-    def _():
-        for ref, k in ((own_refs[-1], core), (other_refs[-1], 1 - core)):
-            for t in range(2):
-                x = (place + 2 * NZ - 2 * k - t) % NX
-                for o in range(2):
-                    half = (k + o + side) % 2
-                    rows = pl.ds(pl.multiple_of(half * HALF + x * SUB, SUB), SUB)
-                    value = ref[t, o]
-                    high = value.astype(jnp.bfloat16)
-                    x_ref[rows, pl.ds(0, cells)] = high
-                    if not exact:
-                        low = (value - high.astype(jnp.float32)).astype(jnp.bfloat16)
-                        x_ref[rows, pl.ds(cells, cells)] = low
-        extra_ref[...] = jnp.zeros_like(extra_ref)
-        if not exact:
-            for m in range(n_fields):
-                total = jnp.zeros((8, cells), jnp.float32)
-                for a_ref, b_ref in ((own_refs[m], own_refs[-1]), (other_refs[m], other_refs[-1])):
-                    product = a_ref[...] * b_ref[...]
-                    total = total + jnp.sum(product.reshape(HALF // 8, 8, cells), axis=0)
-                total = jnp.sum(total, axis=0, keepdims=True)
-                power = exponent(total)
-                total = total * jnp.exp2(-power)
-                high = total.astype(jnp.bfloat16).astype(jnp.float32)
-                extra_ref[pl.ds(3 * m + 1, 1), :] = power
-                extra_ref[pl.ds(3 * m + 2, 1), :] = high
-                extra_ref[pl.ds(3 * m + 3, 1), :] = (total - high) * 256.0
-
-    def part(rates):
+    for ref, k in ((own_refs[-1], core), (other_refs[-1], 1 - core)):
+        for t in range(2):
+            x = (place + 2 * NZ - 2 * k - t) % NX
+            for o in range(2):
+                half = (k + o + side) % 2
+                rows = pl.ds(pl.multiple_of(half * HALF + x * SUB, SUB), SUB)
+                value = ref[t, o].astype(jnp.float32)
+                high = value.astype(jnp.bfloat16)
+                x_ref[rows, pl.ds(0, cells)] = high
+                if not exact:
+                    low = (value - high.astype(jnp.float32)).astype(jnp.bfloat16)
+                    x_ref[rows, pl.ds(cells, cells)] = low
+    extra_ref[...] = jnp.zeros_like(extra_ref)
+    if not exact:
+        for m in range(n_fields):
+            total = jnp.zeros((8, cells), jnp.float32)
+            for a_ref, b_ref in ((own_refs[m], own_refs[-1]), (other_refs[m], other_refs[-1])):
+                product = a_ref[...] * b_ref[...]
+                total = total + jnp.sum(product.reshape(HALF // 8, 8, cells), axis=0)
+            total = jnp.sum(total, axis=0, keepdims=True)
+            power = exponent(total)
+            total = total * jnp.exp2(-power)
+            high = total.astype(jnp.bfloat16).astype(jnp.float32)
+            extra_ref[pl.ds(3 * m + 1, 1), :] = power
+            extra_ref[pl.ds(3 * m + 2, 1), :] = high
+            extra_ref[pl.ds(3 * m + 3, 1), :] = (total - high) * 256.0
+
+    for g in range(NY):
+        y = (g + 2 * core) % NY
         total = None
         for j in range(TERMS):
-            product = jnp.dot(rates[j, 0], x_ref[...], preferred_element_type=jnp.float32)
+            rates = kept_ref[j, 2 * g] if g < 2 else got_ref[j, g - 2]
+            product = jnp.dot(rates, x_ref[...], preferred_element_type=jnp.float32)
             if not exact:
                 product = product[:, :cells] + product[:, cells:]
             product = w_ref[pl.ds(j, 1), :] * product
@@ -127,52 +141,34 @@
         for x in range(NX):
             block = total[x * SUB : (x + 1) * SUB, :]
             power = exponent(jnp.max(jnp.abs(block), axis=0, keepdims=True))
-            out_ref[x, 0, pl.ds(0, SUB), :] = block * jnp.exp2(-power)
-            out_ref[x, 0, pl.ds(SUB, EXTRA), :] = extra_ref[...]
-            out_ref[x, 0, pl.ds(SUB, 1), :] = power
-
-    @pl.when(step < 2)
-    def _():
-        part(kept_ref)
-
-    @pl.when(step >= 2)
-    def _():
-        part(got_ref)
+            out_ref[x, y, pl.ds(0, SUB), :] = block * jnp.exp2(-power)
+            out_ref[x, y, pl.ds(SUB, EXTRA), :] = extra_ref[...]
+            out_ref[x, y, pl.ds(SUB, 1), :] = power
 
 
 def apply_rates(at, kept, got, weights, fields, exact):
     cells = weights.shape[1]
     rows = SUB + EXTRA
-    whole = lambda a: pl.BlockSpec(a.shape, lambda g, at: (0,) * a.ndim)
     own, other = [f[0] for f in fields], [f[1] for f in fields]
-    block = (TERMS, 1, HALF, COLS)
 
     def kernel(*refs):
         matmul_kernel(len(fields), exact, *refs)
 
-    out = pl.pallas_call(
+    out = call(
         kernel,
-        out_shape=jax.ShapeDtypeStruct((NX, NY, rows, cells), jnp.float32),
-        grid_spec=pltpu.PrefetchScalarGridSpec(
-            num_scalar_prefetch=1,
-            grid=(NY,),
-            in_specs=[
-                pl.BlockSpec(block, lambda g, at: (0, 2 * jnp.minimum(g, 1), 0, 0)),
-                pl.BlockSpec(block, lambda g, at: (0, jnp.maximum(g - 2, 0), 0, 0)),
-                whole(weights),
-                *[whole(a) for a in own],
-                *[whole(a) for a in other],
-            ],
-            out_specs=pl.BlockSpec(
-                (NX, 1, rows, cells), lambda g, at: (0, (g + 2 * at[0]) % NY, 0, 0)
-            ),
-            scratch_shapes=[
-                pltpu.VMEM((COLS, cells if exact else 2 * cells), jnp.bfloat16),
-                pltpu.VMEM((EXTRA, cells), jnp.float32),
-            ],
-        ),
-        name="rates",
-    )(at, kept, got, weights, *own, *other)
+        "rates",
+        jax.ShapeDtypeStruct((NX, NY, rows, cells), jnp.float32),
+        at,
+        kept,
+        got,
+        weights,
+        *own,
+        *other,
+        scratch=[
+            pltpu.VMEM((COLS, cells if exact else 2 * cells), jnp.bfloat16),
+            pltpu.VMEM((EXTRA, cells), jnp.float32),
+        ],
+    )
     return out.reshape(NX * NY, rows, cells)
 
 
@@ -225,11 +221,8 @@
         outs = (jax.ShapeDtypeStruct((SUB, cells), jnp.float32),)
     else:
         outs = (jax.ShapeDtypeStruct((2 * KRYLOV, cells // 2), jnp.float32),)
-    return pl.pallas_call(
-        kernel,
-        out_shape=(*outs, jax.ShapeDtypeStruct(gram.shape, jnp.float32)),
-        name=f"combine{j}",
-    )(got, gram, *fields)
+    outs = (*outs, jax.ShapeDtypeStruct(gram.shape, jnp.float32))
+    return call(kernel, f"combine{j}", outs, got, gram, *fields)
 
 
 def finish_kernel(p_ref, q_ref, gram_ref, dots_ref, out_ref):
@@ -275,8 +268,10 @@
     exchange = lambda v, axes: lax.all_to_all(v, axes, 0, 0, tiled=True)
 
     rates = rate_terms.reshape(TERMS, 2 * NK, HALF, COLS)
+    rates = pltpu.with_memory_space_constraint(rates, pltpu.VMEM)
     away = rate_terms.reshape(TERMS, 2, NK, HALF, COLS)[:, :, 1]
     got_rates = lax.ppermute(away, "k", SWAP)
+    got_rates = pltpu.with_memory_space_constraint(got_rates, pltpu.VMEM)
 
     onehot = (temp_bins[:, None] == jnp.arange(n_bins, dtype=jnp.int32)[None, :]).astype(
         jnp.float32
@@ -311,11 +306,8 @@
             dots, gram = combine(j, met, gram, pieces)
     dots = dots + lax.ppermute(dots, "k", SWAP)
     dots = exchange(jnp.broadcast_to(dots[None], (NZ * NX * NY, *dots.shape)), ("z", "x", "y"))
-    return pl.pallas_call(
-        finish_kernel,
-        out_shape=jax.ShapeDtypeStruct(populations.shape, jnp.float32),
-        name="finish",
-    )(populations, outer, gram, dots)
+    out = jax.ShapeDtypeStruct(populations.shape, jnp.float32)
+    return call(finish_kernel, "finish", out, populations, outer, gram, dots)
 
 
 def solution(mesh):

time: 278 us -> 224 us (0.81)
  Pallas kernels: 53.7 us -> 20.8 us
  other arithmetic: 28.7 us -> 3.37 us
  waiting for transfers between devices: 58 us -> 62.1 us
    pallas_call x11, Pallas kernels: 53.7 us -> 20.8 us  [call(): pl.pallas_call(kernel, out_shape=outs, in_specs=[pl.BlockSpec(memory_spac...]
    convert_element_type x10, other arithmetic: 13.2 us -> 1.25 us  [reduce(): return exchange(partial.astype(WIRE), ('x', 'y')).astype(jnp.float32)]
    another operation x9, other arithmetic: 3.47 us -> 0.12 us  [spread(): both = jnp.stack([piece, lax.ppermute(piece, 'k', SWAP)])]
    convert_element_type x4, other arithmetic: 3.38 us -> 0.03 us  [body(): fields.append(spread(q.astype(WIRE)))]
    ppermute x5, waiting for transfers between devices: 2.28 us -> 5.58 us  [spread(): both = jnp.stack([piece, lax.ppermute(piece, 'k', SWAP)])]
    another operation x5, other arithmetic: 3.7 us -> 0.81 us  [spread(): jnp.stack([lax.ppermute(both, ('z', 'k', 'x'), pairs) for pairs in SPREAD])]
  transfers between devices with their start and end apart: 25 -> 25, of which waited for: 16 -> 17; matrix products, arithmetic and copies ran while one was open for 3% -> 1% of each run, Pallas kernels for 0% -> 0%
where the time goes in v3:
time: 224 us
  blocking collectives  90.7 us (40%)
  waiting for transfers between devices  62.1 us (28%)
  starting transfers between devices  38.9 us (17%)
  Pallas kernels  20.8 us (9%)
  local copies, waits for them, and re-layouts  7.29 us (3%)
  other arithmetic  3.37 us (2%)
    all_to_all x5, blocking collectives, body(): exchange = lambda v, axes: lax.all_to_all(v, axes, 0, 0, tiled=True)  90.7 us
    ppermute x10, waiting for transfers between devices, spread(): lax.ppermute(both, ('z', 'k', 'x'), pairs)  38.8 us
    pallas_call x11, Pallas kernels, call(): pl.pallas_call(kernel, out_shape=outs, in_specs=[pl.BlockSpec(memory_spac...  20.8 us
    ppermute x10, starting transfers between devices, spread(): lax.ppermute(both, ('z', 'k', 'x'), pairs)  18.3 us
    all_to_all x1, waiting for transfers between devices, body(): exchange = lambda v, axes: lax.all_to_all(v, axes, 0, 0, tiled=True)  11 us
    all_to_all x1, starting transfers between devices, body(): exchange = lambda v, axes: lax.all_to_all(v, axes, 0, 0, tiled=True)  9.1 us
    ppermute x5, waiting for transfers between devices, spread(): other = lax.ppermute(own, 'k', SWAP)  6.33 us
    ppermute x5, starting transfers between devices, spread(): both = jnp.stack([piece, lax.ppermute(piece, 'k', SWAP)])  6.12 us
  transfers between devices with their start and end apart: 25, of which 17 were waited for; matrix products, arithmetic and copies ran while one was open for 1% of the time, Pallas kernels for 0%

profile of v3, /device:TPU:0, one launch (start us, length us, event | category | flops | bytes accessed | tf_op | source)
XLA Modules:
  0.0 223.8 jit_solution(1331439190179733009)
XLA Ops:
  0.0 3.8 %slice_bitcast_fusion = bf16[6,2,256,512]{3,2,1,0:T(8,128)(2,1)} fusion(bf16[6,2,2,256,512]{4,3,2,1,0:T(8,128)(2,1)} %bitcast.45), kind=kLoop, calls=%fused_computation | loop fusion | bytes 6291456 | tf_op jit(solution)/shard_map/squeeze | solution.py:272
  4.5 5.8 %collective-permute-start.2 = (bf16[64,256]{1,0:T(8,128)(2,1)S(1)}, bf16[64,256]{1,0:T(8,128)(2,1)S(1)}, u32[]{:S(2)}, u32[]{:S(2)}) collective-permute-start(bf16[64,256]{1,0:T(8,128)(2,1)S(1)} %collective-permute-done.1), channel_id=1, source_target_pairs={{0,16},{16,0},{1,17},{17,1},{2,18},{18,2},{3,19},{19,3},{4,20},{20... | collective-permute-start | bytes 98312 | tf_op jit(solution)/shard_map/ppermute | solution.py:284
  11.1 1.9 collective-permute-start.4
  13.7 8.8 %collective-permute-done.4 = bf16[2,64,256]{2,1,0:T(8,128)(2,1)S(1)} collective-permute-done((bf16[2,64,256]{2,1,0:T(8,128)(2,1)S(1)}, bf16[2,64,256]{2,1,0:T(8,128)(2,1)S(1)}, u32[]{:S(2)}, u32[]{:S(2)}) %collective-permute-start.4) | collective-permute-done | bytes 65568 | tf_op jit(solution)/shard_map/ppermute | solution.py:285
  23.2 3.2 %collective-permute-start.5 = (bf16[2,2,64,256]{3,2,1,0:T(8,128)(2,1)}, bf16[2,2,64,256]{3,2,1,0:T(8,128)(2,1)}, u32[]{:S(2)}, u32[]{:S(2)}) collective-permute-start(bf16[2,2,64,256]{3,2,1,0:T(8,128)(2,1)} %get-tuple-element.33), channel_id=1, source_target_pairs={{0,16},{16,0},{1,17},{17,1},{2,18},{18,2},{3,19},{19,3},{4,20},{20... | collective-permute-start | bytes 393224 | tf_op jit(solution)/shard_map/ppermute | solution.py:286
  28.7 2.8 %copy-done.1 = bf16[6,1024,512]{2,1,0:T(8,128)(2,1)S(1)} copy-done((bf16[6,1024,512]{2,1,0:T(8,128)(2,1)S(1)}, bf16[6,1024,512]{2,1,0:T(8,128)(2,1)}, u32[]{:S(2)}) %copy-start.1) | copy-done | bytes 6291480
  31.5 2.4 %rates.5 = f32[4,4,80,256]{3,2,1,0:T(8,128)S(1)} custom-call(s32[3]{0:T(128)S(1)} %pad_add_fusion.refs_0_, bf16[6,4,256,512]{3,2,1,0:T(8,128)(2,1)S(1)} %bitcast.46, bf16[6,2,256,512]{3,2,1,0:T(8,128)(2,1)S(1)} %collective-permute-done.refs_2_, f32[8,256]{1,0:T(8,128)S(1)} %pad.4.refs_3_, f32[2,2,64,256]{3,2,1,0:T(8,128)S(1)} %get-tuple-element.34.refs_4_, ...), custom_call_target="tpu_custom_call" | custom-call | tf_op jit(solution)/shard_map/rates/pallas_call | solution.py:85
  34.1 22.4 %all_to_all.30 = f16[16,80,256]{2,1,0:T(8,128)(2,1)S(1)} all-to-all(f16[16,80,256]{2,1,0:T(8,128)(2,1)S(1)} %bitcast.55), channel_id=1, replica_groups=mesh['z'=4,'k'=2,'x'=4,'y'=4] {'x','y'}, dimensions={0} | all-to-all | bytes 1310720 | tf_op jit(solution)/shard_map/all_to_all | solution.py:268
  56.8 1.2 collective-permute-done.6
  58.7 3.3 %collective-permute-start.8 = (f16[2,64,256]{2,1,0:T(8,128)(2,1)S(1)}, f16[2,64,256]{2,1,0:T(8,128)(2,1)S(1)}, u32[]{:S(2)}, u32[]{:S(2)}) collective-permute-start(f16[2,64,256]{2,1,0:T(8,128)(2,1)S(1)} %pad_maximum_fusion.7), channel_id=1, source_target_pairs={{0,32},{4,64},{8,96},{12,0},{16,112},{20,16},{24,48},{28,80},{32,3... | collective-permute-start | bytes 196616 | tf_op jit(solution)/shard_map/ppermute | solution.py:285
  61.9 6.4 %collective-permute-done.8 = f16[2,64,256]{2,1,0:T(8,128)(2,1)S(1)} collective-permute-done((f16[2,64,256]{2,1,0:T(8,128)(2,1)S(1)}, f16[2,64,256]{2,1,0:T(8,128)(2,1)S(1)}, u32[]{:S(2)}, u32[]{:S(2)}) %collective-permute-start.8) | collective-permute-done | bytes 65568 | tf_op jit(solution)/shard_map/ppermute | solution.py:285
  68.5 1.3 collective-permute-done.9
  69.9 4.1 %rates.6 = f32[4,4,80,256]{3,2,1,0:T(8,128)S(1)} custom-call(s32[3]{0:T(128)S(1)} %pad_add_fusion.refs_0_, bf16[6,4,256,512]{3,2,1,0:T(8,128)(2,1)S(1)} %bitcast.47, bf16[6,2,256,512]{3,2,1,0:T(8,128)(2,1)S(1)} %collective-permute-done.refs_2_, f32[8,256]{1,0:T(8,128)S(1)} %pad.4.refs_3_, f32[2,2,64,256]{3,2,1,0:T(8,128)S(1)} %get-tuple-element.32.refs_4_, ...), custom_call_target="tpu_custom_call" | custom-call | tf_op jit(solution)/shard_map/rates/pallas_call | solution.py:85
  74.1 17.7 %all_to_all.31 = f16[16,80,256]{2,1,0:T(8,128)(2,1)S(1)} all-to-all(f16[16,80,256]{2,1,0:T(8,128)(2,1)S(1)} %bitcast.56), channel_id=1, replica_groups=mesh['z'=4,'k'=2,'x'=4,'y'=4] {'x','y'}, dimensions={0} | all-to-all | bytes 1310720 | tf_op jit(solution)/shard_map/all_to_all | solution.py:268
  94.1 3.3 %collective-permute-start.12 = (f16[2,64,256]{2,1,0:T(8,128)(2,1)S(1)}, f16[2,64,256]{2,1,0:T(8,128)(2,1)S(1)}, u32[]{:S(2)}, u32[]{:S(2)}) collective-permute-start(f16[2,64,256]{2,1,0:T(8,128)(2,1)S(1)} %pad_maximum_fusion.8), channel_id=1, source_target_pairs={{0,32},{4,64},{8,96},{12,0},{16,112},{20,16},{24,48},{28,80},{32,3... | collective-permute-start | bytes 196616 | tf_op jit(solution)/shard_map/ppermute | solution.py:285
  97.4 7.8 %collective-permute-done.12 = f16[2,64,256]{2,1,0:T(8,128)(2,1)S(1)} collective-permute-done((f16[2,64,256]{2,1,0:T(8,128)(2,1)S(1)}, f16[2,64,256]{2,1,0:T(8,128)(2,1)S(1)}, u32[]{:S(2)}, u32[]{:S(2)}) %collective-permute-start.12) | collective-permute-done | bytes 65568 | tf_op jit(solution)/shard_map/ppermute | solution.py:285
  105.5 1.3 collective-permute-done.13
  106.9 4.2 %rates.7 = f32[4,4,80,256]{3,2,1,0:T(8,128)S(1)} custom-call(s32[3]{0:T(128)S(1)} %pad_add_fusion.refs_0_, bf16[6,4,256,512]{3,2,1,0:T(8,128)(2,1)S(1)} %bitcast.48, bf16[6,2,256,512]{3,2,1,0:T(8,128)(2,1)S(1)} %collective-permute-done.refs_2_, f32[8,256]{1,0:T(8,128)S(1)} %pad.4.refs_3_, f32[2,2,64,256]{3,2,1,0:T(8,128)S(1)} %get-tuple-element.32.refs_4_, ...), custom_call_target="tpu_custom_call" | custom-call | tf_op jit(solution)/shard_map/rates/pallas_call | solution.py:85
  111.3 16.8 %all_to_all.32 = f16[16,80,256]{2,1,0:T(8,128)(2,1)S(1)} all-to-all(f16[16,80,256]{2,1,0:T(8,128)(2,1)S(1)} %bitcast.57), channel_id=1, replica_groups=mesh['z'=4,'k'=2,'x'=4,'y'=4] {'x','y'}, dimensions={0} | all-to-all | bytes 1310720 | tf_op jit(solution)/shard_map/all_to_all | solution.py:268
  128.4 1.2 collective-permute-done.14
  130.3 3.3 %collective-permute-start.16 = (f16[2,64,256]{2,1,0:T(8,128)(2,1)S(1)}, f16[2,64,256]{2,1,0:T(8,128)(2,1)S(1)}, u32[]{:S(2)}, u32[]{:S(2)}) collective-permute-start(f16[2,64,256]{2,1,0:T(8,128)(2,1)S(1)} %pad_maximum_fusion.9), channel_id=1, source_target_pairs={{0,32},{4,64},{8,96},{12,0},{16,112},{20,16},{24,48},{28,80},{32,3... | collective-permute-start | bytes 196616 | tf_op jit(solution)/shard_map/ppermute | solution.py:285
  133.6 7.8 %collective-permute-done.16 = f16[2,64,256]{2,1,0:T(8,128)(2,1)S(1)} collective-permute-done((f16[2,64,256]{2,1,0:T(8,128)(2,1)S(1)}, f16[2,64,256]{2,1,0:T(8,128)(2,1)S(1)}, u32[]{:S(2)}, u32[]{:S(2)}) %collective-permute-start.16) | collective-permute-done | bytes 65568 | tf_op jit(solution)/shard_map/ppermute | solution.py:285
  141.5 1.3 collective-permute-done.17
  142.9 4.2 %rates.8 = f32[4,4,80,256]{3,2,1,0:T(8,128)S(1)} custom-call(s32[3]{0:T(128)S(1)} %pad_add_fusion.refs_0_, bf16[6,4,256,512]{3,2,1,0:T(8,128)(2,1)S(1)} %bitcast.49, bf16[6,2,256,512]{3,2,1,0:T(8,128)(2,1)S(1)} %collective-permute-done.refs_2_, f32[8,256]{1,0:T(8,128)S(1)} %pad.4.refs_3_, f32[2,2,64,256]{3,2,1,0:T(8,128)S(1)} %get-tuple-element.32.refs_4_, ...), custom_call_target="tpu_custom_call" | custom-call | tf_op jit(solution)/shard_map/rates/pallas_call | solution.py:85
  147.3 17.1 %all_to_all.33 = f16[16,80,256]{2,1,0:T(8,128)(2,1)S(1)} all-to-all(f16[16,80,256]{2,1,0:T(8,128)(2,1)S(1)} %bitcast.58), channel_id=1, replica_groups=mesh['z'=4,'k'=2,'x'=4,'y'=4] {'x','y'}, dimensions={0} | all-to-all | bytes 1310720 | tf_op jit(solution)/shard_map/all_to_all | solution.py:268
  166.7 3.3 %collective-permute-start.21 = (f16[2,64,256]{2,1,0:T(8,128)(2,1)S(1)}, f16[2,64,256]{2,1,0:T(8,128)(2,1)S(1)}, u32[]{:S(2)}, u32[]{:S(2)}) collective-permute-start(f16[2,64,256]{2,1,0:T(8,128)(2,1)S(1)} %pad_maximum_fusion.10), channel_id=1, source_target_pairs={{0,32},{4,64},{8,96},{12,0},{16,112},{20,16},{24,48},{28,80},{32,3... | collective-permute-start | bytes 196616 | tf_op jit(solution)/shard_map/ppermute | solution.py:285
  170.0 7.8 %collective-permute-done.21 = f16[2,64,256]{2,1,0:T(8,128)(2,1)S(1)} collective-permute-done((f16[2,64,256]{2,1,0:T(8,128)(2,1)S(1)}, f16[2,64,256]{2,1,0:T(8,128)(2,1)S(1)}, u32[]{:S(2)}, u32[]{:S(2)}) %collective-permute-start.21) | collective-permute-done | bytes 65568 | tf_op jit(solution)/shard_map/ppermute | solution.py:285
  178.2 1.3 collective-permute-done.22
  179.5 4.3 %rates.9 = f32[4,4,80,256]{3,2,1,0:T(8,128)S(1)} custom-call(s32[3]{0:T(128)S(1)} %pad_add_fusion.refs_0_, bf16[6,4,256,512]{3,2,1,0:T(8,128)(2,1)S(1)} %bitcast.50, bf16[6,2,256,512]{3,2,1,0:T(8,128)(2,1)S(1)} %collective-permute-done.refs_2_, f32[8,256]{1,0:T(8,128)S(1)} %pad.4.refs_3_, f32[2,2,64,256]{3,2,1,0:T(8,128)S(1)} %get-tuple-element.32.refs_4_, ...), custom_call_target="tpu_custom_call" | custom-call | tf_op jit(solution)/shard_map/rates/pallas_call | solution.py:85
  183.9 16.7 %all_to_all.34 = f16[16,80,256]{2,1,0:T(8,128)(2,1)S(1)} all-to-all(f16[16,80,256]{2,1,0:T(8,128)(2,1)S(1)} %bitcast.59), channel_id=1, replica_groups=mesh['z'=4,'k'=2,'x'=4,'y'=4] {'x','y'}, dimensions={0} | all-to-all | bytes 1310720 | tf_op jit(solution)/shard_map/all_to_all | solution.py:268
  202.9 9.1 %all-to-all-start.5 = ((f32[64,8,128]{2,1,0:T(8,128)}), f32[64,8,128]{2,1,0:T(8,128)S(1)}, u32[]{:S(2)}, u32[]{:S(2)}) async-start(f32[64,8,128]{2,1,0:T(8,128)} %broadcast_in_dim.5), calls=%async_computation.5 | async-start | bytes 524288 | tf_op jit(solution)/shard_map/all_to_all | solution.py:268
  212.1 11.0 %all-to-all-done.5.dots_ref = f32[64,8,128]{2,1,0:T(8,128)S(1)} async-done(((f32[64,8,128]{2,1,0:T(8,128)}), f32[64,8,128]{2,1,0:T(8,128)S(1)}, u32[]{:S(2)}, u32[]{:S(2)}) %all-to-all-start.5) | async-done | bytes 262176 | tf_op jit(solution)/shard_map/all_to_all | solution.py:268
  (86 shorter events, 16.3 us)
Async XLA Ops:
  0.0 26.4 %copy-start = (f32[64,6]{0,1:T(8,128)S(1)}, f32[64,6]{0,1:T(8,128)}, u32[]{:S(2)}) copy-start(f32[64,6]{0,1:T(8,128)} %param.7) | copy-start | bytes 4612
  0.0 3.8 %copy-start.3 = (f32[64,256]{1,0:T(8,128)S(1)}, f32[64,256]{1,0:T(8,128)}, u32[]{:S(2)}) copy-start(f32[64,256]{1,0:T(8,128)} %p_ref.1) | copy-start | bytes 196612
  0.0 26.4 %copy-start.4 = (s32[256]{0:T(256)S(1)}, s32[256]{0:T(256)}, u32[]{:S(2)}) copy-start(s32[256]{0:T(256)} %param.6) | copy-start | bytes 3076
  3.8 24.9 %collective-permute-start = (bf16[6,2,256,512]{3,2,1,0:T(8,128)(2,1)}, bf16[6,2,256,512]{3,2,1,0:T(8,128)(2,1)S(1)}, u32[]{:S(2)}, u32[]{:S(2)}) collective-permute-start(bf16[6,2,256,512]{3,2,1,0:T(8,128)(2,1)} %slice_bitcast_fusion), channel_id=1, source_target_pairs={{0,16},{16,0},{1,17},{17,1},{2,18},{18,2},{3,19},{19,3},{4,20},{20... | collective-permute-start | bytes 9437192 | tf_op jit(solution)/shard_map/ppermute | solution.py:273
  3.8 0.7 collective-permute-start.1
  4.5 6.6 %collective-permute-start.2 = (bf16[64,256]{1,0:T(8,128)(2,1)S(1)}, bf16[64,256]{1,0:T(8,128)(2,1)S(1)}, u32[]{:S(2)}, u32[]{:S(2)}) collective-permute-start(bf16[64,256]{1,0:T(8,128)(2,1)S(1)} %collective-permute-done.1), channel_id=1, source_target_pairs={{0,16},{16,0},{1,17},{17,1},{2,18},{18,2},{3,19},{19,3},{4,20},{20... | collective-permute-start | bytes 98312 | tf_op jit(solution)/shard_map/ppermute | solution.py:284
  11.1 11.4 %collective-permute-start.4 = (bf16[2,64,256]{2,1,0:T(8,128)(2,1)S(1)}, bf16[2,64,256]{2,1,0:T(8,128)(2,1)S(1)}, u32[]{:S(2)}, u32[]{:S(2)}) collective-permute-start(bf16[2,64,256]{2,1,0:T(8,128)(2,1)S(1)} %pad_maximum_fusion.6), channel_id=1, source_target_pairs={{0,32},{4,64},{8,96},{12,0},{16,112},{20,16},{24,48},{28,80},{32,3... | collective-permute-start | bytes 196616 | tf_op jit(solution)/shard_map/ppermute | solution.py:285
  13.0 9.5 %collective-permute-start.3 = (bf16[2,64,256]{2,1,0:T(8,128)(2,1)S(1)}, bf16[2,64,256]{2,1,0:T(8,128)(2,1)S(1)}, u32[]{:S(2)}, u32[]{:S(2)}) collective-permute-start(bf16[2,64,256]{2,1,0:T(8,128)(2,1)S(1)} %pad_maximum_fusion.6), channel_id=1, source_target_pairs={{0,0},{4,32},{8,64},{12,96},{16,80},{20,112},{24,16},{28,48},{32,4... | collective-permute-start | bytes 196616 | tf_op jit(solution)/shard_map/ppermute | solution.py:285
  23.2 4.5 %collective-permute-start.5 = (bf16[2,2,64,256]{3,2,1,0:T(8,128)(2,1)}, bf16[2,2,64,256]{3,2,1,0:T(8,128)(2,1)}, u32[]{:S(2)}, u32[]{:S(2)}) collective-permute-start(bf16[2,2,64,256]{3,2,1,0:T(8,128)(2,1)} %get-tuple-element.33), channel_id=1, source_target_pairs={{0,16},{16,0},{1,17},{17,1},{2,18},{18,2},{3,19},{19,3},{4,20},{20... | collective-permute-start | bytes 393224 | tf_op jit(solution)/shard_map/ppermute | solution.py:286
  28.7 2.8 %copy-start.1 = (bf16[6,1024,512]{2,1,0:T(8,128)(2,1)S(1)}, bf16[6,1024,512]{2,1,0:T(8,128)(2,1)}, u32[]{:S(2)}) copy-start(bf16[6,1024,512]{2,1,0:T(8,128)(2,1)} %param.4) | copy-start | bytes 18874372
  33.9 35.9 %copy-start.2 = (bf16[6,1024,512]{2,1,0:T(8,128)(2,1)S(1)}, bf16[6,1024,512]{2,1,0:T(8,128)(2,1)}, u32[]{:S(2)}) copy-start(bf16[6,1024,512]{2,1,0:T(8,128)(2,1)} %param.4) | copy-start | bytes 18874372
  56.7 1.3 collective-permute-start.6
  58.0 3.9 %collective-permute-start.7 = (f16[2,64,256]{2,1,0:T(8,128)(2,1)S(1)}, f16[2,64,256]{2,1,0:T(8,128)(2,1)S(1)}, u32[]{:S(2)}, u32[]{:S(2)}) collective-permute-start(f16[2,64,256]{2,1,0:T(8,128)(2,1)S(1)} %pad_maximum_fusion.7), channel_id=1, source_target_pairs={{0,0},{4,32},{8,64},{12,96},{16,80},{20,112},{24,16},{28,48},{32,4... | collective-permute-start | bytes 196616 | tf_op jit(solution)/shard_map/ppermute | solution.py:285
  58.7 9.7 %collective-permute-start.8 = (f16[2,64,256]{2,1,0:T(8,128)(2,1)S(1)}, f16[2,64,256]{2,1,0:T(8,128)(2,1)S(1)}, u32[]{:S(2)}, u32[]{:S(2)}) collective-permute-start(f16[2,64,256]{2,1,0:T(8,128)(2,1)S(1)} %pad_maximum_fusion.7), channel_id=1, source_target_pairs={{0,32},{4,64},{8,96},{12,0},{16,112},{20,16},{24,48},{28,80},{32,3... | collective-permute-start | bytes 196616 | tf_op jit(solution)/shard_map/ppermute | solution.py:285
  68.4 1.4 collective-permute-start.9
  92.1 1.3 collective-permute-start.10
  93.4 3.9 %collective-permute-start.11 = (f16[2,64,256]{2,1,0:T(8,128)(2,1)S(1)}, f16[2,64,256]{2,1,0:T(8,128)(2,1)S(1)}, u32[]{:S(2)}, u32[]{:S(2)}) collective-permute-start(f16[2,64,256]{2,1,0:T(8,128)(2,1)S(1)} %pad_maximum_fusion.8), channel_id=1, source_target_pairs={{0,0},{4,32},{8,64},{12,96},{16,80},{20,112},{24,16},{28,48},{32,4... | collective-permute-start | bytes 196616 | tf_op jit(solution)/shard_map/ppermute | solution.py:285
  94.1 11.1 %collective-permute-start.12 = (f16[2,64,256]{2,1,0:T(8,128)(2,1)S(1)}, f16[2,64,256]{2,1,0:T(8,128)(2,1)S(1)}, u32[]{:S(2)}, u32[]{:S(2)}) collective-permute-start(f16[2,64,256]{2,1,0:T(8,128)(2,1)S(1)} %pad_maximum_fusion.8), channel_id=1, source_target_pairs={{0,32},{4,64},{8,96},{12,0},{16,112},{20,16},{24,48},{28,80},{32,3... | collective-permute-start | bytes 196616 | tf_op jit(solution)/shard_map/ppermute | solution.py:285
  105.2 1.6 collective-permute-start.13
  128.3 1.3 collective-permute-start.14
  129.6 3.9 %collective-permute-start.15 = (f16[2,64,256]{2,1,0:T(8,128)(2,1)S(1)}, f16[2,64,256]{2,1,0:T(8,128)(2,1)S(1)}, u32[]{:S(2)}, u32[]{:S(2)}) collective-permute-start(f16[2,64,256]{2,1,0:T(8,128)(2,1)S(1)} %pad_maximum_fusion.9), channel_id=1, source_target_pairs={{0,0},{4,32},{8,64},{12,96},{16,80},{20,112},{24,16},{28,48},{32,4... | collective-permute-start | bytes 196616 | tf_op jit(solution)/shard_map/ppermute | solution.py:285
  130.3 11.1 %collective-permute-start.16 = (f16[2,64,256]{2,1,0:T(8,128)(2,1)S(1)}, f16[2,64,256]{2,1,0:T(8,128)(2,1)S(1)}, u32[]{:S(2)}, u32[]{:S(2)}) collective-permute-start(f16[2,64,256]{2,1,0:T(8,128)(2,1)S(1)} %pad_maximum_fusion.9), channel_id=1, source_target_pairs={{0,32},{4,64},{8,96},{12,0},{16,112},{20,16},{24,48},{28,80},{32,3... | collective-permute-start | bytes 196616 | tf_op jit(solution)/shard_map/ppermute | solution.py:285
  141.5 1.4 collective-permute-start.17
  164.7 1.3 collective-permute-start.19
  166.0 3.9 %collective-permute-start.20 = (f16[2,64,256]{2,1,0:T(8,128)(2,1)S(1)}, f16[2,64,256]{2,1,0:T(8,128)(2,1)S(1)}, u32[]{:S(2)}, u32[]{:S(2)}) collective-permute-start(f16[2,64,256]{2,1,0:T(8,128)(2,1)S(1)} %pad_maximum_fusion.10), channel_id=1, source_target_pairs={{0,0},{4,32},{8,64},{12,96},{16,80},{20,112},{24,16},{28,48},{32,4... | collective-permute-start | bytes 196616 | tf_op jit(solution)/shard_map/ppermute | solution.py:285
  166.7 11.1 %collective-permute-start.21 = (f16[2,64,256]{2,1,0:T(8,128)(2,1)S(1)}, f16[2,64,256]{2,1,0:T(8,128)(2,1)S(1)}, u32[]{:S(2)}, u32[]{:S(2)}) collective-permute-start(f16[2,64,256]{2,1,0:T(8,128)(2,1)S(1)} %pad_maximum_fusion.10), channel_id=1, source_target_pairs={{0,32},{4,64},{8,96},{12,0},{16,112},{20,16},{24,48},{28,80},{32,3... | collective-permute-start | bytes 196616 | tf_op jit(solution)/shard_map/ppermute | solution.py:285
  177.9 1.6 collective-permute-start.22
  201.0 1.2 collective-permute-start.23
  201.1 11.0 %collective-permute-start.18 = (f32[4,64,256]{2,1,0:T(8,128)S(1)}, f32[4,64,256]{2,1,0:T(8,128)S(1)}, u32[]{:S(2)}, u32[]{:S(2)}) collective-permute-start(f32[4,64,256]{2,1,0:T(8,128)S(1)} %pad_maximum_fusion), channel_id=1, source_target_pairs={{0,0},{4,1},{8,2},{12,3},{16,4},{20,5},{24,6},{28,7},{1,8},{5,9},{... | collective-permute-start | bytes 786440 | tf_op jit(solution)/shard_map/ppermute | solution.py:300
  202.9 20.1 %all-to-all-start.5 = ((f32[64,8,128]{2,1,0:T(8,128)}), f32[64,8,128]{2,1,0:T(8,128)S(1)}, u32[]{:S(2)}, u32[]{:S(2)}) async-start(f32[64,8,128]{2,1,0:T(8,128)} %broadcast_in_dim.5), calls=%async_computation.5 | async-start | bytes 524288 | tf_op jit(solution)/shard_map/all_to_all | solution.py:268

commit v4 on v3

--- a/solution.py
+++ b/solution.py
@@ -19,7 +19,6 @@
 SUB = 64
 HALF = NX * SUB
 COLS = NK * HALF
-EXTRA = 16
 WIRE = jnp.float16
 
 
@@ -27,14 +26,23 @@
     return ((z * NK + k) * NX + x) * NY + y
 
 
-TO_INNER = [
-    (device(z, k, x, y), device(z, (k + x) % 2, y, 2 * k + x // 2))
+TO_OUTER = [
+    (device(z, (k + x) % 2, y, 2 * k + x // 2), device(z, k, x, y))
     for z in range(NZ)
     for k in range(NK)
     for x in range(NX)
     for y in range(NY)
 ]
-TO_OUTER = [(b, a) for a, b in TO_INNER]
+FIRST = [
+    [
+        (device(z, k, x, y), device((y + s) % NZ, x % 2, z, 2 * k + x // 2))
+        for z in range(NZ)
+        for k in range(NK)
+        for x in range(NX)
+        for y in range(NY)
+    ]
+    for s in range(NZ)
+]
 SWAP = [(0, 1), (1, 0)]
 SPREAD = [
     [
@@ -95,26 +103,55 @@
     )(*operands)
 
 
+def away_kernel(rates_ref, out_ref, sems):
+    copies = [
+        pltpu.make_async_copy(rates_ref.at[:, h, 1], out_ref.at[:, h], sems.at[h]) for h in range(2)
+    ]
+    for copy in copies:
+        copy.start()
+    for copy in copies:
+        copy.wait()
+
+
+def give_away(halves):
+    return pl.pallas_call(
+        away_kernel,
+        out_shape=jax.ShapeDtypeStruct((TERMS, 2, HALF, COLS), halves.dtype),
+        in_specs=[pl.BlockSpec(memory_space=pl.ANY)],
+        out_specs=pl.BlockSpec(memory_space=pl.ANY),
+        scratch_shapes=[pltpu.SemaphoreType.DMA((2,))],
+        compiler_params=pltpu.CompilerParams(vmem_limit_bytes=56 << 20),
+        name="away",
+    )(halves)
+
+
+def extras(n_fields):
+    return (1 + 3 * n_fields + 7) // 8 * 8
+
+
 def matmul_kernel(n_fields, exact, at_ref, kept_ref, got_ref, w_ref, *refs):
     own_refs, other_refs = refs[:n_fields], refs[n_fields : 2 * n_fields]
-    out_ref, x_ref, extra_ref = refs[2 * n_fields :]
+    out_ref, x_ref = refs[2 * n_fields :][:2]
     core, place, side = at_ref[0], at_ref[1], at_ref[2]
     cells = w_ref.shape[1]
 
     for ref, k in ((own_refs[-1], core), (other_refs[-1], 1 - core)):
-        for t in range(2):
-            x = (place + 2 * NZ - 2 * k - t) % NX
-            for o in range(2):
-                half = (k + o + side) % 2
-                rows = pl.ds(pl.multiple_of(half * HALF + x * SUB, SUB), SUB)
-                value = ref[t, o].astype(jnp.float32)
-                high = value.astype(jnp.bfloat16)
-                x_ref[rows, pl.ds(0, cells)] = high
-                if not exact:
-                    low = (value - high.astype(jnp.float32)).astype(jnp.bfloat16)
-                    x_ref[rows, pl.ds(cells, cells)] = low
-    extra_ref[...] = jnp.zeros_like(extra_ref)
+        for i in range(NX):
+            if exact:
+                x, half, value = (place + NZ - i) % NX, k, ref[i]
+            else:
+                t, o = divmod(i, 2)
+                x, half = (place + 2 * NZ - 2 * k - t) % NX, (k + o + side) % 2
+                value = ref[t, o]
+            rows = pl.ds(pl.multiple_of(half * HALF + x * SUB, SUB), SUB)
+            high = value.astype(jnp.bfloat16)
+            x_ref[rows, pl.ds(0, cells)] = high
+            if not exact:
+                low = (value - high.astype(jnp.float32)).astype(jnp.bfloat16)
+                x_ref[rows, pl.ds(cells, cells)] = low
     if not exact:
+        extra_ref = refs[-1]
+        extra_ref[...] = jnp.zeros_like(extra_ref)
         for m in range(n_fields):
             total = jnp.zeros((8, cells), jnp.float32)
             for a_ref, b_ref in ((own_refs[m], own_refs[-1]), (other_refs[m], other_refs[-1])):
@@ -132,7 +169,7 @@
         y = (g + 2 * core) % NY
         total = None
         for j in range(TERMS):
-            rates = kept_ref[j, 2 * g] if g < 2 else got_ref[j, g - 2]
+            rates = kept_ref[j, g, 0] if g < 2 else got_ref[j, g - 2]
             product = jnp.dot(rates, x_ref[...], preferred_element_type=jnp.float32)
             if not exact:
                 product = product[:, :cells] + product[:, cells:]
@@ -140,15 +177,19 @@
             total = product if total is None else total + product
         for x in range(NX):
             block = total[x * SUB : (x + 1) * SUB, :]
+            if exact:
+                out_ref[x, y] = block
+                continue
             power = exponent(jnp.max(jnp.abs(block), axis=0, keepdims=True))
             out_ref[x, y, pl.ds(0, SUB), :] = block * jnp.exp2(-power)
-            out_ref[x, y, pl.ds(SUB, EXTRA), :] = extra_ref[...]
+            out_ref[x, y, pl.ds(SUB, extra_ref.shape[0]), :] = extra_ref[...]
             out_ref[x, y, pl.ds(SUB, 1), :] = power
 
 
 def apply_rates(at, kept, got, weights, fields, exact):
     cells = weights.shape[1]
-    rows = SUB + EXTRA
+    more = 0 if exact else extras(len(fields))
+    rows = SUB + more
     own, other = [f[0] for f in fields], [f[1] for f in fields]
 
     def kernel(*refs):
@@ -164,10 +205,8 @@
         weights,
         *own,
         *other,
-        scratch=[
-            pltpu.VMEM((COLS, cells if exact else 2 * cells), jnp.bfloat16),
-            pltpu.VMEM((EXTRA, cells), jnp.float32),
-        ],
+        scratch=[pltpu.VMEM((COLS, cells if exact else 2 * cells), jnp.bfloat16)]
+        + ([] if exact else [pltpu.VMEM((more, cells), jnp.float32)]),
     )
     return out.reshape(NX * NY, rows, cells)
 
@@ -177,8 +216,10 @@
     cells = got_ref.shape[2]
     fresh, inner = None, [None] * j
     for b in range(NX * NY):
-        extra = got_ref[b, pl.ds(SUB, EXTRA), :]
-        value = got_ref[b, pl.ds(0, SUB), :] * jnp.exp2(extra[:1])
+        value = got_ref[b, pl.ds(0, SUB), :]
+        if j > 0:
+            extra = got_ref[b, pl.ds(SUB, extras(j)), :]
+            value = value * jnp.exp2(extra[:1])
         fresh = value if fresh is None else fresh + value
         for m in range(j):
             value = extra[3 * m + 2 : 3 * m + 3] + extra[3 * m + 3 : 3 * m + 4] * (1.0 / 256.0)
@@ -267,11 +308,10 @@
     cells = populations.shape[1]
     exchange = lambda v, axes: lax.all_to_all(v, axes, 0, 0, tiled=True)
 
-    rates = rate_terms.reshape(TERMS, 2 * NK, HALF, COLS)
-    rates = pltpu.with_memory_space_constraint(rates, pltpu.VMEM)
-    away = rate_terms.reshape(TERMS, 2, NK, HALF, COLS)[:, :, 1]
-    got_rates = lax.ppermute(away, "k", SWAP)
-    got_rates = pltpu.with_memory_space_constraint(got_rates, pltpu.VMEM)
+    halves = rate_terms.reshape(TERMS, 2, NK, HALF, COLS)
+    got = lax.ppermute(give_away(halves), "k", SWAP)
+    got = pltpu.with_memory_space_constraint(got, pltpu.VMEM)
+    kept = pltpu.with_memory_space_constraint(halves, pltpu.VMEM)
 
     onehot = (temp_bins[:, None] == jnp.arange(n_bins, dtype=jnp.int32)[None, :]).astype(
         jnp.float32
@@ -289,8 +329,10 @@
     def reduce(partial):
         return exchange(partial.astype(WIRE), ("x", "y")).astype(jnp.float32)
 
-    piece = lax.ppermute(populations.astype(jnp.bfloat16), ALL, TO_INNER)
-    met = reduce(apply_rates(at, rates, got_rates, weights, [spread(piece)], True))
+    piece = populations.astype(jnp.bfloat16)
+    own = jnp.stack([lax.ppermute(piece, ALL, pairs) for pairs in FIRST])
+    first = own, lax.ppermute(own, "k", SWAP)
+    met = reduce(apply_rates(at, kept, got, weights, [first], True))
     gram = jnp.zeros((16, cells), jnp.float32)
     q, gram = combine(0, met, gram, [])
     pieces, fields = [q], []
@@ -298,7 +340,8 @@
         fields.append(spread(q.astype(WIRE)))
         if j == KRYLOV:
             outer = lax.ppermute(jnp.stack(pieces), ALL, TO_OUTER)
-        met = reduce(apply_rates(at, rates, got_rates, weights, fields, False))
+            fields[-1], outer = lax.optimization_barrier((fields[-1], outer))
+        met = reduce(apply_rates(at, kept, got, weights, fields, False))
         if j < KRYLOV:
             q, gram = combine(j, met, gram, pieces)
             pieces.append(q)

time: 224 us -> 315 us (1.41)
  Pallas kernels: 20.8 us -> 117 us
  blocking collectives: 90.7 us -> 130 us
  waiting for transfers between devices: 62.1 us -> 33.1 us
  starting transfers between devices: 38.9 us -> 28.5 us
  local copies, waits for them, and re-layouts: 7.29 us -> 2.84 us
    pallas_call x0 -> x1, Pallas kernels: none -> 96.4 us  [give_away(): pl.pallas_call(away_kernel, out_shape=jax.ShapeDtypeStruct((TERMS, 2, HAL...]
    all_to_all x5 -> x6, blocking collectives: 90.7 us -> 130 us  [body(): exchange = lambda v, axes: lax.all_to_all(v, axes, 0, 0, tiled=True)]
    ppermute x10 -> x8, waiting for transfers between devices: 38.8 us -> 18.2 us  [spread(): lax.ppermute(both, ('z', 'k', 'x'), pairs)]
    ppermute x2 -> x6, starting transfers between devices: 0.67 us -> 15.4 us  [the longest x4 12.6 us: body(): own = jnp.stack([lax.ppermute(piece, ALL, pairs) for pairs in FIRST])]
    ppermute x10 -> x8, starting transfers between devices: 18.3 us -> 6.08 us  [spread(): lax.ppermute(both, ('z', 'k', 'x'), pairs)]
    all_to_all x1 -> x0, waiting for transfers between devices: 11 us -> none  [body(): exchange = lambda v, axes: lax.all_to_all(v, axes, 0, 0, tiled=True)]
    all_to_all x1 -> x0, starting transfers between devices: 9.1 us -> none  [body(): exchange = lambda v, axes: lax.all_to_all(v, axes, 0, 0, tiled=True)]
    ppermute x5 -> x4, starting transfers between devices: 6.12 us -> 0.34 us  [spread(): both = jnp.stack([piece, lax.ppermute(piece, 'k', SWAP)])]
  transfers between devices with their start and end apart: 25 -> 24, of which waited for: 17 -> 15; matrix products, arithmetic and copies ran while one was open for 1% -> 0% of each run, Pallas kernels for 0% -> 0%
where the time goes in v4:
time: 315 us; the launch traced here: 314 us
  blocking collectives  130 us (41%)
  Pallas kernels  117 us (37%)
  waiting for transfers between devices  33.1 us (11%)
  starting transfers between devices  28.5 us (9%)
    all_to_all x6, blocking collectives, body(): exchange = lambda v, axes: lax.all_to_all(v, axes, 0, 0, tiled=True)  130 us
    pallas_call x1, Pallas kernels, give_away(): pl.pallas_call(away_kernel, out_shape=jax.ShapeDtypeStruct((TERMS, 2, HAL...  96.4 us
    pallas_call x11, Pallas kernels, call(): pl.pallas_call(kernel, out_shape=outs, in_specs=[pl.BlockSpec(memory_spac...  20.8 us
    ppermute x8, waiting for transfers between devices, spread(): lax.ppermute(both, ('z', 'k', 'x'), pairs)  18.2 us
    ppermute x4, starting transfers between devices, body(): own = jnp.stack([lax.ppermute(piece, ALL, pairs) for pairs in FIRST])  12.6 us
  transfers between devices with their start and end apart: 24, of which 15 were waited for; matrix products, arithmetic and copies ran while one was open for 0% of the time, Pallas kernels for 0%

profile of v4, /device:TPU:0, one launch (start us, length us, event | category | flops | bytes accessed | tf_op | source)
XLA Modules:
  0.0 314.1 jit_solution(15485178442153581306)
XLA Ops:
  0.0 96.4 %away.1 = bf16[6,2,256,512]{3,2,1,0:T(8,128)(2,1)} custom-call(bf16[6,2,2,256,512]{4,3,2,1,0:T(8,128)(2,1)} %bitcast.40), custom_call_target="tpu_custom_call" | custom-call | tf_op jit(solution)/shard_map/away/pallas_call | solution.py:117
  96.5 6.1 %collective-permute-start.4 = (bf16[64,256]{1,0:T(8,128)(2,1)S(1)}, bf16[64,256]{1,0:T(8,128)(2,1)S(1)}, u32[]{:S(2)}, u32[]{:S(2)}) collective-permute-start(bf16[64,256]{1,0:T(8,128)(2,1)S(1)} %convert_element_type.87), channel_id=1, source_target_pairs={{0,96},{1,0},{2,32},{3,64},{4,112},{5,16},{6,48},{7,80},{8,97},{9,... | collective-permute-start | bytes 98312 | tf_op jit(solution)/shard_map/ppermute | solution.py:333
  102.6 4.0 %collective-permute-start.3 = (bf16[64,256]{1,0:T(8,128)(2,1)S(1)}, bf16[64,256]{1,0:T(8,128)(2,1)S(1)}, u32[]{:S(2)}, u32[]{:S(2)}) collective-permute-start(bf16[64,256]{1,0:T(8,128)(2,1)S(1)} %convert_element_type.87), channel_id=1, source_target_pairs={{0,64},{1,96},{2,0},{3,32},{4,80},{5,112},{6,16},{7,48},{8,65},{9,... | collective-permute-start | bytes 98312 | tf_op jit(solution)/shard_map/ppermute | solution.py:333
  106.6 1.9 collective-permute-start.2
  109.2 4.4 %collective-permute-done.2 = bf16[64,256]{1,0:T(8,128)(2,1)S(1)} collective-permute-done((bf16[64,256]{1,0:T(8,128)(2,1)S(1)}, bf16[64,256]{1,0:T(8,128)(2,1)S(1)}, u32[]{:S(2)}, u32[]{:S(2)}) %collective-permute-start.2) | collective-permute-done | bytes 32800 | tf_op jit(solution)/shard_map/ppermute | solution.py:333
  113.6 2.6 collective-permute-start.5
  117.3 2.8 copy-done.1
  120.1 2.4 rates.5
  122.6 25.1 %all_to_all.30 = f16[16,64,256]{2,1,0:T(8,128)(2,1)S(1)} all-to-all(f16[16,64,256]{2,1,0:T(8,128)(2,1)S(1)} %bitcast.54), channel_id=1, replica_groups=mesh['z'=4,'k'=2,'x'=4,'y'=4] {'x','y'}, dimensions={0} | all-to-all | bytes 1048576 | tf_op jit(solution)/shard_map/all_to_all | solution.py:309
  148.0 1.2 collective-permute-done.6
  149.9 4.9 %collective-permute-done.8 = f16[2,64,256]{2,1,0:T(8,128)(2,1)S(1)} collective-permute-done((f16[2,64,256]{2,1,0:T(8,128)(2,1)S(1)}, f16[2,64,256]{2,1,0:T(8,128)(2,1)S(1)}, u32[]{:S(2)}, u32[]{:S(2)}) %collective-permute-start.8) | collective-permute-done | bytes 65568 | tf_op jit(solution)/shard_map/ppermute | solution.py:325
  154.9 1.2 collective-permute-start.9
  157.1 4.1 %rates.6 = f32[4,4,72,256]{3,2,1,0:T(8,128)S(1)} custom-call(s32[3]{0:T(128)S(1)} %pad_add_fusion.refs_0_, bf16[6,2,2,256,512]{4,3,2,1,0:T(8,128)(2,1)S(1)} %bitcast.42, bf16[6,2,256,512]{3,2,1,0:T(8,128)(2,1)S(1)} %collective-permute-done.refs_2_, f32[8,256]{1,0:T(8,128)S(1)} %pad.4.refs_3_, f32[2,2,64,256]{3,2,1,0:T(8,128)S(1)} %get-tuple-element.38.refs_4_, ...), custom_call_target="tpu_custom_call" | custom-call | tf_op jit(solution)/shard_map/rates/pallas_call | solution.py:93
  161.3 20.8 %all_to_all.31 = f16[16,72,256]{2,1,0:T(8,128)(2,1)S(1)} all-to-all(f16[16,72,256]{2,1,0:T(8,128)(2,1)S(1)} %bitcast.52), channel_id=1, replica_groups=mesh['z'=4,'k'=2,'x'=4,'y'=4] {'x','y'}, dimensions={0} | all-to-all | bytes 1179648 | tf_op jit(solution)/shard_map/all_to_all | solution.py:309
  182.5 1.2 collective-permute-done.10
  183.7 1.7 collective-permute-start.12
  186.0 4.5 %collective-permute-done.12 = f16[2,64,256]{2,1,0:T(8,128)(2,1)S(1)} collective-permute-done((f16[2,64,256]{2,1,0:T(8,128)(2,1)S(1)}, f16[2,64,256]{2,1,0:T(8,128)(2,1)S(1)}, u32[]{:S(2)}, u32[]{:S(2)}) %collective-permute-start.12) | collective-permute-done | bytes 65568 | tf_op jit(solution)/shard_map/ppermute | solution.py:325
  190.6 1.3 collective-permute-start.13
  192.9 4.2 %rates.7 = f32[4,4,72,256]{3,2,1,0:T(8,128)S(1)} custom-call(s32[3]{0:T(128)S(1)} %pad_add_fusion.refs_0_, bf16[6,2,2,256,512]{4,3,2,1,0:T(8,128)(2,1)S(1)} %bitcast.43, bf16[6,2,256,512]{3,2,1,0:T(8,128)(2,1)S(1)} %collective-permute-done.refs_2_, f32[8,256]{1,0:T(8,128)S(1)} %pad.4.refs_3_, f32[2,2,64,256]{3,2,1,0:T(8,128)S(1)} %get-tuple-element.38.refs_4_, ...), custom_call_target="tpu_custom_call" | custom-call | tf_op jit(solution)/shard_map/rates/pallas_call | solution.py:93
  197.3 20.2 %all_to_all.32 = f16[16,72,256]{2,1,0:T(8,128)(2,1)S(1)} all-to-all(f16[16,72,256]{2,1,0:T(8,128)(2,1)S(1)} %bitcast.53), channel_id=1, replica_groups=mesh['z'=4,'k'=2,'x'=4,'y'=4] {'x','y'}, dimensions={0} | all-to-all | bytes 1179648 | tf_op jit(solution)/shard_map/all_to_all | solution.py:309
  217.9 1.2 collective-permute-done.14
  219.1 1.6 collective-permute-start.16
  221.3 4.2 %collective-permute-done.16 = f16[2,64,256]{2,1,0:T(8,128)(2,1)S(1)} collective-permute-done((f16[2,64,256]{2,1,0:T(8,128)(2,1)S(1)}, f16[2,64,256]{2,1,0:T(8,128)(2,1)S(1)}, u32[]{:S(2)}, u32[]{:S(2)}) %collective-permute-start.16) | collective-permute-done | bytes 65568 | tf_op jit(solution)/shard_map/ppermute | solution.py:325
  225.5 2.6 collective-permute-start.17
  229.1 4.2 %rates.8 = f32[4,4,80,256]{3,2,1,0:T(8,128)S(1)} custom-call(s32[3]{0:T(128)S(1)} %pad_add_fusion.refs_0_, bf16[6,2,2,256,512]{4,3,2,1,0:T(8,128)(2,1)S(1)} %bitcast.44, bf16[6,2,256,512]{3,2,1,0:T(8,128)(2,1)S(1)} %collective-permute-done.refs_2_, f32[8,256]{1,0:T(8,128)S(1)} %pad.4.refs_3_, f32[2,2,64,256]{3,2,1,0:T(8,128)S(1)} %get-tuple-element.38.refs_4_, ...), custom_call_target="tpu_custom_call" | custom-call | tf_op jit(solution)/shard_map/rates/pallas_call | solution.py:93
  233.5 22.1 %all_to_all.33 = f16[16,80,256]{2,1,0:T(8,128)(2,1)S(1)} all-to-all(f16[16,80,256]{2,1,0:T(8,128)(2,1)S(1)} %bitcast.50), channel_id=1, replica_groups=mesh['z'=4,'k'=2,'x'=4,'y'=4] {'x','y'}, dimensions={0} | all-to-all | bytes 1310720 | tf_op jit(solution)/shard_map/all_to_all | solution.py:309
  256.0 1.2 collective-permute-done.18
  258.6 4.7 %collective-permute-done.20 = f16[2,64,256]{2,1,0:T(8,128)(2,1)S(1)} collective-permute-done((f16[2,64,256]{2,1,0:T(8,128)(2,1)S(1)}, f16[2,64,256]{2,1,0:T(8,128)(2,1)S(1)}, u32[]{:S(2)}, u32[]{:S(2)}) %collective-permute-start.20) | collective-permute-done | bytes 65568 | tf_op jit(solution)/shard_map/ppermute | solution.py:325
  265.3 4.3 %rates.9 = f32[4,4,80,256]{3,2,1,0:T(8,128)S(1)} custom-call(s32[3]{0:T(128)S(1)} %pad_add_fusion.refs_0_, bf16[6,2,2,256,512]{4,3,2,1,0:T(8,128)(2,1)S(1)} %bitcast.45, bf16[6,2,256,512]{3,2,1,0:T(8,128)(2,1)S(1)} %collective-permute-done.refs_2_, f32[8,256]{1,0:T(8,128)S(1)} %pad.4.refs_3_, f32[2,2,64,256]{3,2,1,0:T(8,128)S(1)} %get-tuple-element.38.refs_4_, ...), custom_call_target="tpu_custom_call" | custom-call | tf_op jit(solution)/shard_map/rates/pallas_call | solution.py:93
  269.7 24.9 %all_to_all.34 = f16[16,80,256]{2,1,0:T(8,128)(2,1)S(1)} all-to-all(f16[16,80,256]{2,1,0:T(8,128)(2,1)S(1)} %bitcast.51), channel_id=1, replica_groups=mesh['z'=4,'k'=2,'x'=4,'y'=4] {'x','y'}, dimensions={0} | all-to-all | bytes 1310720 | tf_op jit(solution)/shard_map/all_to_all | solution.py:309
  295.1 1.2 collective-permute-done.23
  296.3 17.0 %all_to_all.35.dots_ref = f32[64,8,128]{2,1,0:T(8,128)S(1)} all-to-all(f32[64,8,128]{2,1,0:T(8,128)S(1)} %broadcast_in_dim.5), channel_id=1, replica_groups=mesh['z'=4,'k'=2,'x'=4,'y'=4] {'z','x','y'}, dimensions={0} | all-to-all | bytes 524288 | tf_op jit(solution)/shard_map/all_to_all | solution.py:309
  (83 shorter events, 13.5 us)
Async XLA Ops:
  0.0 116.3 %copy-start = (f32[64,6]{0,1:T(8,128)S(1)}, f32[64,6]{0,1:T(8,128)}, u32[]{:S(2)}) copy-start(f32[64,6]{0,1:T(8,128)} %param.7) | copy-start | bytes 4612
  0.0 96.5 %copy-start.3 = (f32[64,256]{1,0:T(8,128)S(1)}, f32[64,256]{1,0:T(8,128)}, u32[]{:S(2)}) copy-start(f32[64,256]{1,0:T(8,128)} %p_ref.1) | copy-start | bytes 196612
  0.0 116.3 %copy-start.4 = (s32[256]{0:T(256)S(1)}, s32[256]{0:T(256)}, u32[]{:S(2)}) copy-start(s32[256]{0:T(256)} %param.6) | copy-start | bytes 3076
  96.4 20.9 %collective-permute-start = (bf16[6,2,256,512]{3,2,1,0:T(8,128)(2,1)}, bf16[6,2,256,512]{3,2,1,0:T(8,128)(2,1)S(1)}, u32[]{:S(2)}, u32[]{:S(2)}) collective-permute-start(bf16[6,2,256,512]{3,2,1,0:T(8,128)(2,1)} %away.1), channel_id=1, source_target_pairs={{0,16},{16,0},{1,17},{17,1},{2,18},{18,2},{3,19},{19,3},{4,20},{20... | collective-permute-start | bytes 9437192 | tf_op jit(solution)/shard_map/ppermute | solution.py:312
  96.5 12.7 %collective-permute-start.4 = (bf16[64,256]{1,0:T(8,128)(2,1)S(1)}, bf16[64,256]{1,0:T(8,128)(2,1)S(1)}, u32[]{:S(2)}, u32[]{:S(2)}) collective-permute-start(bf16[64,256]{1,0:T(8,128)(2,1)S(1)} %convert_element_type.87), channel_id=1, source_target_pairs={{0,96},{1,0},{2,32},{3,64},{4,112},{5,16},{6,48},{7,80},{8,97},{9,... | collective-permute-start | bytes 98312 | tf_op jit(solution)/shard_map/ppermute | solution.py:333
  102.6 6.6 %collective-permute-start.3 = (bf16[64,256]{1,0:T(8,128)(2,1)S(1)}, bf16[64,256]{1,0:T(8,128)(2,1)S(1)}, u32[]{:S(2)}, u32[]{:S(2)}) collective-permute-start(bf16[64,256]{1,0:T(8,128)(2,1)S(1)} %convert_element_type.87), channel_id=1, source_target_pairs={{0,64},{1,96},{2,0},{3,32},{4,80},{5,112},{6,16},{7,48},{8,65},{9,... | collective-permute-start | bytes 98312 | tf_op jit(solution)/shard_map/ppermute | solution.py:333
  106.6 7.0 %collective-permute-start.2 = (bf16[64,256]{1,0:T(8,128)(2,1)S(1)}, bf16[64,256]{1,0:T(8,128)(2,1)S(1)}, u32[]{:S(2)}, u32[]{:S(2)}) collective-permute-start(bf16[64,256]{1,0:T(8,128)(2,1)S(1)} %convert_element_type.87), channel_id=1, source_target_pairs={{0,32},{1,64},{2,96},{3,0},{4,48},{5,80},{6,112},{7,16},{8,33},{9,... | collective-permute-start | bytes 98312 | tf_op jit(solution)/shard_map/ppermute | solution.py:333
  108.5 5.1 %collective-permute-start.1 = (bf16[64,256]{1,0:T(8,128)(2,1)S(1)}, bf16[64,256]{1,0:T(8,128)(2,1)S(1)}, u32[]{:S(2)}, u32[]{:S(2)}) collective-permute-start(bf16[64,256]{1,0:T(8,128)(2,1)S(1)} %convert_element_type.87), channel_id=1, source_target_pairs={{0,0},{1,32},{2,64},{3,96},{4,16},{5,48},{6,80},{7,112},{8,1},{9,3... | collective-permute-start | bytes 98312 | tf_op jit(solution)/shard_map/ppermute | solution.py:333
  113.6 3.6 %collective-permute-start.5 = (bf16[4,64,256]{2,1,0:T(8,128)(2,1)S(1)}, bf16[4,64,256]{2,1,0:T(8,128)(2,1)S(1)}, u32[]{:S(2)}, u32[]{:S(2)}) collective-permute-start(bf16[4,64,256]{2,1,0:T(8,128)(2,1)S(1)} %pad_maximum_fusion.1.refs_4_), channel_id=1, source_target_pairs={{0,16},{16,0},{1,17},{17,1},{2,18},{18,2},{3,19},{19,3},{4,20},{20... | collective-permute-start | bytes 393224 | tf_op jit(solution)/shard_map/ppermute | solution.py:334
  117.3 2.8 copy-start.1
  122.5 34.6 %copy-start.2 = (bf16[6,1024,512]{2,1,0:T(8,128)(2,1)S(1)}, bf16[6,1024,512]{2,1,0:T(8,128)(2,1)}, u32[]{:S(2)}) copy-start(bf16[6,1024,512]{2,1,0:T(8,128)(2,1)} %param.4) | copy-start | bytes 18874372
  147.9 1.3 collective-permute-start.6
  149.2 5.7 %collective-permute-start.8 = (f16[2,64,256]{2,1,0:T(8,128)(2,1)S(1)}, f16[2,64,256]{2,1,0:T(8,128)(2,1)S(1)}, u32[]{:S(2)}, u32[]{:S(2)}) collective-permute-start(f16[2,64,256]{2,1,0:T(8,128)(2,1)S(1)} %pad_maximum_fusion.6), channel_id=1, source_target_pairs={{0,32},{4,64},{8,96},{12,0},{16,112},{20,16},{24,48},{28,80},{32,3... | collective-permute-start | bytes 196616 | tf_op jit(solution)/shard_map/ppermute | solution.py:325
  149.2 5.6 %collective-permute-start.7 = (f16[2,64,256]{2,1,0:T(8,128)(2,1)S(1)}, f16[2,64,256]{2,1,0:T(8,128)(2,1)S(1)}, u32[]{:S(2)}, u32[]{:S(2)}) collective-permute-start(f16[2,64,256]{2,1,0:T(8,128)(2,1)S(1)} %pad_maximum_fusion.6), channel_id=1, source_target_pairs={{0,0},{4,32},{8,64},{12,96},{16,80},{20,112},{24,16},{28,48},{32,4... | collective-permute-start | bytes 196616 | tf_op jit(solution)/shard_map/ppermute | solution.py:325
  154.9 2.2 collective-permute-start.9
  182.3 1.3 collective-permute-start.10
  183.7 6.9 %collective-permute-start.12 = (f16[2,64,256]{2,1,0:T(8,128)(2,1)S(1)}, f16[2,64,256]{2,1,0:T(8,128)(2,1)S(1)}, u32[]{:S(2)}, u32[]{:S(2)}) collective-permute-start(f16[2,64,256]{2,1,0:T(8,128)(2,1)S(1)} %pad_maximum_fusion.7), channel_id=1, source_target_pairs={{0,32},{4,64},{8,96},{12,0},{16,112},{20,16},{24,48},{28,80},{32,3... | collective-permute-start | bytes 196616 | tf_op jit(solution)/shard_map/ppermute | solution.py:325
  185.4 5.1 %collective-permute-start.11 = (f16[2,64,256]{2,1,0:T(8,128)(2,1)S(1)}, f16[2,64,256]{2,1,0:T(8,128)(2,1)S(1)}, u32[]{:S(2)}, u32[]{:S(2)}) collective-permute-start(f16[2,64,256]{2,1,0:T(8,128)(2,1)S(1)} %pad_maximum_fusion.7), channel_id=1, source_target_pairs={{0,0},{4,32},{8,64},{12,96},{16,80},{20,112},{24,16},{28,48},{32,4... | collective-permute-start | bytes 196616 | tf_op jit(solution)/shard_map/ppermute | solution.py:325
  190.6 2.3 collective-permute-start.13
  217.7 1.3 collective-permute-start.14
  219.1 6.4 %collective-permute-start.16 = (f16[2,64,256]{2,1,0:T(8,128)(2,1)S(1)}, f16[2,64,256]{2,1,0:T(8,128)(2,1)S(1)}, u32[]{:S(2)}, u32[]{:S(2)}) collective-permute-start(f16[2,64,256]{2,1,0:T(8,128)(2,1)S(1)} %pad_maximum_fusion.8), channel_id=1, source_target_pairs={{0,32},{4,64},{8,96},{12,0},{16,112},{20,16},{24,48},{28,80},{32,3... | collective-permute-start | bytes 196616 | tf_op jit(solution)/shard_map/ppermute | solution.py:325
  220.6 4.8 %collective-permute-start.15 = (f16[2,64,256]{2,1,0:T(8,128)(2,1)S(1)}, f16[2,64,256]{2,1,0:T(8,128)(2,1)S(1)}, u32[]{:S(2)}, u32[]{:S(2)}) collective-permute-start(f16[2,64,256]{2,1,0:T(8,128)(2,1)S(1)} %pad_maximum_fusion.8), channel_id=1, source_target_pairs={{0,0},{4,32},{8,64},{12,96},{16,80},{20,112},{24,16},{28,48},{32,4... | collective-permute-start | bytes 196616 | tf_op jit(solution)/shard_map/ppermute | solution.py:325
  225.5 3.6 %collective-permute-start.17 = (f16[2,2,64,256]{3,2,1,0:T(8,128)(2,1)S(1)}, f16[2,2,64,256]{3,2,1,0:T(8,128)(2,1)S(1)}, u32[]{:S(2)}, u32[]{:S(2)}) collective-permute-start(f16[2,2,64,256]{3,2,1,0:T(8,128)(2,1)S(1)} %get-tuple-element.33), channel_id=1, source_target_pairs={{0,16},{16,0},{1,17},{17,1},{2,18},{18,2},{3,19},{19,3},{4,20},{20... | collective-permute-start | bytes 393224 | tf_op jit(solution)/shard_map/ppermute | solution.py:326
  255.9 1.3 collective-permute-start.18
  257.2 6.1 %collective-permute-start.20 = (f16[2,64,256]{2,1,0:T(8,128)(2,1)S(1)}, f16[2,64,256]{2,1,0:T(8,128)(2,1)S(1)}, u32[]{:S(2)}, u32[]{:S(2)}) collective-permute-start(f16[2,64,256]{2,1,0:T(8,128)(2,1)S(1)} %pad_maximum_fusion.9), channel_id=1, source_target_pairs={{0,32},{4,64},{8,96},{12,0},{16,112},{20,16},{24,48},{28,80},{32,3... | collective-permute-start | bytes 196616 | tf_op jit(solution)/shard_map/ppermute | solution.py:325
  257.2 6.1 %collective-permute-start.19 = (f16[2,64,256]{2,1,0:T(8,128)(2,1)S(1)}, f16[2,64,256]{2,1,0:T(8,128)(2,1)S(1)}, u32[]{:S(2)}, u32[]{:S(2)}) collective-permute-start(f16[2,64,256]{2,1,0:T(8,128)(2,1)S(1)} %pad_maximum_fusion.9), channel_id=1, source_target_pairs={{0,0},{4,32},{8,64},{12,96},{16,80},{20,112},{24,16},{28,48},{32,4... | collective-permute-start | bytes 196616 | tf_op jit(solution)/shard_map/ppermute | solution.py:325
  257.9 7.3 %collective-permute-start.22 = (f32[4,64,256]{2,1,0:T(8,128)S(1)}, f32[4,64,256]{2,1,0:T(8,128)S(1)}, u32[]{:S(2)}, u32[]{:S(2)}) collective-permute-start(f32[4,64,256]{2,1,0:T(8,128)S(1)} %pad_maximum_fusion), channel_id=1, source_target_pairs={{0,0},{4,1},{8,2},{12,3},{16,4},{20,5},{24,6},{28,7},{1,8},{5,9},{... | collective-permute-start | bytes 786440 | tf_op jit(solution)/shard_map/ppermute | solution.py:342
  263.3 1.9 collective-permute-start.21
  295.0 1.2 collective-permute-start.23

commit v5 on v4

--- a/solution.py
+++ b/solution.py
@@ -7,6 +7,7 @@
 from jax.experimental.pallas import tpu as pltpu
 from jax.sharding import Mesh, PartitionSpec as P
 
+
 KRYLOV = 4
 TAYLOR = 8
 TERMS = 6
@@ -26,23 +27,14 @@
     return ((z * NK + k) * NX + x) * NY + y
 
 
-TO_OUTER = [
-    (device(z, (k + x) % 2, y, 2 * k + x // 2), device(z, k, x, y))
+TO_INNER = [
+    (device(z, k, x, y), device(z, (k + x) % 2, y, 2 * k + x // 2))
     for z in range(NZ)
     for k in range(NK)
     for x in range(NX)
     for y in range(NY)
 ]
-FIRST = [
-    [
-        (device(z, k, x, y), device((y + s) % NZ, x % 2, z, 2 * k + x // 2))
-        for z in range(NZ)
-        for k in range(NK)
-        for x in range(NX)
-        for y in range(NY)
-    ]
-    for s in range(NZ)
-]
+TO_OUTER = [(b, a) for a, b in TO_INNER]
 SWAP = [(0, 1), (1, 0)]
 SPREAD = [
     [
@@ -88,38 +80,34 @@
     return combos, hess
 
 
-def call(kernel, name, outs, *operands, scratch=()):
+def call(kernel, outs, *operands, scratch=(), far=(), limit=16):
     vmem = pl.BlockSpec(memory_space=pltpu.VMEM)
+    specs = [
+        pl.BlockSpec(memory_space=pltpu.SMEM) if a.dtype == jnp.int32 else vmem for a in operands
+    ]
+    for i in far:
+        specs[i] = pl.BlockSpec(memory_space=pl.ANY)
     return pl.pallas_call(
         kernel,
         out_shape=outs,
-        in_specs=[
-            pl.BlockSpec(memory_space=pltpu.SMEM) if a.dtype == jnp.int32 else vmem for a in operands
-        ],
+        in_specs=specs,
         out_specs=jax.tree.map(lambda _: vmem, outs),
         scratch_shapes=scratch,
-        compiler_params=pltpu.CompilerParams(vmem_limit_bytes=16 << 20),
-        name=name,
+        compiler_params=pltpu.CompilerParams(vmem_limit_bytes=limit << 20),
     )(*operands)
 
 
-def away_kernel(rates_ref, out_ref, sems):
-    copies = [
-        pltpu.make_async_copy(rates_ref.at[:, h, 1], out_ref.at[:, h], sems.at[h]) for h in range(2)
-    ]
-    for copy in copies:
-        copy.start()
-    for copy in copies:
-        copy.wait()
+def away_kernel(rates_ref, out_ref):
+    out_ref[0] = rates_ref[0, :, 0]
 
 
 def give_away(halves):
     return pl.pallas_call(
         away_kernel,
         out_shape=jax.ShapeDtypeStruct((TERMS, 2, HALF, COLS), halves.dtype),
-        in_specs=[pl.BlockSpec(memory_space=pl.ANY)],
-        out_specs=pl.BlockSpec(memory_space=pl.ANY),
-        scratch_shapes=[pltpu.SemaphoreType.DMA((2,))],
+        grid=(TERMS,),
+        in_specs=[pl.BlockSpec((1, 2, 1, HALF, COLS), lambda g: (g, 0, 1, 0, 0))],
+        out_specs=pl.BlockSpec((1, 2, HALF, COLS), lambda g: (g, 0, 0, 0)),
         compiler_params=pltpu.CompilerParams(vmem_limit_bytes=56 << 20),
         name="away",
     )(halves)
@@ -134,15 +122,20 @@
     out_ref, x_ref = refs[2 * n_fields :][:2]
     core, place, side = at_ref[0], at_ref[1], at_ref[2]
     cells = w_ref.shape[1]
+    copies = []
+    if exact:
+        held_ref, sems = refs[-2:]
+        for h in range(2):
+            copies.append(
+                pltpu.make_async_copy(kept_ref.at[:, h, 0], held_ref.at[:, h], sems.at[h])
+            )
+            copies[h].start()
 
     for ref, k in ((own_refs[-1], core), (other_refs[-1], 1 - core)):
         for i in range(NX):
-            if exact:
-                x, half, value = (place + NZ - i) % NX, k, ref[i]
-            else:
-                t, o = divmod(i, 2)
-                x, half = (place + 2 * NZ - 2 * k - t) % NX, (k + o + side) % 2
-                value = ref[t, o]
+            t, o = divmod(i, 2)
+            x, half = (place + 2 * NZ - 2 * k - t) % NX, (k + o + side) % 2
+            value = ref[t, o]
             rows = pl.ds(pl.multiple_of(half * HALF + x * SUB, SUB), SUB)
             high = value.astype(jnp.bfloat16)
             x_ref[rows, pl.ds(0, cells)] = high
@@ -165,11 +158,16 @@
             extra_ref[pl.ds(3 * m + 2, 1), :] = high
             extra_ref[pl.ds(3 * m + 3, 1), :] = (total - high) * 256.0
 
-    for g in range(NY):
+    for g in (2, 3, 0, 1):
         y = (g + 2 * core) % NY
         total = None
+        if exact and g < 2:
+            copies[g].wait()
         for j in range(TERMS):
-            rates = kept_ref[j, g, 0] if g < 2 else got_ref[j, g - 2]
+            if g >= 2:
+                rates = got_ref[j, g - 2]
+            else:
+                rates = held_ref[j, g] if exact else kept_ref[j, g, 0]
             product = jnp.dot(rates, x_ref[...], preferred_element_type=jnp.float32)
             if not exact:
                 product = product[:, :cells] + product[:, cells:]
@@ -191,13 +189,17 @@
     more = 0 if exact else extras(len(fields))
     rows = SUB + more
     own, other = [f[0] for f in fields], [f[1] for f in fields]
+    if exact:
+        held = pltpu.VMEM((TERMS, 2, HALF, COLS), kept.dtype)
+        last = [held, pltpu.SemaphoreType.DMA((2,))]
+    else:
+        last = [pltpu.VMEM((more, cells), jnp.float32)]
 
     def kernel(*refs):
         matmul_kernel(len(fields), exact, *refs)
 
     out = call(
         kernel,
-        "rates",
         jax.ShapeDtypeStruct((NX, NY, rows, cells), jnp.float32),
         at,
         kept,
@@ -205,15 +207,15 @@
         weights,
         *own,
         *other,
-        scratch=[pltpu.VMEM((COLS, cells if exact else 2 * cells), jnp.bfloat16)]
-        + ([] if exact else [pltpu.VMEM((more, cells), jnp.float32)]),
+        scratch=[pltpu.VMEM((COLS, cells if exact else 2 * cells), jnp.bfloat16)] + last,
+        far=(1,) if exact else (),
+        limit=46 if exact else 16,
     )
     return out.reshape(NX * NY, rows, cells)
 
 
 def combine_kernel(j, got_ref, gram_ref, *refs):
     q_refs, outs = refs[:j], refs[j:]
-    cells = got_ref.shape[2]
     fresh, inner = None, [None] * j
     for b in range(NX * NY):
         value = got_ref[b, pl.ds(0, SUB), :]
@@ -263,7 +265,7 @@
     else:
         outs = (jax.ShapeDtypeStruct((2 * KRYLOV, cells // 2), jnp.float32),)
     outs = (*outs, jax.ShapeDtypeStruct(gram.shape, jnp.float32))
-    return call(kernel, f"combine{j}", outs, got, gram, *fields)
+    return call(kernel, outs, got, gram, *fields)
 
 
 def finish_kernel(p_ref, q_ref, gram_ref, dots_ref, out_ref):
@@ -309,7 +311,8 @@
     exchange = lambda v, axes: lax.all_to_all(v, axes, 0, 0, tiled=True)
 
     halves = rate_terms.reshape(TERMS, 2, NK, HALF, COLS)
-    got = lax.ppermute(give_away(halves), "k", SWAP)
+    away = give_away(halves)
+    got = lax.ppermute(away, "k", SWAP)
     got = pltpu.with_memory_space_constraint(got, pltpu.VMEM)
     kept = pltpu.with_memory_space_constraint(halves, pltpu.VMEM)
 
@@ -321,18 +324,18 @@
     at = jnp.stack([core, lax.axis_index("z"), lax.axis_index("y") // 2]).astype(jnp.int32)
 
     def spread(piece):
+        wide = jnp.float32 if piece.dtype == WIRE else piece.dtype
         both = jnp.stack([piece, lax.ppermute(piece, "k", SWAP)])
         own = jnp.stack([lax.ppermute(both, ("z", "k", "x"), pairs) for pairs in SPREAD])
         other = lax.ppermute(own, "k", SWAP)
-        return own.astype(jnp.float32), other.astype(jnp.float32)
+        return own.astype(wide), other.astype(wide)
 
     def reduce(partial):
         return exchange(partial.astype(WIRE), ("x", "y")).astype(jnp.float32)
 
-    piece = populations.astype(jnp.bfloat16)
-    own = jnp.stack([lax.ppermute(piece, ALL, pairs) for pairs in FIRST])
-    first = own, lax.ppermute(own, "k", SWAP)
-    met = reduce(apply_rates(at, kept, got, weights, [first], True))
+    piece = lax.ppermute(populations.astype(jnp.bfloat16), ALL, TO_INNER)
+    first = spread(piece)
+    met = reduce(apply_rates(at, halves, got, weights, [first], True))
     gram = jnp.zeros((16, cells), jnp.float32)
     q, gram = combine(0, met, gram, [])
     pieces, fields = [q], []
@@ -340,8 +343,8 @@
         fields.append(spread(q.astype(WIRE)))
         if j == KRYLOV:
             outer = lax.ppermute(jnp.stack(pieces), ALL, TO_OUTER)
-            fields[-1], outer = lax.optimization_barrier((fields[-1], outer))
-        met = reduce(apply_rates(at, kept, got, weights, fields, False))
+        partial = apply_rates(at, kept, got, weights, fields, False)
+        met = reduce(partial)
         if j < KRYLOV:
             q, gram = combine(j, met, gram, pieces)
             pieces.append(q)
@@ -350,12 +353,10 @@
     dots = dots + lax.ppermute(dots, "k", SWAP)
     dots = exchange(jnp.broadcast_to(dots[None], (NZ * NX * NY, *dots.shape)), ("z", "x", "y"))
     out = jax.ShapeDtypeStruct(populations.shape, jnp.float32)
-    return call(finish_kernel, "finish", out, populations, outer, gram, dots)
+    return call(finish_kernel, out, populations, outer, gram, dots)
 
 
 def solution(mesh):
     named = Mesh(mesh.devices.reshape(NZ, NK, NX, NY), ALL)
     placed = (P(None, ("z", "k"), ("x", "y")), P(ALL, None), P(), P())
-    return jax.shard_map(
-        body, mesh=named, in_specs=placed, out_specs=P(ALL, None), check_vma=False
-    )
+    return jax.shard_map(body, mesh=named, in_specs=placed, out_specs=P(ALL, None), check_vma=False)

time: 315 us -> 219 us (0.70)
  Pallas kernels: 117 us -> 27.1 us
  blocking collectives: 130 us -> 87.2 us
  waiting for transfers between devices: 33.1 us -> 61.7 us
  starting transfers between devices: 28.5 us -> 39.8 us
    pallas_call x1, Pallas kernels: 96.4 us -> 5.3 us  [give_away(): pl.pallas_call(away_kernel, out_shape=jax.ShapeDtypeStruct((TERMS, 2, HAL...]
    all_to_all x6 -> x5, blocking collectives: 130 us -> 87.2 us  [body(): exchange = lambda v, axes: lax.all_to_all(v, axes, 0, 0, tiled=True)]
    ppermute x8 -> x10, waiting for transfers between devices: 18.2 us -> 38.4 us  [spread(): lax.ppermute(both, ('z', 'k', 'x'), pairs)]
    ppermute x8 -> x10, starting transfers between devices: 6.08 us -> 22.8 us  [spread(): lax.ppermute(both, ('z', 'k', 'x'), pairs)]
    ppermute x6 -> x2, starting transfers between devices: 15.4 us -> 0.67 us  [the longest x1 0.66 us: body(): piece = lax.ppermute(populations.astype(jnp.bfloat16), ALL, TO_INNER)]
    all_to_all x0 -> x1, waiting for transfers between devices: none -> 11 us  [body(): exchange = lambda v, axes: lax.all_to_all(v, axes, 0, 0, tiled=True)]
    all_to_all x0 -> x1, starting transfers between devices: none -> 8.65 us  [body(): exchange = lambda v, axes: lax.all_to_all(v, axes, 0, 0, tiled=True)]
    ppermute x4 -> x5, starting transfers between devices: 0.34 us -> 6.12 us  [spread(): both = jnp.stack([piece, lax.ppermute(piece, 'k', SWAP)])]
  transfers between devices with their start and end apart: 24 -> 25, of which waited for: 15 -> 17; matrix products, arithmetic and copies ran while one was open for 0% -> 0% of each run, Pallas kernels for 0% -> 0%
where the time goes in v5:
time: 219 us
  blocking collectives  87.2 us (40%)
  waiting for transfers between devices  61.7 us (28%)
  starting transfers between devices  39.8 us (18%)
  Pallas kernels  27.1 us (12%)
    all_to_all x5, blocking collectives, body(): exchange = lambda v, axes: lax.all_to_all(v, axes, 0, 0, tiled=True)  87.2 us
    ppermute x10, waiting for transfers between devices, spread(): lax.ppermute(both, ('z', 'k', 'x'), pairs)  38.4 us
    ppermute x10, starting transfers between devices, spread(): lax.ppermute(both, ('z', 'k', 'x'), pairs)  22.8 us
    pallas_call x11, Pallas kernels, call(): pl.pallas_call(kernel, out_shape=outs, in_specs=specs, out_specs=jax.tree...  21.8 us
    all_to_all x1, waiting for transfers between devices, body(): exchange = lambda v, axes: lax.all_to_all(v, axes, 0, 0, tiled=True)  11 us
    all_to_all x1, starting transfers between devices, body(): exchange = lambda v, axes: lax.all_to_all(v, axes, 0, 0, tiled=True)  8.65 us
    ppermute x5, waiting for transfers between devices, spread(): other = lax.ppermute(own, 'k', SWAP)  6.3 us
    ppermute x5, starting transfers between devices, spread(): both = jnp.stack([piece, lax.ppermute(piece, 'k', SWAP)])  6.12 us
  transfers between devices with their start and end apart: 25, of which 17 were waited for; matrix products, arithmetic and copies ran while one was open for 0% of the time, Pallas kernels for 0%

profile of v5, /device:TPU:0, one launch (start us, length us, event | category | flops | bytes accessed | tf_op | source)
XLA Modules:
  0.0 218.8 jit_solution(8661891343715452830)
XLA Ops:
  0.0 5.3 %away.1 = bf16[6,2,256,512]{3,2,1,0:T(8,128)(2,1)} custom-call(bf16[6,2,2,256,512]{4,3,2,1,0:T(8,128)(2,1)} %bitcast.40), custom_call_target="tpu_custom_call" | custom-call | tf_op jit(solution)/shard_map/away/pallas_call | solution.py:105
  6.0 5.8 %collective-permute-start.2 = (bf16[64,256]{1,0:T(8,128)(2,1)S(1)}, bf16[64,256]{1,0:T(8,128)(2,1)S(1)}, u32[]{:S(2)}, u32[]{:S(2)}) collective-permute-start(bf16[64,256]{1,0:T(8,128)(2,1)S(1)} %collective-permute-done.1), channel_id=1, source_target_pairs={{0,16},{16,0},{1,17},{17,1},{2,18},{18,2},{3,19},{19,3},{4,20},{20... | collective-permute-start | bytes 98312 | tf_op jit(solution)/shard_map/ppermute | solution.py:328
  13.3 5.0 %collective-permute-start.4 = (bf16[2,64,256]{2,1,0:T(8,128)(2,1)S(1)}, bf16[2,64,256]{2,1,0:T(8,128)(2,1)S(1)}, u32[]{:S(2)}, u32[]{:S(2)}) collective-permute-start(bf16[2,64,256]{2,1,0:T(8,128)(2,1)S(1)} %pad_maximum_fusion.6), channel_id=1, source_target_pairs={{0,32},{4,64},{8,96},{12,0},{16,112},{20,16},{24,48},{28,80},{32,3... | collective-permute-start | bytes 196616 | tf_op jit(solution)/shard_map/ppermute | solution.py:329
  18.3 8.3 %collective-permute-done.4 = bf16[2,64,256]{2,1,0:T(8,128)(2,1)S(1)} collective-permute-done((bf16[2,64,256]{2,1,0:T(8,128)(2,1)S(1)}, bf16[2,64,256]{2,1,0:T(8,128)(2,1)S(1)}, u32[]{:S(2)}, u32[]{:S(2)}) %collective-permute-start.4) | collective-permute-done | bytes 65568 | tf_op jit(solution)/shard_map/ppermute | solution.py:329
  28.1 3.4 %shard_map.46 = f32[4,4,64,256]{3,2,1,0:T(8,128)S(1)} custom-call(s32[3]{0:T(128)S(1)} %pad_add_fusion.refs_0_, bf16[6,2,2,256,512]{4,3,2,1,0:T(8,128)(2,1)} %bitcast.41, bf16[6,2,256,512]{3,2,1,0:T(8,128)(2,1)S(1)} %collective-permute-done.refs_2_, f32[8,256]{1,0:T(8,128)S(1)} %pad.4.refs_3_, bf16[2,2,64,256]{3,2,1,0:T(8,128)(2,1)S(1)} %pad_maximum_fusion.1.refs_4_, ...), custom_call_target="tpu_custom_call" | custom-call | tf_op jit(solution)/shard_map/pallas_call | solution.py:90
  31.6 20.0 %all_to_all.30 = f16[16,64,256]{2,1,0:T(8,128)(2,1)S(1)} all-to-all(f16[16,64,256]{2,1,0:T(8,128)(2,1)S(1)} %bitcast.56), channel_id=1, replica_groups=mesh['z'=4,'k'=2,'x'=4,'y'=4] {'x','y'}, dimensions={0} | all-to-all | bytes 1048576 | tf_op jit(solution)/shard_map/all_to_all | solution.py:311
  51.9 1.2 collective-permute-done.6
  53.8 4.6 %collective-permute-start.8 = (f16[2,64,256]{2,1,0:T(8,128)(2,1)S(1)}, f16[2,64,256]{2,1,0:T(8,128)(2,1)S(1)}, u32[]{:S(2)}, u32[]{:S(2)}) collective-permute-start(f16[2,64,256]{2,1,0:T(8,128)(2,1)S(1)} %pad_maximum_fusion.7), channel_id=1, source_target_pairs={{0,32},{4,64},{8,96},{12,0},{16,112},{20,16},{24,48},{28,80},{32,3... | collective-permute-start | bytes 196616 | tf_op jit(solution)/shard_map/ppermute | solution.py:329
  58.4 6.2 %collective-permute-done.8 = f16[2,64,256]{2,1,0:T(8,128)(2,1)S(1)} collective-permute-done((f16[2,64,256]{2,1,0:T(8,128)(2,1)S(1)}, f16[2,64,256]{2,1,0:T(8,128)(2,1)S(1)}, u32[]{:S(2)}, u32[]{:S(2)}) %collective-permute-start.8) | collective-permute-done | bytes 65568 | tf_op jit(solution)/shard_map/ppermute | solution.py:329
  64.7 1.3 collective-permute-done.9
  66.1 4.1 %shard_map.48 = f32[4,4,72,256]{3,2,1,0:T(8,128)S(1)} custom-call(s32[3]{0:T(128)S(1)} %pad_add_fusion.refs_0_, bf16[6,2,2,256,512]{4,3,2,1,0:T(8,128)(2,1)S(1)} %bitcast.44, bf16[6,2,256,512]{3,2,1,0:T(8,128)(2,1)S(1)} %collective-permute-done.refs_2_, f32[8,256]{1,0:T(8,128)S(1)} %pad.4.refs_3_, f32[2,2,64,256]{3,2,1,0:T(8,128)S(1)} %get-tuple-element.32.refs_4_, ...), custom_call_target="tpu_custom_call" | custom-call | tf_op jit(solution)/shard_map/pallas_call | solution.py:90
  70.4 17.4 %all_to_all.31 = f16[16,72,256]{2,1,0:T(8,128)(2,1)S(1)} all-to-all(f16[16,72,256]{2,1,0:T(8,128)(2,1)S(1)} %bitcast.54), channel_id=1, replica_groups=mesh['z'=4,'k'=2,'x'=4,'y'=4] {'x','y'}, dimensions={0} | all-to-all | bytes 1179648 | tf_op jit(solution)/shard_map/all_to_all | solution.py:311
  88.1 1.2 collective-permute-done.10
  90.0 3.3 %collective-permute-start.12 = (f16[2,64,256]{2,1,0:T(8,128)(2,1)S(1)}, f16[2,64,256]{2,1,0:T(8,128)(2,1)S(1)}, u32[]{:S(2)}, u32[]{:S(2)}) collective-permute-start(f16[2,64,256]{2,1,0:T(8,128)(2,1)S(1)} %pad_maximum_fusion.8), channel_id=1, source_target_pairs={{0,32},{4,64},{8,96},{12,0},{16,112},{20,16},{24,48},{28,80},{32,3... | collective-permute-start | bytes 196616 | tf_op jit(solution)/shard_map/ppermute | solution.py:329
  93.3 8.0 %collective-permute-done.12 = f16[2,64,256]{2,1,0:T(8,128)(2,1)S(1)} collective-permute-done((f16[2,64,256]{2,1,0:T(8,128)(2,1)S(1)}, f16[2,64,256]{2,1,0:T(8,128)(2,1)S(1)}, u32[]{:S(2)}, u32[]{:S(2)}) %collective-permute-start.12) | collective-permute-done | bytes 65568 | tf_op jit(solution)/shard_map/ppermute | solution.py:329
  101.7 1.3 collective-permute-done.13
  103.0 4.3 %shard_map.50 = f32[4,4,72,256]{3,2,1,0:T(8,128)S(1)} custom-call(s32[3]{0:T(128)S(1)} %pad_add_fusion.refs_0_, bf16[6,2,2,256,512]{4,3,2,1,0:T(8,128)(2,1)S(1)} %bitcast.45, bf16[6,2,256,512]{3,2,1,0:T(8,128)(2,1)S(1)} %collective-permute-done.refs_2_, f32[8,256]{1,0:T(8,128)S(1)} %pad.4.refs_3_, f32[2,2,64,256]{3,2,1,0:T(8,128)S(1)} %get-tuple-element.32.refs_4_, ...), custom_call_target="tpu_custom_call" | custom-call | tf_op jit(solution)/shard_map/pallas_call | solution.py:90
  107.4 16.1 %all_to_all.32 = f16[16,72,256]{2,1,0:T(8,128)(2,1)S(1)} all-to-all(f16[16,72,256]{2,1,0:T(8,128)(2,1)S(1)} %bitcast.55), channel_id=1, replica_groups=mesh['z'=4,'k'=2,'x'=4,'y'=4] {'x','y'}, dimensions={0} | all-to-all | bytes 1179648 | tf_op jit(solution)/shard_map/all_to_all | solution.py:311
  123.9 1.2 collective-permute-done.14
  125.7 3.3 %collective-permute-start.16 = (f16[2,64,256]{2,1,0:T(8,128)(2,1)S(1)}, f16[2,64,256]{2,1,0:T(8,128)(2,1)S(1)}, u32[]{:S(2)}, u32[]{:S(2)}) collective-permute-start(f16[2,64,256]{2,1,0:T(8,128)(2,1)S(1)} %pad_maximum_fusion.9), channel_id=1, source_target_pairs={{0,32},{4,64},{8,96},{12,0},{16,112},{20,16},{24,48},{28,80},{32,3... | collective-permute-start | bytes 196616 | tf_op jit(solution)/shard_map/ppermute | solution.py:329
  129.0 8.0 %collective-permute-done.16 = f16[2,64,256]{2,1,0:T(8,128)(2,1)S(1)} collective-permute-done((f16[2,64,256]{2,1,0:T(8,128)(2,1)S(1)}, f16[2,64,256]{2,1,0:T(8,128)(2,1)S(1)}, u32[]{:S(2)}, u32[]{:S(2)}) %collective-permute-start.16) | collective-permute-done | bytes 65568 | tf_op jit(solution)/shard_map/ppermute | solution.py:329
  137.1 1.3 collective-permute-done.17
  138.5 4.2 %shard_map.52 = f32[4,4,80,256]{3,2,1,0:T(8,128)S(1)} custom-call(s32[3]{0:T(128)S(1)} %pad_add_fusion.refs_0_, bf16[6,2,2,256,512]{4,3,2,1,0:T(8,128)(2,1)S(1)} %bitcast.46, bf16[6,2,256,512]{3,2,1,0:T(8,128)(2,1)S(1)} %collective-permute-done.refs_2_, f32[8,256]{1,0:T(8,128)S(1)} %pad.4.refs_3_, f32[2,2,64,256]{3,2,1,0:T(8,128)S(1)} %get-tuple-element.32.refs_4_, ...), custom_call_target="tpu_custom_call" | custom-call | tf_op jit(solution)/shard_map/pallas_call | solution.py:90
  142.8 16.7 %all_to_all.33 = f16[16,80,256]{2,1,0:T(8,128)(2,1)S(1)} all-to-all(f16[16,80,256]{2,1,0:T(8,128)(2,1)S(1)} %bitcast.52), channel_id=1, replica_groups=mesh['z'=4,'k'=2,'x'=4,'y'=4] {'x','y'}, dimensions={0} | all-to-all | bytes 1310720 | tf_op jit(solution)/shard_map/all_to_all | solution.py:311
  160.0 1.2 collective-permute-done.19
  161.8 3.3 %collective-permute-start.21 = (f16[2,64,256]{2,1,0:T(8,128)(2,1)S(1)}, f16[2,64,256]{2,1,0:T(8,128)(2,1)S(1)}, u32[]{:S(2)}, u32[]{:S(2)}) collective-permute-start(f16[2,64,256]{2,1,0:T(8,128)(2,1)S(1)} %pad_maximum_fusion.10), channel_id=1, source_target_pairs={{0,32},{4,64},{8,96},{12,0},{16,112},{20,16},{24,48},{28,80},{32,3... | collective-permute-start | bytes 196616 | tf_op jit(solution)/shard_map/ppermute | solution.py:329
  165.1 7.8 %collective-permute-done.21 = f16[2,64,256]{2,1,0:T(8,128)(2,1)S(1)} collective-permute-done((f16[2,64,256]{2,1,0:T(8,128)(2,1)S(1)}, f16[2,64,256]{2,1,0:T(8,128)(2,1)S(1)}, u32[]{:S(2)}, u32[]{:S(2)}) %collective-permute-start.21) | collective-permute-done | bytes 65568 | tf_op jit(solution)/shard_map/ppermute | solution.py:329
  173.3 1.3 collective-permute-done.22
  174.7 4.3 %shard_map.54 = f32[4,4,80,256]{3,2,1,0:T(8,128)S(1)} custom-call(s32[3]{0:T(128)S(1)} %pad_add_fusion.refs_0_, bf16[6,2,2,256,512]{4,3,2,1,0:T(8,128)(2,1)S(1)} %bitcast.47, bf16[6,2,256,512]{3,2,1,0:T(8,128)(2,1)S(1)} %collective-permute-done.refs_2_, f32[8,256]{1,0:T(8,128)S(1)} %pad.4.refs_3_, f32[2,2,64,256]{3,2,1,0:T(8,128)S(1)} %get-tuple-element.32.refs_4_, ...), custom_call_target="tpu_custom_call" | custom-call | tf_op jit(solution)/shard_map/pallas_call | solution.py:90
  179.0 17.0 %all_to_all.34 = f16[16,80,256]{2,1,0:T(8,128)(2,1)S(1)} all-to-all(f16[16,80,256]{2,1,0:T(8,128)(2,1)S(1)} %bitcast.53), channel_id=1, replica_groups=mesh['z'=4,'k'=2,'x'=4,'y'=4] {'x','y'}, dimensions={0} | all-to-all | bytes 1310720 | tf_op jit(solution)/shard_map/all_to_all | solution.py:311
  198.4 8.6 %all-to-all-start.5 = ((f32[64,8,128]{2,1,0:T(8,128)}), f32[64,8,128]{2,1,0:T(8,128)S(1)}, u32[]{:S(2)}, u32[]{:S(2)}) async-start(f32[64,8,128]{2,1,0:T(8,128)} %broadcast_in_dim.5), calls=%async_computation.5 | async-start | bytes 524288 | tf_op jit(solution)/shard_map/all_to_all | solution.py:311
  207.0 11.0 %all-to-all-done.5.dots_ref = f32[64,8,128]{2,1,0:T(8,128)S(1)} async-done(((f32[64,8,128]{2,1,0:T(8,128)}), f32[64,8,128]{2,1,0:T(8,128)S(1)}, u32[]{:S(2)}, u32[]{:S(2)}) %all-to-all-start.5) | async-done | bytes 262176 | tf_op jit(solution)/shard_map/all_to_all | solution.py:311
  (86 shorter events, 12.3 us)
Async XLA Ops:
  0.0 26.7 %copy-start = (f32[64,6]{0,1:T(8,128)S(1)}, f32[64,6]{0,1:T(8,128)}, u32[]{:S(2)}) copy-start(f32[64,6]{0,1:T(8,128)} %param.7) | copy-start | bytes 4612
  0.0 5.3 %copy-start.1 = (f32[64,256]{1,0:T(8,128)S(1)}, f32[64,256]{1,0:T(8,128)}, u32[]{:S(2)}) copy-start(f32[64,256]{1,0:T(8,128)} %p_ref.1) | copy-start | bytes 196612
  0.0 26.8 %copy-start.2 = (s32[256]{0:T(256)S(1)}, s32[256]{0:T(256)}, u32[]{:S(2)}) copy-start(s32[256]{0:T(256)} %param.6) | copy-start | bytes 3076
  5.3 22.8 %collective-permute-start = (bf16[6,2,256,512]{3,2,1,0:T(8,128)(2,1)}, bf16[6,2,256,512]{3,2,1,0:T(8,128)(2,1)S(1)}, u32[]{:S(2)}, u32[]{:S(2)}) collective-permute-start(bf16[6,2,256,512]{3,2,1,0:T(8,128)(2,1)} %away.1), channel_id=1, source_target_pairs={{0,16},{16,0},{1,17},{17,1},{2,18},{18,2},{3,19},{19,3},{4,20},{20... | collective-permute-start | bytes 9437192 | tf_op jit(solution)/shard_map/ppermute | solution.py:315
  5.3 0.7 collective-permute-start.1
  6.0 6.6 %collective-permute-start.2 = (bf16[64,256]{1,0:T(8,128)(2,1)S(1)}, bf16[64,256]{1,0:T(8,128)(2,1)S(1)}, u32[]{:S(2)}, u32[]{:S(2)}) collective-permute-start(bf16[64,256]{1,0:T(8,128)(2,1)S(1)} %collective-permute-done.1), channel_id=1, source_target_pairs={{0,16},{16,0},{1,17},{17,1},{2,18},{18,2},{3,19},{19,3},{4,20},{20... | collective-permute-start | bytes 98312 | tf_op jit(solution)/shard_map/ppermute | solution.py:328
  12.7 5.7 %collective-permute-start.3 = (bf16[2,64,256]{2,1,0:T(8,128)(2,1)S(1)}, bf16[2,64,256]{2,1,0:T(8,128)(2,1)S(1)}, u32[]{:S(2)}, u32[]{:S(2)}) collective-permute-start(bf16[2,64,256]{2,1,0:T(8,128)(2,1)S(1)} %pad_maximum_fusion.6), channel_id=1, source_target_pairs={{0,0},{4,32},{8,64},{12,96},{16,80},{20,112},{24,16},{28,48},{32,4... | collective-permute-start | bytes 196616 | tf_op jit(solution)/shard_map/ppermute | solution.py:329
  13.3 13.3 %collective-permute-start.4 = (bf16[2,64,256]{2,1,0:T(8,128)(2,1)S(1)}, bf16[2,64,256]{2,1,0:T(8,128)(2,1)S(1)}, u32[]{:S(2)}, u32[]{:S(2)}) collective-permute-start(bf16[2,64,256]{2,1,0:T(8,128)(2,1)S(1)} %pad_maximum_fusion.6), channel_id=1, source_target_pairs={{0,32},{4,64},{8,96},{12,0},{16,112},{20,16},{24,48},{28,80},{32,3... | collective-permute-start | bytes 196616 | tf_op jit(solution)/shard_map/ppermute | solution.py:329
  26.7 1.4 collective-permute-start.5
  27.0 39.1 %slice-start = ((s8[6291456]{0:T(1024)(128)(4,1)}), s8[4194304]{0:T(1024)(128)(4,1)S(1)}, s32[]{:S(2)}) async-start(s8[6291456]{0:T(1024)(128)(4,1)} %bitcast.42), calls=%async_computation.6 | async-start | bytes 8388608
  27.1 39.0 %slice-start.1 = ((s8[6291456]{0:T(1024)(128)(4,1)}), s8[2097152]{0:T(1024)(128)(4,1)S(1)}, s32[]{:S(2)}) async-start(s8[6291456]{0:T(1024)(128)(4,1)} %bitcast.42), calls=%async_computation.7 | async-start | bytes 4194304
  51.8 1.3 collective-permute-start.6
  53.1 5.3 %collective-permute-start.7 = (f16[2,64,256]{2,1,0:T(8,128)(2,1)S(1)}, f16[2,64,256]{2,1,0:T(8,128)(2,1)S(1)}, u32[]{:S(2)}, u32[]{:S(2)}) collective-permute-start(f16[2,64,256]{2,1,0:T(8,128)(2,1)S(1)} %pad_maximum_fusion.7), channel_id=1, source_target_pairs={{0,0},{4,32},{8,64},{12,96},{16,80},{20,112},{24,16},{28,48},{32,4... | collective-permute-start | bytes 196616 | tf_op jit(solution)/shard_map/ppermute | solution.py:329
  53.8 10.8 %collective-permute-start.8 = (f16[2,64,256]{2,1,0:T(8,128)(2,1)S(1)}, f16[2,64,256]{2,1,0:T(8,128)(2,1)S(1)}, u32[]{:S(2)}, u32[]{:S(2)}) collective-permute-start(f16[2,64,256]{2,1,0:T(8,128)(2,1)S(1)} %pad_maximum_fusion.7), channel_id=1, source_target_pairs={{0,32},{4,64},{8,96},{12,0},{16,112},{20,16},{24,48},{28,80},{32,3... | collective-permute-start | bytes 196616 | tf_op jit(solution)/shard_map/ppermute | solution.py:329
  64.6 1.4 collective-permute-start.9
  88.0 1.3 collective-permute-start.10
  89.4 4.0 %collective-permute-start.11 = (f16[2,64,256]{2,1,0:T(8,128)(2,1)S(1)}, f16[2,64,256]{2,1,0:T(8,128)(2,1)S(1)}, u32[]{:S(2)}, u32[]{:S(2)}) collective-permute-start(f16[2,64,256]{2,1,0:T(8,128)(2,1)S(1)} %pad_maximum_fusion.8), channel_id=1, source_target_pairs={{0,0},{4,32},{8,64},{12,96},{16,80},{20,112},{24,16},{28,48},{32,4... | collective-permute-start | bytes 196616 | tf_op jit(solution)/shard_map/ppermute | solution.py:329
  90.0 11.3 %collective-permute-start.12 = (f16[2,64,256]{2,1,0:T(8,128)(2,1)S(1)}, f16[2,64,256]{2,1,0:T(8,128)(2,1)S(1)}, u32[]{:S(2)}, u32[]{:S(2)}) collective-permute-start(f16[2,64,256]{2,1,0:T(8,128)(2,1)S(1)} %pad_maximum_fusion.8), channel_id=1, source_target_pairs={{0,32},{4,64},{8,96},{12,0},{16,112},{20,16},{24,48},{28,80},{32,3... | collective-permute-start | bytes 196616 | tf_op jit(solution)/shard_map/ppermute | solution.py:329
  101.4 1.6 collective-permute-start.13
  123.7 1.3 collective-permute-start.14
  125.1 4.0 %collective-permute-start.15 = (f16[2,64,256]{2,1,0:T(8,128)(2,1)S(1)}, f16[2,64,256]{2,1,0:T(8,128)(2,1)S(1)}, u32[]{:S(2)}, u32[]{:S(2)}) collective-permute-start(f16[2,64,256]{2,1,0:T(8,128)(2,1)S(1)} %pad_maximum_fusion.9), channel_id=1, source_target_pairs={{0,0},{4,32},{8,64},{12,96},{16,80},{20,112},{24,16},{28,48},{32,4... | collective-permute-start | bytes 196616 | tf_op jit(solution)/shard_map/ppermute | solution.py:329
  125.7 11.3 %collective-permute-start.16 = (f16[2,64,256]{2,1,0:T(8,128)(2,1)S(1)}, f16[2,64,256]{2,1,0:T(8,128)(2,1)S(1)}, u32[]{:S(2)}, u32[]{:S(2)}) collective-permute-start(f16[2,64,256]{2,1,0:T(8,128)(2,1)S(1)} %pad_maximum_fusion.9), channel_id=1, source_target_pairs={{0,32},{4,64},{8,96},{12,0},{16,112},{20,16},{24,48},{28,80},{32,3... | collective-permute-start | bytes 196616 | tf_op jit(solution)/shard_map/ppermute | solution.py:329
  137.0 1.4 collective-permute-start.17
  159.9 1.3 collective-permute-start.19
  161.2 3.9 %collective-permute-start.20 = (f16[2,64,256]{2,1,0:T(8,128)(2,1)S(1)}, f16[2,64,256]{2,1,0:T(8,128)(2,1)S(1)}, u32[]{:S(2)}, u32[]{:S(2)}) collective-permute-start(f16[2,64,256]{2,1,0:T(8,128)(2,1)S(1)} %pad_maximum_fusion.10), channel_id=1, source_target_pairs={{0,0},{4,32},{8,64},{12,96},{16,80},{20,112},{24,16},{28,48},{32,4... | collective-permute-start | bytes 196616 | tf_op jit(solution)/shard_map/ppermute | solution.py:329
  161.8 11.1 %collective-permute-start.21 = (f16[2,64,256]{2,1,0:T(8,128)(2,1)S(1)}, f16[2,64,256]{2,1,0:T(8,128)(2,1)S(1)}, u32[]{:S(2)}, u32[]{:S(2)}) collective-permute-start(f16[2,64,256]{2,1,0:T(8,128)(2,1)S(1)} %pad_maximum_fusion.10), channel_id=1, source_target_pairs={{0,32},{4,64},{8,96},{12,0},{16,112},{20,16},{24,48},{28,80},{32,3... | collective-permute-start | bytes 196616 | tf_op jit(solution)/shard_map/ppermute | solution.py:329
  173.0 1.6 collective-permute-start.22
  196.4 1.2 collective-permute-start.23
  196.5 10.5 %collective-permute-start.18 = (f32[4,64,256]{2,1,0:T(8,128)S(1)}, f32[4,64,256]{2,1,0:T(8,128)S(1)}, u32[]{:S(2)}, u32[]{:S(2)}) collective-permute-start(f32[4,64,256]{2,1,0:T(8,128)S(1)} %pad_maximum_fusion), channel_id=1, source_target_pairs={{0,0},{4,1},{8,2},{12,3},{16,4},{20,5},{24,6},{28,7},{1,8},{5,9},{... | collective-permute-start | bytes 786440 | tf_op jit(solution)/shard_map/ppermute | solution.py:345
  198.4 19.7 %all-to-all-start.5 = ((f32[64,8,128]{2,1,0:T(8,128)}), f32[64,8,128]{2,1,0:T(8,128)S(1)}, u32[]{:S(2)}, u32[]{:S(2)}) async-start(f32[64,8,128]{2,1,0:T(8,128)} %broadcast_in_dim.5), calls=%async_computation.5 | async-start | bytes 524288 | tf_op jit(solution)/shard_map/all_to_all | solution.py:311

commit v6 on v5

--- a/solution.py
+++ b/solution.py
@@ -95,22 +95,6 @@
         scratch_shapes=scratch,
         compiler_params=pltpu.CompilerParams(vmem_limit_bytes=limit << 20),
     )(*operands)
-
-
-def away_kernel(rates_ref, out_ref):
-    out_ref[0] = rates_ref[0, :, 0]
-
-
-def give_away(halves):
-    return pl.pallas_call(
-        away_kernel,
-        out_shape=jax.ShapeDtypeStruct((TERMS, 2, HALF, COLS), halves.dtype),
-        grid=(TERMS,),
-        in_specs=[pl.BlockSpec((1, 2, 1, HALF, COLS), lambda g: (g, 0, 1, 0, 0))],
-        out_specs=pl.BlockSpec((1, 2, HALF, COLS), lambda g: (g, 0, 0, 0)),
-        compiler_params=pltpu.CompilerParams(vmem_limit_bytes=56 << 20),
-        name="away",
-    )(halves)
 
 
 def extras(n_fields):
@@ -268,6 +252,10 @@
     return call(kernel, outs, got, gram, *fields)
 
 
+def pair_kernel(mine_ref, other_ref, out_ref):
+    out_ref[...] = jnp.broadcast_to((mine_ref[...] + other_ref[...])[None], out_ref.shape)
+
+
 def finish_kernel(p_ref, q_ref, gram_ref, dots_ref, out_ref):
     gram = {}
     for m in range(1, KRYLOV + 1):
@@ -311,9 +299,7 @@
     exchange = lambda v, axes: lax.all_to_all(v, axes, 0, 0, tiled=True)
 
     halves = rate_terms.reshape(TERMS, 2, NK, HALF, COLS)
-    away = give_away(halves)
-    got = lax.ppermute(away, "k", SWAP)
-    got = pltpu.with_memory_space_constraint(got, pltpu.VMEM)
+    away = halves[:, :, 1]
     kept = pltpu.with_memory_space_constraint(halves, pltpu.VMEM)
 
     onehot = (temp_bins[:, None] == jnp.arange(n_bins, dtype=jnp.int32)[None, :]).astype(
@@ -323,9 +309,8 @@
     weights = jnp.pad(weights.T, ((0, 2), (0, 0)))
     at = jnp.stack([core, lax.axis_index("z"), lax.axis_index("y") // 2]).astype(jnp.int32)
 
-    def spread(piece):
-        wide = jnp.float32 if piece.dtype == WIRE else piece.dtype
-        both = jnp.stack([piece, lax.ppermute(piece, "k", SWAP)])
+    def spread(both):
+        wide = jnp.float32 if both.dtype == WIRE else both.dtype
         own = jnp.stack([lax.ppermute(both, ("z", "k", "x"), pairs) for pairs in SPREAD])
         other = lax.ppermute(own, "k", SWAP)
         return own.astype(wide), other.astype(wide)
@@ -334,15 +319,20 @@
         return exchange(partial.astype(WIRE), ("x", "y")).astype(jnp.float32)
 
     piece = lax.ppermute(populations.astype(jnp.bfloat16), ALL, TO_INNER)
-    first = spread(piece)
+    both = jnp.stack([piece, lax.ppermute(piece, "k", SWAP)])
+    away, both = lax.optimization_barrier((away, both))
+    got = lax.ppermute(away, "k", SWAP)
+    got = pltpu.with_memory_space_constraint(got, pltpu.VMEM)
+    first = spread(both)
     met = reduce(apply_rates(at, halves, got, weights, [first], True))
     gram = jnp.zeros((16, cells), jnp.float32)
     q, gram = combine(0, met, gram, [])
     pieces, fields = [q], []
     for j in range(1, KRYLOV + 1):
-        fields.append(spread(q.astype(WIRE)))
+        piece = q.astype(WIRE)
+        fields.append(spread(jnp.stack([piece, lax.ppermute(piece, "k", SWAP)])))
         if j == KRYLOV:
-            outer = lax.ppermute(jnp.stack(pieces), ALL, TO_OUTER)
+            outer = lax.ppermute(jnp.stack(pieces).astype(WIRE), ALL, TO_OUTER)
         partial = apply_rates(at, kept, got, weights, fields, False)
         met = reduce(partial)
         if j < KRYLOV:
@@ -350,8 +340,14 @@
             pieces.append(q)
         else:
             dots, gram = combine(j, met, gram, pieces)
-    dots = dots + lax.ppermute(dots, "k", SWAP)
-    dots = exchange(jnp.broadcast_to(dots[None], (NZ * NX * NY, *dots.shape)), ("z", "x", "y"))
+    dots = call(
+        pair_kernel,
+        jax.ShapeDtypeStruct((NZ * NX * NY, *dots.shape), dots.dtype),
+        dots,
+        lax.ppermute(dots, "k", SWAP),
+    )
+    dots = exchange(dots, ("z", "x", "y"))
+    outer = outer.astype(jnp.float32)
     out = jax.ShapeDtypeStruct(populations.shape, jnp.float32)
     return call(finish_kernel, out, populations, outer, gram, dots)
 

time: 219 us -> 215 us (0.982)
  Pallas kernels: 27.1 us -> 22.5 us
  waiting for transfers between devices: 61.7 us -> 58.6 us
  local copies, waits for them, and re-layouts: 0.81 us -> 3.83 us
  starting transfers between devices: 39.8 us -> 37 us
    pallas_call x1 -> x0, Pallas kernels: 5.3 us -> none  [give_away(): pl.pallas_call(away_kernel, out_shape=jax.ShapeDtypeStruct((TERMS, 2, HAL...]
    squeeze x0 -> x1, local copies, waits for them, and re-layouts: none -> 3.74 us  [body(): away = halves[:, :, 1]]
    all_to_all x1, starting transfers between devices: 8.65 us -> 5.31 us  [body(): exchange = lambda v, axes: lax.all_to_all(v, axes, 0, 0, tiled=True)]
    ppermute x10, waiting for transfers between devices: 38.4 us -> 36 us  [spread(): lax.ppermute(both, ('z', 'k', 'x'), pairs)]
    pallas_call x11 -> x12, Pallas kernels: 21.8 us -> 22.5 us  [call(): pl.pallas_call(kernel, out_shape=outs, in_specs=specs, out_specs=jax.tree...]
  transfers between devices with their start and end apart: 25 -> 25, of which waited for: 17 -> 16; matrix products, arithmetic and copies ran while one was open for 0% -> 2% of each run, Pallas kernels for 0% -> 0%
where the time goes in v6:
time: 215 us; the launch traced here: 214 us
  blocking collectives  89.3 us (42%)
  waiting for transfers between devices  58.6 us (27%)
  starting transfers between devices  37 us (17%)
  Pallas kernels  22.5 us (10%)
  local copies, waits for them, and re-layouts  3.83 us (2%)
  other arithmetic  2.45 us (1%)
    all_to_all x5, blocking collectives, body(): exchange = lambda v, axes: lax.all_to_all(v, axes, 0, 0, tiled=True)  89.3 us
    ppermute x10, waiting for transfers between devices, spread(): lax.ppermute(both, ('z', 'k', 'x'), pairs)  36 us
    ppermute x10, starting transfers between devices, spread(): lax.ppermute(both, ('z', 'k', 'x'), pairs)  23.9 us
    pallas_call x12, Pallas kernels, call(): pl.pallas_call(kernel, out_shape=outs, in_specs=specs, out_specs=jax.tree...  22.5 us
    all_to_all x1, waiting for transfers between devices, body(): exchange = lambda v, axes: lax.all_to_all(v, axes, 0, 0, tiled=True)  10.5 us
    ppermute x5, waiting for transfers between devices, spread(): other = lax.ppermute(own, 'k', SWAP)  6.3 us
    all_to_all x1, starting transfers between devices, body(): exchange = lambda v, axes: lax.all_to_all(v, axes, 0, 0, tiled=True)  5.31 us
    ppermute x1, starting transfers between devices, body(): both = jnp.stack([piece, lax.ppermute(piece, 'k', SWAP)])  5.1 us
  transfers between devices with their start and end apart: 25, of which 16 were waited for; matrix products, arithmetic and copies ran while one was open for 2% of the time, Pallas kernels for 0%

profile of v6, /device:TPU:0, one launch (start us, length us, event | category | flops | bytes accessed | tf_op | source)
XLA Modules:
  0.0 214.4 jit_solution(16163978597401053255)
XLA Ops:
  1.5 5.1 %collective-permute-start.1 = (bf16[64,256]{1,0:T(8,128)(2,1)S(1)}, bf16[64,256]{1,0:T(8,128)(2,1)S(1)}, u32[]{:S(2)}, u32[]{:S(2)}) collective-permute-start(bf16[64,256]{1,0:T(8,128)(2,1)S(1)} %collective-permute-done), channel_id=1, source_target_pairs={{0,16},{16,0},{1,17},{17,1},{2,18},{18,2},{3,19},{19,3},{4,20},{20... | collective-permute-start | bytes 98312 | tf_op jit(solution)/shard_map/ppermute | solution.py:322
  6.6 3.7 %slice_bitcast_fusion = bf16[6,2,256,512]{3,2,1,0:T(8,128)(2,1)} fusion(bf16[6,2,2,256,512]{4,3,2,1,0:T(8,128)(2,1)} %bitcast.40), kind=kLoop, calls=%fused_computation | loop fusion | bytes 6291456 | tf_op jit(solution)/shard_map/squeeze | solution.py:302
  11.2 6.1 %collective-permute-start.4 = (bf16[2,64,256]{2,1,0:T(8,128)(2,1)S(1)}, bf16[2,64,256]{2,1,0:T(8,128)(2,1)S(1)}, u32[]{:S(2)}, u32[]{:S(2)}) collective-permute-start(bf16[2,64,256]{2,1,0:T(8,128)(2,1)S(1)} %pad_maximum_fusion.6), channel_id=1, source_target_pairs={{0,32},{4,64},{8,96},{12,0},{16,112},{20,16},{24,48},{28,80},{32,3... | collective-permute-start | bytes 196616 | tf_op jit(solution)/shard_map/ppermute | solution.py:314
  17.3 7.3 %collective-permute-done.4 = bf16[2,64,256]{2,1,0:T(8,128)(2,1)S(1)} collective-permute-done((bf16[2,64,256]{2,1,0:T(8,128)(2,1)S(1)}, bf16[2,64,256]{2,1,0:T(8,128)(2,1)S(1)}, u32[]{:S(2)}, u32[]{:S(2)}) %collective-permute-start.4) | collective-permute-done | bytes 65568 | tf_op jit(solution)/shard_map/ppermute | solution.py:314
  26.1 3.4 %shard_map.46 = f32[4,4,64,256]{3,2,1,0:T(8,128)S(1)} custom-call(s32[3]{0:T(128)S(1)} %pad_add_fusion.refs_0_, bf16[6,2,2,256,512]{4,3,2,1,0:T(8,128)(2,1)} %bitcast.41, bf16[6,2,256,512]{3,2,1,0:T(8,128)(2,1)S(1)} %collective-permute-done.2.refs_2_, f32[8,256]{1,0:T(8,128)S(1)} %pad.4.refs_3_, bf16[2,2,64,256]{3,2,1,0:T(8,128)(2,1)S(1)} %pad_maximum_fusion.refs_4_, ...), custom_call_target="tpu_custom_call" | custom-call | tf_op jit(solution)/shard_map/pallas_call | solution.py:90
  29.6 20.6 %all_to_all.30 = f16[16,64,256]{2,1,0:T(8,128)(2,1)S(1)} all-to-all(f16[16,64,256]{2,1,0:T(8,128)(2,1)S(1)} %bitcast.52), channel_id=1, replica_groups=mesh['z'=4,'k'=2,'x'=4,'y'=4] {'x','y'}, dimensions={0} | all-to-all | bytes 1048576 | tf_op jit(solution)/shard_map/all_to_all | solution.py:299
  50.5 1.2 collective-permute-done.6
  52.4 4.6 %collective-permute-start.8 = (f16[2,64,256]{2,1,0:T(8,128)(2,1)S(1)}, f16[2,64,256]{2,1,0:T(8,128)(2,1)S(1)}, u32[]{:S(2)}, u32[]{:S(2)}) collective-permute-start(f16[2,64,256]{2,1,0:T(8,128)(2,1)S(1)} %pad_maximum_fusion.7), channel_id=1, source_target_pairs={{0,32},{4,64},{8,96},{12,0},{16,112},{20,16},{24,48},{28,80},{32,3... | collective-permute-start | bytes 196616 | tf_op jit(solution)/shard_map/ppermute | solution.py:314
  57.0 4.8 %collective-permute-done.8 = f16[2,64,256]{2,1,0:T(8,128)(2,1)S(1)} collective-permute-done((f16[2,64,256]{2,1,0:T(8,128)(2,1)S(1)}, f16[2,64,256]{2,1,0:T(8,128)(2,1)S(1)}, u32[]{:S(2)}, u32[]{:S(2)}) %collective-permute-start.8) | collective-permute-done | bytes 65568 | tf_op jit(solution)/shard_map/ppermute | solution.py:314
  61.9 1.3 collective-permute-done.9
  63.3 4.1 %shard_map.48 = f32[4,4,72,256]{3,2,1,0:T(8,128)S(1)} custom-call(s32[3]{0:T(128)S(1)} %pad_add_fusion.refs_0_, bf16[6,2,2,256,512]{4,3,2,1,0:T(8,128)(2,1)S(1)} %bitcast.44, bf16[6,2,256,512]{3,2,1,0:T(8,128)(2,1)S(1)} %collective-permute-done.2.refs_2_, f32[8,256]{1,0:T(8,128)S(1)} %pad.4.refs_3_, f32[2,2,64,256]{3,2,1,0:T(8,128)S(1)} %get-tuple-element.36.refs_4_, ...), custom_call_target="tpu_custom_call" | custom-call | tf_op jit(solution)/shard_map/pallas_call | solution.py:90
  67.6 18.8 %all_to_all.31 = f16[16,72,256]{2,1,0:T(8,128)(2,1)S(1)} all-to-all(f16[16,72,256]{2,1,0:T(8,128)(2,1)S(1)} %bitcast.50), channel_id=1, replica_groups=mesh['z'=4,'k'=2,'x'=4,'y'=4] {'x','y'}, dimensions={0} | all-to-all | bytes 1179648 | tf_op jit(solution)/shard_map/all_to_all | solution.py:299
  86.8 1.2 collective-permute-done.10
  88.6 3.3 %collective-permute-start.12 = (f16[2,64,256]{2,1,0:T(8,128)(2,1)S(1)}, f16[2,64,256]{2,1,0:T(8,128)(2,1)S(1)}, u32[]{:S(2)}, u32[]{:S(2)}) collective-permute-start(f16[2,64,256]{2,1,0:T(8,128)(2,1)S(1)} %pad_maximum_fusion.8), channel_id=1, source_target_pairs={{0,32},{4,64},{8,96},{12,0},{16,112},{20,16},{24,48},{28,80},{32,3... | collective-permute-start | bytes 196616 | tf_op jit(solution)/shard_map/ppermute | solution.py:314
  91.9 8.0 %collective-permute-done.12 = f16[2,64,256]{2,1,0:T(8,128)(2,1)S(1)} collective-permute-done((f16[2,64,256]{2,1,0:T(8,128)(2,1)S(1)}, f16[2,64,256]{2,1,0:T(8,128)(2,1)S(1)}, u32[]{:S(2)}, u32[]{:S(2)}) %collective-permute-start.12) | collective-permute-done | bytes 65568 | tf_op jit(solution)/shard_map/ppermute | solution.py:314
  100.3 1.3 collective-permute-done.13
  101.6 4.3 %shard_map.50 = f32[4,4,72,256]{3,2,1,0:T(8,128)S(1)} custom-call(s32[3]{0:T(128)S(1)} %pad_add_fusion.refs_0_, bf16[6,2,2,256,512]{4,3,2,1,0:T(8,128)(2,1)S(1)} %bitcast.45, bf16[6,2,256,512]{3,2,1,0:T(8,128)(2,1)S(1)} %collective-permute-done.2.refs_2_, f32[8,256]{1,0:T(8,128)S(1)} %pad.4.refs_3_, f32[2,2,64,256]{3,2,1,0:T(8,128)S(1)} %get-tuple-element.36.refs_4_, ...), custom_call_target="tpu_custom_call" | custom-call | tf_op jit(solution)/shard_map/pallas_call | solution.py:90
  106.0 16.1 %all_to_all.32 = f16[16,72,256]{2,1,0:T(8,128)(2,1)S(1)} all-to-all(f16[16,72,256]{2,1,0:T(8,128)(2,1)S(1)} %bitcast.51), channel_id=1, replica_groups=mesh['z'=4,'k'=2,'x'=4,'y'=4] {'x','y'}, dimensions={0} | all-to-all | bytes 1179648 | tf_op jit(solution)/shard_map/all_to_all | solution.py:299
  122.5 1.2 collective-permute-done.14
  124.4 3.3 %collective-permute-start.16 = (f16[2,64,256]{2,1,0:T(8,128)(2,1)S(1)}, f16[2,64,256]{2,1,0:T(8,128)(2,1)S(1)}, u32[]{:S(2)}, u32[]{:S(2)}) collective-permute-start(f16[2,64,256]{2,1,0:T(8,128)(2,1)S(1)} %pad_maximum_fusion.9), channel_id=1, source_target_pairs={{0,32},{4,64},{8,96},{12,0},{16,112},{20,16},{24,48},{28,80},{32,3... | collective-permute-start | bytes 196616 | tf_op jit(solution)/shard_map/ppermute | solution.py:314
  127.7 8.0 %collective-permute-done.16 = f16[2,64,256]{2,1,0:T(8,128)(2,1)S(1)} collective-permute-done((f16[2,64,256]{2,1,0:T(8,128)(2,1)S(1)}, f16[2,64,256]{2,1,0:T(8,128)(2,1)S(1)}, u32[]{:S(2)}, u32[]{:S(2)}) %collective-permute-start.16) | collective-permute-done | bytes 65568 | tf_op jit(solution)/shard_map/ppermute | solution.py:314
  135.8 1.3 collective-permute-done.17
  137.1 4.2 %shard_map.52 = f32[4,4,80,256]{3,2,1,0:T(8,128)S(1)} custom-call(s32[3]{0:T(128)S(1)} %pad_add_fusion.refs_0_, bf16[6,2,2,256,512]{4,3,2,1,0:T(8,128)(2,1)S(1)} %bitcast.46, bf16[6,2,256,512]{3,2,1,0:T(8,128)(2,1)S(1)} %collective-permute-done.2.refs_2_, f32[8,256]{1,0:T(8,128)S(1)} %pad.4.refs_3_, f32[2,2,64,256]{3,2,1,0:T(8,128)S(1)} %get-tuple-element.36.refs_4_, ...), custom_call_target="tpu_custom_call" | custom-call | tf_op jit(solution)/shard_map/pallas_call | solution.py:90
  141.4 16.7 %all_to_all.33 = f16[16,80,256]{2,1,0:T(8,128)(2,1)S(1)} all-to-all(f16[16,80,256]{2,1,0:T(8,128)(2,1)S(1)} %bitcast.48), channel_id=1, replica_groups=mesh['z'=4,'k'=2,'x'=4,'y'=4] {'x','y'}, dimensions={0} | all-to-all | bytes 1310720 | tf_op jit(solution)/shard_map/all_to_all | solution.py:299
  158.6 1.2 collective-permute-done.19
  160.4 3.3 %collective-permute-start.21 = (f16[2,64,256]{2,1,0:T(8,128)(2,1)S(1)}, f16[2,64,256]{2,1,0:T(8,128)(2,1)S(1)}, u32[]{:S(2)}, u32[]{:S(2)}) collective-permute-start(f16[2,64,256]{2,1,0:T(8,128)(2,1)S(1)} %pad_maximum_fusion.10), channel_id=1, source_target_pairs={{0,32},{4,64},{8,96},{12,0},{16,112},{20,16},{24,48},{28,80},{32,3... | collective-permute-start | bytes 196616 | tf_op jit(solution)/shard_map/ppermute | solution.py:314
  163.7 7.8 %collective-permute-done.21 = f16[2,64,256]{2,1,0:T(8,128)(2,1)S(1)} collective-permute-done((f16[2,64,256]{2,1,0:T(8,128)(2,1)S(1)}, f16[2,64,256]{2,1,0:T(8,128)(2,1)S(1)}, u32[]{:S(2)}, u32[]{:S(2)}) %collective-permute-start.21) | collective-permute-done | bytes 65568 | tf_op jit(solution)/shard_map/ppermute | solution.py:314
  171.9 1.3 collective-permute-done.22
  173.3 4.3 %shard_map.54 = f32[4,4,80,256]{3,2,1,0:T(8,128)S(1)} custom-call(s32[3]{0:T(128)S(1)} %pad_add_fusion.refs_0_, bf16[6,2,2,256,512]{4,3,2,1,0:T(8,128)(2,1)S(1)} %bitcast.47, bf16[6,2,256,512]{3,2,1,0:T(8,128)(2,1)S(1)} %collective-permute-done.2.refs_2_, f32[8,256]{1,0:T(8,128)S(1)} %pad.4.refs_3_, f32[2,2,64,256]{3,2,1,0:T(8,128)S(1)} %get-tuple-element.36.refs_4_, ...), custom_call_target="tpu_custom_call" | custom-call | tf_op jit(solution)/shard_map/pallas_call | solution.py:90
  177.6 17.0 %all_to_all.34 = f16[16,80,256]{2,1,0:T(8,128)(2,1)S(1)} all-to-all(f16[16,80,256]{2,1,0:T(8,128)(2,1)S(1)} %bitcast.49), channel_id=1, replica_groups=mesh['z'=4,'k'=2,'x'=4,'y'=4] {'x','y'}, dimensions={0} | all-to-all | bytes 1310720 | tf_op jit(solution)/shard_map/all_to_all | solution.py:299
  197.0 5.3 %all-to-all-start.5 = ((f32[64,8,128]{2,1,0:T(8,128)}), f32[64,8,128]{2,1,0:T(8,128)S(1)}, u32[]{:S(2)}, u32[]{:S(2)}) async-start(f32[64,8,128]{2,1,0:T(8,128)} %shard_map.56), calls=%async_computation.5 | async-start | bytes 524288 | tf_op jit(solution)/shard_map/all_to_all | solution.py:299
  203.1 10.5 %all-to-all-done.5.dots_ref = f32[64,8,128]{2,1,0:T(8,128)S(1)} async-done(((f32[64,8,128]{2,1,0:T(8,128)}), f32[64,8,128]{2,1,0:T(8,128)S(1)}, u32[]{:S(2)}, u32[]{:S(2)}) %all-to-all-start.5) | async-done | bytes 262176 | tf_op jit(solution)/shard_map/all_to_all | solution.py:299
  (86 shorter events, 13.1 us)
Async XLA Ops:
  0.0 24.7 %copy-start = (f32[64,6]{0,1:T(8,128)S(1)}, f32[64,6]{0,1:T(8,128)}, u32[]{:S(2)}) copy-start(f32[64,6]{0,1:T(8,128)} %param.7) | copy-start | bytes 4612
  0.9 0.7 collective-permute-start
  1.5 8.8 %collective-permute-start.1 = (bf16[64,256]{1,0:T(8,128)(2,1)S(1)}, bf16[64,256]{1,0:T(8,128)(2,1)S(1)}, u32[]{:S(2)}, u32[]{:S(2)}) collective-permute-start(bf16[64,256]{1,0:T(8,128)(2,1)S(1)} %collective-permute-done), channel_id=1, source_target_pairs={{0,16},{16,0},{1,17},{17,1},{2,18},{18,2},{3,19},{19,3},{4,20},{20... | collective-permute-start | bytes 98312 | tf_op jit(solution)/shard_map/ppermute | solution.py:322
  6.6 18.1 %copy-start.2 = (s32[256]{0:T(256)S(1)}, s32[256]{0:T(256)}, u32[]{:S(2)}) copy-start(s32[256]{0:T(256)} %param.6) | copy-start | bytes 3076
  10.4 15.7 %collective-permute-start.2 = (bf16[6,2,256,512]{3,2,1,0:T(8,128)(2,1)}, bf16[6,2,256,512]{3,2,1,0:T(8,128)(2,1)S(1)}, u32[]{:S(2)}, u32[]{:S(2)}) collective-permute-start(bf16[6,2,256,512]{3,2,1,0:T(8,128)(2,1)} %slice_bitcast_fusion), channel_id=1, source_target_pairs={{0,16},{16,0},{1,17},{17,1},{2,18},{18,2},{3,19},{19,3},{4,20},{20... | collective-permute-start | bytes 9437192 | tf_op jit(solution)/shard_map/ppermute | solution.py:324
  10.5 6.8 %collective-permute-start.3 = (bf16[2,64,256]{2,1,0:T(8,128)(2,1)S(1)}, bf16[2,64,256]{2,1,0:T(8,128)(2,1)S(1)}, u32[]{:S(2)}, u32[]{:S(2)}) collective-permute-start(bf16[2,64,256]{2,1,0:T(8,128)(2,1)S(1)} %pad_maximum_fusion.6), channel_id=1, source_target_pairs={{0,0},{4,32},{8,64},{12,96},{16,80},{20,112},{24,16},{28,48},{32,4... | collective-permute-start | bytes 196616 | tf_op jit(solution)/shard_map/ppermute | solution.py:314
  11.2 13.5 %collective-permute-start.4 = (bf16[2,64,256]{2,1,0:T(8,128)(2,1)S(1)}, bf16[2,64,256]{2,1,0:T(8,128)(2,1)S(1)}, u32[]{:S(2)}, u32[]{:S(2)}) collective-permute-start(bf16[2,64,256]{2,1,0:T(8,128)(2,1)S(1)} %pad_maximum_fusion.6), channel_id=1, source_target_pairs={{0,32},{4,64},{8,96},{12,0},{16,112},{20,16},{24,48},{28,80},{32,3... | collective-permute-start | bytes 196616 | tf_op jit(solution)/shard_map/ppermute | solution.py:314
  24.6 1.4 collective-permute-start.5
  24.9 38.4 %slice-start = ((s8[6291456]{0:T(1024)(128)(4,1)}), s8[4194304]{0:T(1024)(128)(4,1)S(1)}, s32[]{:S(2)}) async-start(s8[6291456]{0:T(1024)(128)(4,1)} %bitcast.42), calls=%async_computation.6 | async-start | bytes 8388608
  25.1 38.2 %slice-start.1 = ((s8[6291456]{0:T(1024)(128)(4,1)}), s8[2097152]{0:T(1024)(128)(4,1)S(1)}, s32[]{:S(2)}) async-start(s8[6291456]{0:T(1024)(128)(4,1)} %bitcast.42), calls=%async_computation.7 | async-start | bytes 4194304
  50.4 1.3 collective-permute-start.6
  51.7 5.3 %collective-permute-start.7 = (f16[2,64,256]{2,1,0:T(8,128)(2,1)S(1)}, f16[2,64,256]{2,1,0:T(8,128)(2,1)S(1)}, u32[]{:S(2)}, u32[]{:S(2)}) collective-permute-start(f16[2,64,256]{2,1,0:T(8,128)(2,1)S(1)} %pad_maximum_fusion.7), channel_id=1, source_target_pairs={{0,0},{4,32},{8,64},{12,96},{16,80},{20,112},{24,16},{28,48},{32,4... | collective-permute-start | bytes 196616 | tf_op jit(solution)/shard_map/ppermute | solution.py:314
  52.4 9.4 %collective-permute-start.8 = (f16[2,64,256]{2,1,0:T(8,128)(2,1)S(1)}, f16[2,64,256]{2,1,0:T(8,128)(2,1)S(1)}, u32[]{:S(2)}, u32[]{:S(2)}) collective-permute-start(f16[2,64,256]{2,1,0:T(8,128)(2,1)S(1)} %pad_maximum_fusion.7), channel_id=1, source_target_pairs={{0,32},{4,64},{8,96},{12,0},{16,112},{20,16},{24,48},{28,80},{32,3... | collective-permute-start | bytes 196616 | tf_op jit(solution)/shard_map/ppermute | solution.py:314
  61.8 1.4 collective-permute-start.9
  86.7 1.3 collective-permute-start.10
  88.0 4.0 %collective-permute-start.11 = (f16[2,64,256]{2,1,0:T(8,128)(2,1)S(1)}, f16[2,64,256]{2,1,0:T(8,128)(2,1)S(1)}, u32[]{:S(2)}, u32[]{:S(2)}) collective-permute-start(f16[2,64,256]{2,1,0:T(8,128)(2,1)S(1)} %pad_maximum_fusion.8), channel_id=1, source_target_pairs={{0,0},{4,32},{8,64},{12,96},{16,80},{20,112},{24,16},{28,48},{32,4... | collective-permute-start | bytes 196616 | tf_op jit(solution)/shard_map/ppermute | solution.py:314
  88.6 11.3 %collective-permute-start.12 = (f16[2,64,256]{2,1,0:T(8,128)(2,1)S(1)}, f16[2,64,256]{2,1,0:T(8,128)(2,1)S(1)}, u32[]{:S(2)}, u32[]{:S(2)}) collective-permute-start(f16[2,64,256]{2,1,0:T(8,128)(2,1)S(1)} %pad_maximum_fusion.8), channel_id=1, source_target_pairs={{0,32},{4,64},{8,96},{12,0},{16,112},{20,16},{24,48},{28,80},{32,3... | collective-permute-start | bytes 196616 | tf_op jit(solution)/shard_map/ppermute | solution.py:314
  100.0 1.6 collective-permute-start.13
  122.4 1.3 collective-permute-start.14
  123.7 4.0 %collective-permute-start.15 = (f16[2,64,256]{2,1,0:T(8,128)(2,1)S(1)}, f16[2,64,256]{2,1,0:T(8,128)(2,1)S(1)}, u32[]{:S(2)}, u32[]{:S(2)}) collective-permute-start(f16[2,64,256]{2,1,0:T(8,128)(2,1)S(1)} %pad_maximum_fusion.9), channel_id=1, source_target_pairs={{0,0},{4,32},{8,64},{12,96},{16,80},{20,112},{24,16},{28,48},{32,4... | collective-permute-start | bytes 196616 | tf_op jit(solution)/shard_map/ppermute | solution.py:314
  124.4 11.3 %collective-permute-start.16 = (f16[2,64,256]{2,1,0:T(8,128)(2,1)S(1)}, f16[2,64,256]{2,1,0:T(8,128)(2,1)S(1)}, u32[]{:S(2)}, u32[]{:S(2)}) collective-permute-start(f16[2,64,256]{2,1,0:T(8,128)(2,1)S(1)} %pad_maximum_fusion.9), channel_id=1, source_target_pairs={{0,32},{4,64},{8,96},{12,0},{16,112},{20,16},{24,48},{28,80},{32,3... | collective-permute-start | bytes 196616 | tf_op jit(solution)/shard_map/ppermute | solution.py:314
  135.7 1.4 collective-permute-start.17
  158.5 1.3 collective-permute-start.19
  159.8 3.9 %collective-permute-start.20 = (f16[2,64,256]{2,1,0:T(8,128)(2,1)S(1)}, f16[2,64,256]{2,1,0:T(8,128)(2,1)S(1)}, u32[]{:S(2)}, u32[]{:S(2)}) collective-permute-start(f16[2,64,256]{2,1,0:T(8,128)(2,1)S(1)} %pad_maximum_fusion.10), channel_id=1, source_target_pairs={{0,0},{4,32},{8,64},{12,96},{16,80},{20,112},{24,16},{28,48},{32,4... | collective-permute-start | bytes 196616 | tf_op jit(solution)/shard_map/ppermute | solution.py:314
  160.4 11.1 %collective-permute-start.21 = (f16[2,64,256]{2,1,0:T(8,128)(2,1)S(1)}, f16[2,64,256]{2,1,0:T(8,128)(2,1)S(1)}, u32[]{:S(2)}, u32[]{:S(2)}) collective-permute-start(f16[2,64,256]{2,1,0:T(8,128)(2,1)S(1)} %pad_maximum_fusion.10), channel_id=1, source_target_pairs={{0,32},{4,64},{8,96},{12,0},{16,112},{20,16},{24,48},{28,80},{32,3... | collective-permute-start | bytes 196616 | tf_op jit(solution)/shard_map/ppermute | solution.py:314
  171.6 1.6 collective-permute-start.22
  194.8 18.8 %copy-start.1 = (f32[64,256]{1,0:T(8,128)S(1)}, f32[64,256]{1,0:T(8,128)}, u32[]{:S(2)}) copy-start(f32[64,256]{1,0:T(8,128)} %p_ref.1) | copy-start | bytes 196612
  195.0 1.2 collective-permute-start.23
  197.0 16.6 %all-to-all-start.5 = ((f32[64,8,128]{2,1,0:T(8,128)}), f32[64,8,128]{2,1,0:T(8,128)S(1)}, u32[]{:S(2)}, u32[]{:S(2)}) async-start(f32[64,8,128]{2,1,0:T(8,128)} %shard_map.56), calls=%async_computation.5 | async-start | bytes 524288 | tf_op jit(solution)/shard_map/all_to_all | solution.py:299
  202.3 0.7 collective-permute-start.18

commit v7 on v6

--- a/solution.py
+++ b/solution.py
@@ -73,7 +73,7 @@
             for n in range(1, j + 1):
                 inner = inner + d[n] * g(m, n)
             square = square + d[m] * inner
-        length = jnp.sqrt(jnp.maximum(square, 0.0) + epsilon)
+        length = jnp.sqrt(jnp.maximum(square, 1e-7 * g(j + 1, j + 1)) + epsilon)
         hess[(j + 1, j)] = length
         inv = 1.0 / length
         combos[j + 1] = {m: (inv if m == j + 1 else d[m] * inv) for m in d}
@@ -311,7 +311,8 @@
 
     def spread(both):
         wide = jnp.float32 if both.dtype == WIRE else both.dtype
-        own = jnp.stack([lax.ppermute(both, ("z", "k", "x"), pairs) for pairs in SPREAD])
+        own = [lax.ppermute(both, ("z", "k", "x"), pairs) for pairs in SPREAD]
+        own = jnp.stack(own)
         other = lax.ppermute(own, "k", SWAP)
         return own.astype(wide), other.astype(wide)
 
@@ -330,7 +331,8 @@
     pieces, fields = [q], []
     for j in range(1, KRYLOV + 1):
         piece = q.astype(WIRE)
-        fields.append(spread(jnp.stack([piece, lax.ppermute(piece, "k", SWAP)])))
+        both = jnp.stack([piece, lax.ppermute(piece, "k", SWAP)])
+        fields.append(spread(both))
         if j == KRYLOV:
             outer = lax.ppermute(jnp.stack(pieces).astype(WIRE), ALL, TO_OUTER)
         partial = apply_rates(at, kept, got, weights, fields, False)
@@ -346,8 +348,8 @@
         dots,
         lax.ppermute(dots, "k", SWAP),
     )
+    dots, outer = lax.optimization_barrier((dots, outer.astype(jnp.float32)))
     dots = exchange(dots, ("z", "x", "y"))
-    outer = outer.astype(jnp.float32)
     out = jax.ShapeDtypeStruct(populations.shape, jnp.float32)
     return call(finish_kernel, out, populations, outer, gram, dots)
 

time: 215 us -> 217 us (level)
  blocking collectives: 89.3 us -> 98.8 us
  starting transfers between devices: 37 us -> 31.1 us
    ppermute x14 -> x10, starting transfers between devices: 24.3 us -> 8.42 us  [spread(): own = [lax.ppermute(both, ('z', 'k', 'x'), pairs) for pairs in SPREAD]]
    all_to_all x5, blocking collectives: 89.3 us -> 98.8 us  [body(): exchange = lambda v, axes: lax.all_to_all(v, axes, 0, 0, tiled=True)]
    ppermute x14 -> x10, waiting for transfers between devices: 40.7 us -> 31.1 us  [spread(): own = [lax.ppermute(both, ('z', 'k', 'x'), pairs) for pairs in SPREAD]]
    ppermute x5, starting transfers between devices: 0.83 us -> 7.1 us  [spread(): other = lax.ppermute(own, 'k', SWAP)]
    ppermute x1 -> x5, waiting for transfers between devices: 0.01 us -> 4.71 us  [body(): both = jnp.stack([piece, lax.ppermute(piece, 'k', SWAP)])]
    all_to_all x1, waiting for transfers between devices: 10.5 us -> 14.7 us  [body(): exchange = lambda v, axes: lax.all_to_all(v, axes, 0, 0, tiled=True)]
    all_to_all x1, starting transfers between devices: 5.31 us -> 8.65 us  [body(): exchange = lambda v, axes: lax.all_to_all(v, axes, 0, 0, tiled=True)]
    ppermute x1 -> x5, starting transfers between devices: 5.1 us -> 5.44 us  [body(): both = jnp.stack([piece, lax.ppermute(piece, 'k', SWAP)])]
where the time goes in v7:
time: 217 us
  blocking collectives  98.8 us (46%)
  waiting for transfers between devices  56.9 us (26%)
  starting transfers between devices  31.1 us (14%)
  Pallas kernels  22.1 us (10%)
  local copies, waits for them, and re-layouts  3.85 us (2%)
  other arithmetic  3.28 us (2%)
    all_to_all x5, blocking collectives, body(): exchange = lambda v, axes: lax.all_to_all(v, axes, 0, 0, tiled=True)  98.8 us
    ppermute x10, waiting for transfers between devices, spread(): own = [lax.ppermute(both, ('z', 'k', 'x'), pairs) for pairs in SPREAD]  31.1 us
    pallas_call x12, Pallas kernels, call(): pl.pallas_call(kernel, out_shape=outs, in_specs=specs, out_specs=jax.tree...  22.1 us
    all_to_all x1, waiting for transfers between devices, body(): exchange = lambda v, axes: lax.all_to_all(v, axes, 0, 0, tiled=True)  14.7 us
    all_to_all x1, starting transfers between devices, body(): exchange = lambda v, axes: lax.all_to_all(v, axes, 0, 0, tiled=True)  8.65 us
    ppermute x10, starting transfers between devices, spread(): own = [lax.ppermute(both, ('z', 'k', 'x'), pairs) for pairs in SPREAD]  8.42 us
    ppermute x5, starting transfers between devices, spread(): other = lax.ppermute(own, 'k', SWAP)  7.1 us
    ppermute x5, starting transfers between devices, body(): both = jnp.stack([piece, lax.ppermute(piece, 'k', SWAP)])  5.44 us
  transfers between devices with their start and end apart: 25, of which 16 were waited for; matrix products, arithmetic and copies ran while one was open for 2% of the time, Pallas kernels for 0%

profile of v7, /device:TPU:0, one launch (start us, length us, event | category | flops | bytes accessed | tf_op | source)
XLA Modules:
  0.0 216.8 jit_solution(1799382478129196473)
XLA Ops:
  1.5 5.1 %collective-permute-start.1 = (bf16[64,256]{1,0:T(8,128)(2,1)S(1)}, bf16[64,256]{1,0:T(8,128)(2,1)S(1)}, u32[]{:S(2)}, u32[]{:S(2)}) collective-permute-start(bf16[64,256]{1,0:T(8,128)(2,1)S(1)} %collective-permute-done), channel_id=1, source_target_pairs={{0,16},{16,0},{1,17},{17,1},{2,18},{18,2},{3,19},{19,3},{4,20},{20... | collective-permute-start | bytes 98312 | tf_op jit(solution)/shard_map/ppermute | solution.py:323
  6.6 3.7 %slice_bitcast_fusion = bf16[6,2,256,512]{3,2,1,0:T(8,128)(2,1)} fusion(bf16[6,2,2,256,512]{4,3,2,1,0:T(8,128)(2,1)} %bitcast.40), kind=kLoop, calls=%fused_computation | loop fusion | bytes 6291456 | tf_op jit(solution)/shard_map/squeeze | solution.py:302
  10.5 2.0 collective-permute-start.4
  13.1 9.0 %collective-permute-done.4 = bf16[2,64,256]{2,1,0:T(8,128)(2,1)S(1)} collective-permute-done((bf16[2,64,256]{2,1,0:T(8,128)(2,1)S(1)}, bf16[2,64,256]{2,1,0:T(8,128)(2,1)S(1)}, u32[]{:S(2)}, u32[]{:S(2)}) %collective-permute-start.4) | collective-permute-done | bytes 65568 | tf_op jit(solution)/shard_map/ppermute | solution.py:314
  22.1 3.7 %collective-permute-start.5 = (bf16[2,2,64,256]{3,2,1,0:T(8,128)(2,1)S(1)}, bf16[2,2,64,256]{3,2,1,0:T(8,128)(2,1)S(1)}, u32[]{:S(2)}, u32[]{:S(2)}) collective-permute-start(bf16[2,2,64,256]{3,2,1,0:T(8,128)(2,1)S(1)} %pad_maximum_fusion.refs_4_), channel_id=1, source_target_pairs={{0,16},{16,0},{1,17},{17,1},{2,18},{18,2},{3,19},{19,3},{4,20},{20... | collective-permute-start | bytes 393224 | tf_op jit(solution)/shard_map/ppermute | solution.py:316
  26.8 3.7 %shard_map.46 = f32[4,4,64,256]{3,2,1,0:T(8,128)S(1)} custom-call(s32[3]{0:T(128)S(1)} %pad_add_fusion.refs_0_, bf16[6,2,2,256,512]{4,3,2,1,0:T(8,128)(2,1)} %bitcast.41, bf16[6,2,256,512]{3,2,1,0:T(8,128)(2,1)S(1)} %collective-permute-done.2.refs_2_, f32[8,256]{1,0:T(8,128)S(1)} %pad.4.refs_3_, bf16[2,2,64,256]{3,2,1,0:T(8,128)(2,1)S(1)} %pad_maximum_fusion.refs_4_, ...), custom_call_target="tpu_custom_call" | custom-call | tf_op jit(solution)/shard_map/pallas_call | solution.py:90
  30.7 21.1 %all_to_all.30 = f16[16,64,256]{2,1,0:T(8,128)(2,1)S(1)} all-to-all(f16[16,64,256]{2,1,0:T(8,128)(2,1)S(1)} %bitcast.51), channel_id=1, replica_groups=mesh['z'=4,'k'=2,'x'=4,'y'=4] {'x','y'}, dimensions={0} | all-to-all | bytes 1048576 | tf_op jit(solution)/shard_map/all_to_all | solution.py:299
  52.1 1.2 collective-permute-done.6
  54.0 6.6 %collective-permute-done.8 = f16[2,64,256]{2,1,0:T(8,128)(2,1)S(1)} collective-permute-done((f16[2,64,256]{2,1,0:T(8,128)(2,1)S(1)}, f16[2,64,256]{2,1,0:T(8,128)(2,1)S(1)}, u32[]{:S(2)}, u32[]{:S(2)}) %collective-permute-start.8) | collective-permute-done | bytes 65568 | tf_op jit(solution)/shard_map/ppermute | solution.py:314
  60.8 1.3 collective-permute-done.9
  62.2 4.1 %shard_map.48 = f32[4,4,72,256]{3,2,1,0:T(8,128)S(1)} custom-call(s32[3]{0:T(128)S(1)} %pad_add_fusion.refs_0_, bf16[6,2,2,256,512]{4,3,2,1,0:T(8,128)(2,1)S(1)} %bitcast.44, bf16[6,2,256,512]{3,2,1,0:T(8,128)(2,1)S(1)} %collective-permute-done.2.refs_2_, f32[8,256]{1,0:T(8,128)S(1)} %pad.4.refs_3_, f32[2,2,64,256]{3,2,1,0:T(8,128)S(1)} %get-tuple-element.40.refs_4_, ...), custom_call_target="tpu_custom_call" | custom-call | tf_op jit(solution)/shard_map/pallas_call | solution.py:90
  66.5 20.0 %all_to_all.31 = f16[16,72,256]{2,1,0:T(8,128)(2,1)S(1)} all-to-all(f16[16,72,256]{2,1,0:T(8,128)(2,1)S(1)} %bitcast.49), channel_id=1, replica_groups=mesh['z'=4,'k'=2,'x'=4,'y'=4] {'x','y'}, dimensions={0} | all-to-all | bytes 1179648 | tf_op jit(solution)/shard_map/all_to_all | solution.py:299
  86.8 1.2 collective-permute-done.10
  88.0 1.5 collective-permute-start.12
  90.2 4.9 %collective-permute-done.12 = f16[2,64,256]{2,1,0:T(8,128)(2,1)S(1)} collective-permute-done((f16[2,64,256]{2,1,0:T(8,128)(2,1)S(1)}, f16[2,64,256]{2,1,0:T(8,128)(2,1)S(1)}, u32[]{:S(2)}, u32[]{:S(2)}) %collective-permute-start.12) | collective-permute-done | bytes 65568 | tf_op jit(solution)/shard_map/ppermute | solution.py:314
  96.9 4.3 %shard_map.50 = f32[4,4,72,256]{3,2,1,0:T(8,128)S(1)} custom-call(s32[3]{0:T(128)S(1)} %pad_add_fusion.refs_0_, bf16[6,2,2,256,512]{4,3,2,1,0:T(8,128)(2,1)S(1)} %bitcast.45, bf16[6,2,256,512]{3,2,1,0:T(8,128)(2,1)S(1)} %collective-permute-done.2.refs_2_, f32[8,256]{1,0:T(8,128)S(1)} %pad.4.refs_3_, f32[2,2,64,256]{3,2,1,0:T(8,128)S(1)} %get-tuple-element.40.refs_4_, ...), custom_call_target="tpu_custom_call" | custom-call | tf_op jit(solution)/shard_map/pallas_call | solution.py:90
  101.3 20.6 %all_to_all.32 = f16[16,72,256]{2,1,0:T(8,128)(2,1)S(1)} all-to-all(f16[16,72,256]{2,1,0:T(8,128)(2,1)S(1)} %bitcast.50), channel_id=1, replica_groups=mesh['z'=4,'k'=2,'x'=4,'y'=4] {'x','y'}, dimensions={0} | all-to-all | bytes 1179648 | tf_op jit(solution)/shard_map/all_to_all | solution.py:299
  122.3 1.2 collective-permute-done.14
  123.5 1.5 collective-permute-start.16
  125.7 4.4 %collective-permute-done.16 = f16[2,64,256]{2,1,0:T(8,128)(2,1)S(1)} collective-permute-done((f16[2,64,256]{2,1,0:T(8,128)(2,1)S(1)}, f16[2,64,256]{2,1,0:T(8,128)(2,1)S(1)}, u32[]{:S(2)}, u32[]{:S(2)}) %collective-permute-start.16) | collective-permute-done | bytes 65568 | tf_op jit(solution)/shard_map/ppermute | solution.py:314
  130.1 2.2 %collective-permute-start.17 = (f16[2,2,64,256]{3,2,1,0:T(8,128)(2,1)S(1)}, f16[2,2,64,256]{3,2,1,0:T(8,128)(2,1)S(1)}, u32[]{:S(2)}, u32[]{:S(2)}) collective-permute-start(f16[2,2,64,256]{3,2,1,0:T(8,128)(2,1)S(1)} %get-tuple-element.35), channel_id=1, source_target_pairs={{0,16},{16,0},{1,17},{17,1},{2,18},{18,2},{3,19},{19,3},{4,20},{20... | collective-permute-start | bytes 393224 | tf_op jit(solution)/shard_map/ppermute | solution.py:316
  132.3 1.0 collective-permute-done.17
  133.3 4.2 %shard_map.52 = f32[4,4,80,256]{3,2,1,0:T(8,128)S(1)} custom-call(s32[3]{0:T(128)S(1)} %pad_add_fusion.refs_0_, bf16[6,2,2,256,512]{4,3,2,1,0:T(8,128)(2,1)S(1)} %bitcast.46, bf16[6,2,256,512]{3,2,1,0:T(8,128)(2,1)S(1)} %collective-permute-done.2.refs_2_, f32[8,256]{1,0:T(8,128)S(1)} %pad.4.refs_3_, f32[2,2,64,256]{3,2,1,0:T(8,128)S(1)} %get-tuple-element.40.refs_4_, ...), custom_call_target="tpu_custom_call" | custom-call | tf_op jit(solution)/shard_map/pallas_call | solution.py:90
  137.6 22.1 %all_to_all.33 = f16[16,80,256]{2,1,0:T(8,128)(2,1)S(1)} all-to-all(f16[16,80,256]{2,1,0:T(8,128)(2,1)S(1)} %bitcast.48), channel_id=1, replica_groups=mesh['z'=4,'k'=2,'x'=4,'y'=4] {'x','y'}, dimensions={0} | all-to-all | bytes 1310720 | tf_op jit(solution)/shard_map/all_to_all | solution.py:299
  160.1 1.2 collective-permute-done.18
  162.1 6.3 %collective-permute-done.20 = f16[2,64,256]{2,1,0:T(8,128)(2,1)S(1)} collective-permute-done((f16[2,64,256]{2,1,0:T(8,128)(2,1)S(1)}, f16[2,64,256]{2,1,0:T(8,128)(2,1)S(1)}, u32[]{:S(2)}, u32[]{:S(2)}) %collective-permute-start.20) | collective-permute-done | bytes 65568 | tf_op jit(solution)/shard_map/ppermute | solution.py:314
  168.7 1.3 collective-permute-done.21
  170.0 4.3 %shard_map.54 = f32[4,4,80,256]{3,2,1,0:T(8,128)S(1)} custom-call(s32[3]{0:T(128)S(1)} %pad_add_fusion.refs_0_, bf16[6,2,2,256,512]{4,3,2,1,0:T(8,128)(2,1)S(1)} %bitcast.47, bf16[6,2,256,512]{3,2,1,0:T(8,128)(2,1)S(1)} %collective-permute-done.2.refs_2_, f32[8,256]{1,0:T(8,128)S(1)} %pad.4.refs_3_, f32[2,2,64,256]{3,2,1,0:T(8,128)S(1)} %get-tuple-element.40.refs_4_, ...), custom_call_target="tpu_custom_call" | custom-call | tf_op jit(solution)/shard_map/pallas_call | solution.py:90
  175.3 8.6 %all-to-all-start.4 = ((f16[16,80,256]{2,1,0:T(8,128)(2,1)}), f16[16,80,256]{2,1,0:T(8,128)(2,1)S(1)}, u32[]{:S(2)}, u32[]{:S(2)}) async-start(f16[16,80,256]{2,1,0:T(8,128)(2,1)} %bitcast.30), calls=%async_computation.4 | async-start | bytes 1310720 | tf_op jit(solution)/shard_map/all_to_all | solution.py:299
  184.7 14.7 %all-to-all-done.4 = f16[16,80,256]{2,1,0:T(8,128)(2,1)S(1)} async-done(((f16[16,80,256]{2,1,0:T(8,128)(2,1)}), f16[16,80,256]{2,1,0:T(8,128)(2,1)S(1)}, u32[]{:S(2)}, u32[]{:S(2)}) %all-to-all-start.4) | async-done | bytes 655392 | tf_op jit(solution)/shard_map/all_to_all | solution.py:299
  199.9 1.1 collective-permute-done.22.other_ref
  201.0 15.0 %all_to_all.34.dots_ref = f32[64,8,128]{2,1,0:T(8,128)S(1)} all-to-all(f32[64,8,128]{2,1,0:T(8,128)S(1)} %shard_map.56), channel_id=1, replica_groups=mesh['z'=4,'k'=2,'x'=4,'y'=4] {'z','x','y'}, dimensions={0} | all-to-all | bytes 524288 | tf_op jit(solution)/shard_map/all_to_all | solution.py:299
  (90 shorter events, 13.2 us)
Async XLA Ops:
  0.0 25.8 %copy-start = (f32[64,6]{0,1:T(8,128)S(1)}, f32[64,6]{0,1:T(8,128)}, u32[]{:S(2)}) copy-start(f32[64,6]{0,1:T(8,128)} %param.7) | copy-start | bytes 4612
  0.9 0.7 collective-permute-start
  1.5 8.9 %collective-permute-start.1 = (bf16[64,256]{1,0:T(8,128)(2,1)S(1)}, bf16[64,256]{1,0:T(8,128)(2,1)S(1)}, u32[]{:S(2)}, u32[]{:S(2)}) collective-permute-start(bf16[64,256]{1,0:T(8,128)(2,1)S(1)} %collective-permute-done), channel_id=1, source_target_pairs={{0,16},{16,0},{1,17},{17,1},{2,18},{18,2},{3,19},{19,3},{4,20},{20... | collective-permute-start | bytes 98312 | tf_op jit(solution)/shard_map/ppermute | solution.py:323
  6.6 19.2 %copy-start.4 = (s32[256]{0:T(256)S(1)}, s32[256]{0:T(256)}, u32[]{:S(2)}) copy-start(s32[256]{0:T(256)} %param.6) | copy-start | bytes 3076
  10.4 16.4 %collective-permute-start.2 = (bf16[6,2,256,512]{3,2,1,0:T(8,128)(2,1)}, bf16[6,2,256,512]{3,2,1,0:T(8,128)(2,1)S(1)}, u32[]{:S(2)}, u32[]{:S(2)}) collective-permute-start(bf16[6,2,256,512]{3,2,1,0:T(8,128)(2,1)} %slice_bitcast_fusion), channel_id=1, source_target_pairs={{0,16},{16,0},{1,17},{17,1},{2,18},{18,2},{3,19},{19,3},{4,20},{20... | collective-permute-start | bytes 9437192 | tf_op jit(solution)/shard_map/ppermute | solution.py:325
  10.5 11.6 %collective-permute-start.4 = (bf16[2,64,256]{2,1,0:T(8,128)(2,1)S(1)}, bf16[2,64,256]{2,1,0:T(8,128)(2,1)S(1)}, u32[]{:S(2)}, u32[]{:S(2)}) collective-permute-start(bf16[2,64,256]{2,1,0:T(8,128)(2,1)S(1)} %pad_maximum_fusion.6), channel_id=1, source_target_pairs={{0,32},{4,64},{8,96},{12,0},{16,112},{20,16},{24,48},{28,80},{32,3... | collective-permute-start | bytes 196616 | tf_op jit(solution)/shard_map/ppermute | solution.py:314
  12.5 9.6 %collective-permute-start.3 = (bf16[2,64,256]{2,1,0:T(8,128)(2,1)S(1)}, bf16[2,64,256]{2,1,0:T(8,128)(2,1)S(1)}, u32[]{:S(2)}, u32[]{:S(2)}) collective-permute-start(bf16[2,64,256]{2,1,0:T(8,128)(2,1)S(1)} %pad_maximum_fusion.6), channel_id=1, source_target_pairs={{0,0},{4,32},{8,64},{12,96},{16,80},{20,112},{24,16},{28,48},{32,4... | collective-permute-start | bytes 196616 | tf_op jit(solution)/shard_map/ppermute | solution.py:314
  22.1 4.7 %collective-permute-start.5 = (bf16[2,2,64,256]{3,2,1,0:T(8,128)(2,1)S(1)}, bf16[2,2,64,256]{3,2,1,0:T(8,128)(2,1)S(1)}, u32[]{:S(2)}, u32[]{:S(2)}) collective-permute-start(bf16[2,2,64,256]{3,2,1,0:T(8,128)(2,1)S(1)} %pad_maximum_fusion.refs_4_), channel_id=1, source_target_pairs={{0,16},{16,0},{1,17},{17,1},{2,18},{18,2},{3,19},{19,3},{4,20},{20... | collective-permute-start | bytes 393224 | tf_op jit(solution)/shard_map/ppermute | solution.py:316
  26.0 36.2 %slice-start = ((s8[6291456]{0:T(1024)(128)(4,1)}), s8[4194304]{0:T(1024)(128)(4,1)S(1)}, s32[]{:S(2)}) async-start(s8[6291456]{0:T(1024)(128)(4,1)} %bitcast.42), calls=%async_computation.6 | async-start | bytes 8388608
  26.2 36.0 %slice-start.1 = ((s8[6291456]{0:T(1024)(128)(4,1)}), s8[2097152]{0:T(1024)(128)(4,1)S(1)}, s32[]{:S(2)}) async-start(s8[6291456]{0:T(1024)(128)(4,1)} %bitcast.42), calls=%async_computation.7 | async-start | bytes 4194304
  52.0 1.3 collective-permute-start.6
  53.3 7.4 %collective-permute-start.8 = (f16[2,64,256]{2,1,0:T(8,128)(2,1)S(1)}, f16[2,64,256]{2,1,0:T(8,128)(2,1)S(1)}, u32[]{:S(2)}, u32[]{:S(2)}) collective-permute-start(f16[2,64,256]{2,1,0:T(8,128)(2,1)S(1)} %pad_maximum_fusion.7), channel_id=1, source_target_pairs={{0,32},{4,64},{8,96},{12,0},{16,112},{20,16},{24,48},{28,80},{32,3... | collective-permute-start | bytes 196616 | tf_op jit(solution)/shard_map/ppermute | solution.py:314
  53.4 7.3 %collective-permute-start.7 = (f16[2,64,256]{2,1,0:T(8,128)(2,1)S(1)}, f16[2,64,256]{2,1,0:T(8,128)(2,1)S(1)}, u32[]{:S(2)}, u32[]{:S(2)}) collective-permute-start(f16[2,64,256]{2,1,0:T(8,128)(2,1)S(1)} %pad_maximum_fusion.7), channel_id=1, source_target_pairs={{0,0},{4,32},{8,64},{12,96},{16,80},{20,112},{24,16},{28,48},{32,4... | collective-permute-start | bytes 196616 | tf_op jit(solution)/shard_map/ppermute | solution.py:314
  60.7 1.4 collective-permute-start.9
  86.7 1.3 collective-permute-start.10
  88.0 7.1 %collective-permute-start.12 = (f16[2,64,256]{2,1,0:T(8,128)(2,1)S(1)}, f16[2,64,256]{2,1,0:T(8,128)(2,1)S(1)}, u32[]{:S(2)}, u32[]{:S(2)}) collective-permute-start(f16[2,64,256]{2,1,0:T(8,128)(2,1)S(1)} %pad_maximum_fusion.8), channel_id=1, source_target_pairs={{0,32},{4,64},{8,96},{12,0},{16,112},{20,16},{24,48},{28,80},{32,3... | collective-permute-start | bytes 196616 | tf_op jit(solution)/shard_map/ppermute | solution.py:314
  89.5 5.5 %collective-permute-start.11 = (f16[2,64,256]{2,1,0:T(8,128)(2,1)S(1)}, f16[2,64,256]{2,1,0:T(8,128)(2,1)S(1)}, u32[]{:S(2)}, u32[]{:S(2)}) collective-permute-start(f16[2,64,256]{2,1,0:T(8,128)(2,1)S(1)} %pad_maximum_fusion.8), channel_id=1, source_target_pairs={{0,0},{4,32},{8,64},{12,96},{16,80},{20,112},{24,16},{28,48},{32,4... | collective-permute-start | bytes 196616 | tf_op jit(solution)/shard_map/ppermute | solution.py:314
  95.1 1.8 collective-permute-start.13
  122.2 1.3 collective-permute-start.14
  123.5 6.5 %collective-permute-start.16 = (f16[2,64,256]{2,1,0:T(8,128)(2,1)S(1)}, f16[2,64,256]{2,1,0:T(8,128)(2,1)S(1)}, u32[]{:S(2)}, u32[]{:S(2)}) collective-permute-start(f16[2,64,256]{2,1,0:T(8,128)(2,1)S(1)} %pad_maximum_fusion.9), channel_id=1, source_target_pairs={{0,32},{4,64},{8,96},{12,0},{16,112},{20,16},{24,48},{28,80},{32,3... | collective-permute-start | bytes 196616 | tf_op jit(solution)/shard_map/ppermute | solution.py:314
  125.0 5.1 %collective-permute-start.15 = (f16[2,64,256]{2,1,0:T(8,128)(2,1)S(1)}, f16[2,64,256]{2,1,0:T(8,128)(2,1)S(1)}, u32[]{:S(2)}, u32[]{:S(2)}) collective-permute-start(f16[2,64,256]{2,1,0:T(8,128)(2,1)S(1)} %pad_maximum_fusion.9), channel_id=1, source_target_pairs={{0,0},{4,32},{8,64},{12,96},{16,80},{20,112},{24,16},{28,48},{32,4... | collective-permute-start | bytes 196616 | tf_op jit(solution)/shard_map/ppermute | solution.py:314
  130.1 3.2 %collective-permute-start.17 = (f16[2,2,64,256]{3,2,1,0:T(8,128)(2,1)S(1)}, f16[2,2,64,256]{3,2,1,0:T(8,128)(2,1)S(1)}, u32[]{:S(2)}, u32[]{:S(2)}) collective-permute-start(f16[2,2,64,256]{3,2,1,0:T(8,128)(2,1)S(1)} %get-tuple-element.35), channel_id=1, source_target_pairs={{0,16},{16,0},{1,17},{17,1},{2,18},{18,2},{3,19},{19,3},{4,20},{20... | collective-permute-start | bytes 393224 | tf_op jit(solution)/shard_map/ppermute | solution.py:316
  160.0 1.3 collective-permute-start.18
  160.1 9.9 %copy-start.2 = (f16[1,64,256]{2,1,0:T(8,128)(2,1)}, f16[1,64,256]{2,1,0:T(8,128)(2,1)S(1)}, u32[]{:S(2)}) copy-start(f16[1,64,256]{2,1,0:T(8,128)(2,1)S(1)} %convert_bitcast_fusion) | copy-start | bytes 98308
  161.3 7.0 %collective-permute-start.20 = (f16[2,64,256]{2,1,0:T(8,128)(2,1)S(1)}, f16[2,64,256]{2,1,0:T(8,128)(2,1)S(1)}, u32[]{:S(2)}, u32[]{:S(2)}) collective-permute-start(f16[2,64,256]{2,1,0:T(8,128)(2,1)S(1)} %pad_maximum_fusion.10), channel_id=1, source_target_pairs={{0,32},{4,64},{8,96},{12,0},{16,112},{20,16},{24,48},{28,80},{32,3... | collective-permute-start | bytes 196616 | tf_op jit(solution)/shard_map/ppermute | solution.py:314
  161.4 6.9 %collective-permute-start.19 = (f16[2,64,256]{2,1,0:T(8,128)(2,1)S(1)}, f16[2,64,256]{2,1,0:T(8,128)(2,1)S(1)}, u32[]{:S(2)}, u32[]{:S(2)}) collective-permute-start(f16[2,64,256]{2,1,0:T(8,128)(2,1)S(1)} %pad_maximum_fusion.10), channel_id=1, source_target_pairs={{0,0},{4,32},{8,64},{12,96},{16,80},{20,112},{24,16},{28,48},{32,4... | collective-permute-start | bytes 196616 | tf_op jit(solution)/shard_map/ppermute | solution.py:314
  168.4 1.6 collective-permute-start.21
  174.3 9.6 %copy-start.3 = (f16[1,64,256]{2,1,0:T(8,128)(2,1)S(1)}, f16[1,64,256]{2,1,0:T(8,128)(2,1)}, u32[]{:S(2)}) copy-start(f16[1,64,256]{2,1,0:T(8,128)(2,1)} %copy-done.2) | copy-start | bytes 98308
  175.3 24.1 %all-to-all-start.4 = ((f16[16,80,256]{2,1,0:T(8,128)(2,1)}), f16[16,80,256]{2,1,0:T(8,128)(2,1)S(1)}, u32[]{:S(2)}, u32[]{:S(2)}) async-start(f16[16,80,256]{2,1,0:T(8,128)(2,1)} %bitcast.30), calls=%async_computation.4 | async-start | bytes 1310720 | tf_op jit(solution)/shard_map/all_to_all | solution.py:299
  184.0 15.8 %collective-permute-start.23 = (f16[4,64,256]{2,1,0:T(8,128)(2,1)S(1)}, f16[4,64,256]{2,1,0:T(8,128)(2,1)S(1)}, u32[]{:S(2)}, u32[]{:S(2)}) collective-permute-start(f16[4,64,256]{2,1,0:T(8,128)(2,1)S(1)} %pad_maximum_fusion.5), channel_id=1, source_target_pairs={{0,0},{4,1},{8,2},{12,3},{16,4},{20,5},{24,6},{28,7},{1,8},{5,9},{... | collective-permute-start | bytes 393224 | tf_op jit(solution)/shard_map/ppermute | solution.py:337
  199.5 16.5 %copy-start.1 = (f32[64,256]{1,0:T(8,128)S(1)}, f32[64,256]{1,0:T(8,128)}, u32[]{:S(2)}) copy-start(f32[64,256]{1,0:T(8,128)} %p_ref.1) | copy-start | bytes 196612
  199.7 1.2 collective-permute-start.22

commit v8 on v7

--- a/solution.py
+++ b/solution.py
@@ -126,22 +126,6 @@
             if not exact:
                 low = (value - high.astype(jnp.float32)).astype(jnp.bfloat16)
                 x_ref[rows, pl.ds(cells, cells)] = low
-    if not exact:
-        extra_ref = refs[-1]
-        extra_ref[...] = jnp.zeros_like(extra_ref)
-        for m in range(n_fields):
-            total = jnp.zeros((8, cells), jnp.float32)
-            for a_ref, b_ref in ((own_refs[m], own_refs[-1]), (other_refs[m], other_refs[-1])):
-                product = a_ref[...] * b_ref[...]
-                total = total + jnp.sum(product.reshape(HALF // 8, 8, cells), axis=0)
-            total = jnp.sum(total, axis=0, keepdims=True)
-            power = exponent(total)
-            total = total * jnp.exp2(-power)
-            high = total.astype(jnp.bfloat16).astype(jnp.float32)
-            extra_ref[pl.ds(3 * m + 1, 1), :] = power
-            extra_ref[pl.ds(3 * m + 2, 1), :] = high
-            extra_ref[pl.ds(3 * m + 3, 1), :] = (total - high) * 256.0
-
     for g in (2, 3, 0, 1):
         y = (g + 2 * core) % NY
         total = None
@@ -164,8 +148,25 @@
                 continue
             power = exponent(jnp.max(jnp.abs(block), axis=0, keepdims=True))
             out_ref[x, y, pl.ds(0, SUB), :] = block * jnp.exp2(-power)
-            out_ref[x, y, pl.ds(SUB, extra_ref.shape[0]), :] = extra_ref[...]
             out_ref[x, y, pl.ds(SUB, 1), :] = power
+    if not exact:
+        extra_ref = refs[-1]
+        extra_ref[...] = jnp.zeros_like(extra_ref)
+        for m in range(n_fields):
+            total = jnp.zeros((8, cells), jnp.float32)
+            for a_ref, b_ref in ((own_refs[m], own_refs[-1]), (other_refs[m], other_refs[-1])):
+                product = a_ref[...] * b_ref[...]
+                total = total + jnp.sum(product.reshape(HALF // 8, 8, cells), axis=0)
+            total = jnp.sum(total, axis=0, keepdims=True)
+            power = exponent(total)
+            total = total * jnp.exp2(-power)
+            high = total.astype(jnp.bfloat16).astype(jnp.float32)
+            extra_ref[pl.ds(3 * m + 1, 1), :] = power
+            extra_ref[pl.ds(3 * m + 2, 1), :] = high
+            extra_ref[pl.ds(3 * m + 3, 1), :] = (total - high) * 256.0
+        for b in range(NX * NY):
+            x, y = divmod(b, NY)
+            out_ref[x, y, pl.ds(SUB + 1, extra_ref.shape[0] - 1), :] = extra_ref[pl.ds(1, extra_ref.shape[0] - 1), :]
 
 
 def apply_rates(at, kept, got, weights, fields, exact):
@@ -334,7 +335,7 @@
         both = jnp.stack([piece, lax.ppermute(piece, "k", SWAP)])
         fields.append(spread(both))
         if j == KRYLOV:
-            outer = lax.ppermute(jnp.stack(pieces).astype(WIRE), ALL, TO_OUTER)
+            inner = jnp.stack(pieces).astype(WIRE)
         partial = apply_rates(at, kept, got, weights, fields, False)
         met = reduce(partial)
         if j < KRYLOV:
@@ -342,14 +343,16 @@
             pieces.append(q)
         else:
             dots, gram = combine(j, met, gram, pieces)
+            inner, dots = lax.optimization_barrier((inner, dots))
+            outer = lax.ppermute(inner, ALL, TO_OUTER)
     dots = call(
         pair_kernel,
         jax.ShapeDtypeStruct((NZ * NX * NY, *dots.shape), dots.dtype),
         dots,
         lax.ppermute(dots, "k", SWAP),
     )
-    dots, outer = lax.optimization_barrier((dots, outer.astype(jnp.float32)))
     dots = exchange(dots, ("z", "x", "y"))
+    outer = outer.astype(jnp.float32)
     out = jax.ShapeDtypeStruct(populations.shape, jnp.float32)
     return call(finish_kernel, out, populations, outer, gram, dots)
 

time: 217 us -> 218 us (level)
  blocking collectives: 98.8 us -> 83.8 us
  waiting for transfers between devices: 56.9 us -> 66 us
  starting transfers between devices: 31.1 us -> 36.3 us
    all_to_all x5 -> x4, blocking collectives: 98.8 us -> 83.8 us  [body(): exchange = lambda v, axes: lax.all_to_all(v, axes, 0, 0, tiled=True)]
    all_to_all x1 -> x2, waiting for transfers between devices: 14.7 us -> 23.7 us  [body(): exchange = lambda v, axes: lax.all_to_all(v, axes, 0, 0, tiled=True)]
    all_to_all x1 -> x2, starting transfers between devices: 8.65 us -> 13.8 us  [body(): exchange = lambda v, axes: lax.all_to_all(v, axes, 0, 0, tiled=True)]
  transfers between devices with their start and end apart: 25 -> 26, of which waited for: 16 -> 17; matrix products, arithmetic and copies ran while one was open for 2% -> 2% of each run, Pallas kernels for 0% -> 0%
where the time goes in v8:
time: 218 us; the launch traced here: 217 us
  blocking collectives  83.8 us (38%)
  waiting for transfers between devices  66 us (30%)
  starting transfers between devices  36.3 us (17%)
  Pallas kernels  23.1 us (11%)
  local copies, waits for them, and re-layouts  3.86 us (2%)
  other arithmetic  3.28 us (2%)
    all_to_all x4, blocking collectives, body(): exchange = lambda v, axes: lax.all_to_all(v, axes, 0, 0, tiled=True)  83.8 us
    ppermute x10, waiting for transfers between devices, spread(): own = [lax.ppermute(both, ('z', 'k', 'x'), pairs) for pairs in SPREAD]  31.1 us
    all_to_all x2, waiting for transfers between devices, body(): exchange = lambda v, axes: lax.all_to_all(v, axes, 0, 0, tiled=True)  23.7 us
    pallas_call x12, Pallas kernels, call(): pl.pallas_call(kernel, out_shape=outs, in_specs=specs, out_specs=jax.tree...  23.1 us
    all_to_all x2, starting transfers between devices, body(): exchange = lambda v, axes: lax.all_to_all(v, axes, 0, 0, tiled=True)  13.8 us
    ppermute x10, starting transfers between devices, spread(): own = [lax.ppermute(both, ('z', 'k', 'x'), pairs) for pairs in SPREAD]  8.42 us
    ppermute x5, starting transfers between devices, spread(): other = lax.ppermute(own, 'k', SWAP)  7.1 us
    ppermute x5, starting transfers between devices, body(): both = jnp.stack([piece, lax.ppermute(piece, 'k', SWAP)])  5.44 us
  transfers between devices with their start and end apart: 26, of which 17 were waited for; matrix products, arithmetic and copies ran while one was open for 2% of the time, Pallas kernels for 0%

profile of v8, /device:TPU:0, one launch (start us, length us, event | category | flops | bytes accessed | tf_op | source)
XLA Modules:
  0.0 217.1 jit_solution(5038902208205091049)
XLA Ops:
  1.5 5.1 %collective-permute-start.1 = (bf16[64,256]{1,0:T(8,128)(2,1)S(1)}, bf16[64,256]{1,0:T(8,128)(2,1)S(1)}, u32[]{:S(2)}, u32[]{:S(2)}) collective-permute-start(bf16[64,256]{1,0:T(8,128)(2,1)S(1)} %collective-permute-done), channel_id=1, source_target_pairs={{0,16},{16,0},{1,17},{17,1},{2,18},{18,2},{3,19},{19,3},{4,20},{20... | collective-permute-start | bytes 98312 | tf_op jit(solution)/shard_map/ppermute | solution.py:324
  6.6 3.8 %slice_bitcast_fusion = bf16[6,2,256,512]{3,2,1,0:T(8,128)(2,1)} fusion(bf16[6,2,2,256,512]{4,3,2,1,0:T(8,128)(2,1)} %bitcast.40), kind=kLoop, calls=%fused_computation | loop fusion | bytes 6291456 | tf_op jit(solution)/shard_map/squeeze | solution.py:303
  10.5 2.0 collective-permute-start.4
  13.1 9.0 %collective-permute-done.4 = bf16[2,64,256]{2,1,0:T(8,128)(2,1)S(1)} collective-permute-done((bf16[2,64,256]{2,1,0:T(8,128)(2,1)S(1)}, bf16[2,64,256]{2,1,0:T(8,128)(2,1)S(1)}, u32[]{:S(2)}, u32[]{:S(2)}) %collective-permute-start.4) | collective-permute-done | bytes 65568 | tf_op jit(solution)/shard_map/ppermute | solution.py:315
  22.1 3.7 %collective-permute-start.5 = (bf16[2,2,64,256]{3,2,1,0:T(8,128)(2,1)S(1)}, bf16[2,2,64,256]{3,2,1,0:T(8,128)(2,1)S(1)}, u32[]{:S(2)}, u32[]{:S(2)}) collective-permute-start(bf16[2,2,64,256]{3,2,1,0:T(8,128)(2,1)S(1)} %pad_maximum_fusion.refs_4_), channel_id=1, source_target_pairs={{0,16},{16,0},{1,17},{17,1},{2,18},{18,2},{3,19},{19,3},{4,20},{20... | collective-permute-start | bytes 393224 | tf_op jit(solution)/shard_map/ppermute | solution.py:317
  26.8 3.7 %shard_map.46 = f32[4,4,64,256]{3,2,1,0:T(8,128)S(1)} custom-call(s32[3]{0:T(128)S(1)} %pad_add_fusion.refs_0_, bf16[6,2,2,256,512]{4,3,2,1,0:T(8,128)(2,1)} %bitcast.41, bf16[6,2,256,512]{3,2,1,0:T(8,128)(2,1)S(1)} %collective-permute-done.2.refs_2_, f32[8,256]{1,0:T(8,128)S(1)} %pad.4.refs_3_, bf16[2,2,64,256]{3,2,1,0:T(8,128)(2,1)S(1)} %pad_maximum_fusion.refs_4_, ...), custom_call_target="tpu_custom_call" | custom-call | tf_op jit(solution)/shard_map/pallas_call | solution.py:90
  30.7 21.1 %all_to_all.30 = f16[16,64,256]{2,1,0:T(8,128)(2,1)S(1)} all-to-all(f16[16,64,256]{2,1,0:T(8,128)(2,1)S(1)} %bitcast.51), channel_id=1, replica_groups=mesh['z'=4,'k'=2,'x'=4,'y'=4] {'x','y'}, dimensions={0} | all-to-all | bytes 1048576 | tf_op jit(solution)/shard_map/all_to_all | solution.py:300
  52.1 1.2 collective-permute-done.6
  54.1 6.6 %collective-permute-done.8 = f16[2,64,256]{2,1,0:T(8,128)(2,1)S(1)} collective-permute-done((f16[2,64,256]{2,1,0:T(8,128)(2,1)S(1)}, f16[2,64,256]{2,1,0:T(8,128)(2,1)S(1)}, u32[]{:S(2)}, u32[]{:S(2)}) %collective-permute-start.8) | collective-permute-done | bytes 65568 | tf_op jit(solution)/shard_map/ppermute | solution.py:315
  60.8 1.3 collective-permute-done.9
  62.2 4.1 %shard_map.48 = f32[4,4,72,256]{3,2,1,0:T(8,128)S(1)} custom-call(s32[3]{0:T(128)S(1)} %pad_add_fusion.refs_0_, bf16[6,2,2,256,512]{4,3,2,1,0:T(8,128)(2,1)S(1)} %bitcast.44, bf16[6,2,256,512]{3,2,1,0:T(8,128)(2,1)S(1)} %collective-permute-done.2.refs_2_, f32[8,256]{1,0:T(8,128)S(1)} %pad.4.refs_3_, f32[2,2,64,256]{3,2,1,0:T(8,128)S(1)} %get-tuple-element.40.refs_4_, ...), custom_call_target="tpu_custom_call" | custom-call | tf_op jit(solution)/shard_map/pallas_call | solution.py:90
  66.5 20.0 %all_to_all.31 = f16[16,72,256]{2,1,0:T(8,128)(2,1)S(1)} all-to-all(f16[16,72,256]{2,1,0:T(8,128)(2,1)S(1)} %bitcast.49), channel_id=1, replica_groups=mesh['z'=4,'k'=2,'x'=4,'y'=4] {'x','y'}, dimensions={0} | all-to-all | bytes 1179648 | tf_op jit(solution)/shard_map/all_to_all | solution.py:300
  86.8 1.2 collective-permute-done.10
  88.0 1.5 collective-permute-start.12
  90.2 4.9 %collective-permute-done.12 = f16[2,64,256]{2,1,0:T(8,128)(2,1)S(1)} collective-permute-done((f16[2,64,256]{2,1,0:T(8,128)(2,1)S(1)}, f16[2,64,256]{2,1,0:T(8,128)(2,1)S(1)}, u32[]{:S(2)}, u32[]{:S(2)}) %collective-permute-start.12) | collective-permute-done | bytes 65568 | tf_op jit(solution)/shard_map/ppermute | solution.py:315
  97.0 4.2 %shard_map.50 = f32[4,4,72,256]{3,2,1,0:T(8,128)S(1)} custom-call(s32[3]{0:T(128)S(1)} %pad_add_fusion.refs_0_, bf16[6,2,2,256,512]{4,3,2,1,0:T(8,128)(2,1)S(1)} %bitcast.45, bf16[6,2,256,512]{3,2,1,0:T(8,128)(2,1)S(1)} %collective-permute-done.2.refs_2_, f32[8,256]{1,0:T(8,128)S(1)} %pad.4.refs_3_, f32[2,2,64,256]{3,2,1,0:T(8,128)S(1)} %get-tuple-element.40.refs_4_, ...), custom_call_target="tpu_custom_call" | custom-call | tf_op jit(solution)/shard_map/pallas_call | solution.py:90
  101.3 20.6 %all_to_all.32 = f16[16,72,256]{2,1,0:T(8,128)(2,1)S(1)} all-to-all(f16[16,72,256]{2,1,0:T(8,128)(2,1)S(1)} %bitcast.50), channel_id=1, replica_groups=mesh['z'=4,'k'=2,'x'=4,'y'=4] {'x','y'}, dimensions={0} | all-to-all | bytes 1179648 | tf_op jit(solution)/shard_map/all_to_all | solution.py:300
  122.3 1.2 collective-permute-done.14
  123.5 1.5 collective-permute-start.16
  125.6 4.4 %collective-permute-done.16 = f16[2,64,256]{2,1,0:T(8,128)(2,1)S(1)} collective-permute-done((f16[2,64,256]{2,1,0:T(8,128)(2,1)S(1)}, f16[2,64,256]{2,1,0:T(8,128)(2,1)S(1)}, u32[]{:S(2)}, u32[]{:S(2)}) %collective-permute-start.16) | collective-permute-done | bytes 65568 | tf_op jit(solution)/shard_map/ppermute | solution.py:315
  130.1 2.2 collective-permute-start.17
  133.3 4.4 %shard_map.52 = f32[4,4,80,256]{3,2,1,0:T(8,128)S(1)} custom-call(s32[3]{0:T(128)S(1)} %pad_add_fusion.refs_0_, bf16[6,2,2,256,512]{4,3,2,1,0:T(8,128)(2,1)S(1)} %bitcast.46, bf16[6,2,256,512]{3,2,1,0:T(8,128)(2,1)S(1)} %collective-permute-done.2.refs_2_, f32[8,256]{1,0:T(8,128)S(1)} %pad.4.refs_3_, f32[2,2,64,256]{3,2,1,0:T(8,128)S(1)} %get-tuple-element.40.refs_4_, ...), custom_call_target="tpu_custom_call" | custom-call | tf_op jit(solution)/shard_map/pallas_call | solution.py:90
  137.7 22.1 %all_to_all.33 = f16[16,80,256]{2,1,0:T(8,128)(2,1)S(1)} all-to-all(f16[16,80,256]{2,1,0:T(8,128)(2,1)S(1)} %bitcast.48), channel_id=1, replica_groups=mesh['z'=4,'k'=2,'x'=4,'y'=4] {'x','y'}, dimensions={0} | all-to-all | bytes 1310720 | tf_op jit(solution)/shard_map/all_to_all | solution.py:300
  160.3 1.2 collective-permute-done.18
  162.2 6.3 %collective-permute-done.20 = f16[2,64,256]{2,1,0:T(8,128)(2,1)S(1)} collective-permute-done((f16[2,64,256]{2,1,0:T(8,128)(2,1)S(1)}, f16[2,64,256]{2,1,0:T(8,128)(2,1)S(1)}, u32[]{:S(2)}, u32[]{:S(2)}) %collective-permute-start.20) | collective-permute-done | bytes 65568 | tf_op jit(solution)/shard_map/ppermute | solution.py:315
  168.8 1.3 collective-permute-done.21
  170.2 4.4 %shard_map.54 = f32[4,4,80,256]{3,2,1,0:T(8,128)S(1)} custom-call(s32[3]{0:T(128)S(1)} %pad_add_fusion.refs_0_, bf16[6,2,2,256,512]{4,3,2,1,0:T(8,128)(2,1)S(1)} %bitcast.47, bf16[6,2,256,512]{3,2,1,0:T(8,128)(2,1)S(1)} %collective-permute-done.2.refs_2_, f32[8,256]{1,0:T(8,128)S(1)} %pad.4.refs_3_, f32[2,2,64,256]{3,2,1,0:T(8,128)S(1)} %get-tuple-element.40.refs_4_, ...), custom_call_target="tpu_custom_call" | custom-call | tf_op jit(solution)/shard_map/pallas_call | solution.py:90
  175.6 8.6 %all-to-all-start.4 = ((f16[16,80,256]{2,1,0:T(8,128)(2,1)}), f16[16,80,256]{2,1,0:T(8,128)(2,1)S(1)}, u32[]{:S(2)}, u32[]{:S(2)}) async-start(f16[16,80,256]{2,1,0:T(8,128)(2,1)} %bitcast.30), calls=%async_computation.4 | async-start | bytes 1310720 | tf_op jit(solution)/shard_map/all_to_all | solution.py:300
  184.3 13.1 %all-to-all-done.4 = f16[16,80,256]{2,1,0:T(8,128)(2,1)S(1)} async-done(((f16[16,80,256]{2,1,0:T(8,128)(2,1)}), f16[16,80,256]{2,1,0:T(8,128)(2,1)S(1)}, u32[]{:S(2)}, u32[]{:S(2)}) %all-to-all-start.4) | async-done | bytes 655392 | tf_op jit(solution)/shard_map/all_to_all | solution.py:300
  197.9 1.2 collective-permute-done.23.other_ref
  199.8 5.2 %all-to-all-start.5 = ((f32[64,8,128]{2,1,0:T(8,128)}), f32[64,8,128]{2,1,0:T(8,128)S(1)}, u32[]{:S(2)}, u32[]{:S(2)}) async-start(f32[64,8,128]{2,1,0:T(8,128)} %shard_map.56), calls=%async_computation.5 | async-start | bytes 524288 | tf_op jit(solution)/shard_map/all_to_all | solution.py:300
  205.7 10.6 %all-to-all-done.5.dots_ref = f32[64,8,128]{2,1,0:T(8,128)S(1)} async-done(((f32[64,8,128]{2,1,0:T(8,128)}), f32[64,8,128]{2,1,0:T(8,128)S(1)}, u32[]{:S(2)}, u32[]{:S(2)}) %all-to-all-start.5) | async-done | bytes 262176 | tf_op jit(solution)/shard_map/all_to_all | solution.py:300
  (91 shorter events, 14.9 us)
Async XLA Ops:
  0.0 25.8 %copy-start = (f32[64,6]{0,1:T(8,128)S(1)}, f32[64,6]{0,1:T(8,128)}, u32[]{:S(2)}) copy-start(f32[64,6]{0,1:T(8,128)} %param.7) | copy-start | bytes 4612
  0.9 0.7 collective-permute-start
  1.5 8.9 %collective-permute-start.1 = (bf16[64,256]{1,0:T(8,128)(2,1)S(1)}, bf16[64,256]{1,0:T(8,128)(2,1)S(1)}, u32[]{:S(2)}, u32[]{:S(2)}) collective-permute-start(bf16[64,256]{1,0:T(8,128)(2,1)S(1)} %collective-permute-done), channel_id=1, source_target_pairs={{0,16},{16,0},{1,17},{17,1},{2,18},{18,2},{3,19},{19,3},{4,20},{20... | collective-permute-start | bytes 98312 | tf_op jit(solution)/shard_map/ppermute | solution.py:324
  6.6 19.2 %copy-start.4 = (s32[256]{0:T(256)S(1)}, s32[256]{0:T(256)}, u32[]{:S(2)}) copy-start(s32[256]{0:T(256)} %param.6) | copy-start | bytes 3076
  10.4 16.4 %collective-permute-start.2 = (bf16[6,2,256,512]{3,2,1,0:T(8,128)(2,1)}, bf16[6,2,256,512]{3,2,1,0:T(8,128)(2,1)S(1)}, u32[]{:S(2)}, u32[]{:S(2)}) collective-permute-start(bf16[6,2,256,512]{3,2,1,0:T(8,128)(2,1)} %slice_bitcast_fusion), channel_id=1, source_target_pairs={{0,16},{16,0},{1,17},{17,1},{2,18},{18,2},{3,19},{19,3},{4,20},{20... | collective-permute-start | bytes 9437192 | tf_op jit(solution)/shard_map/ppermute | solution.py:326
  10.5 11.6 %collective-permute-start.4 = (bf16[2,64,256]{2,1,0:T(8,128)(2,1)S(1)}, bf16[2,64,256]{2,1,0:T(8,128)(2,1)S(1)}, u32[]{:S(2)}, u32[]{:S(2)}) collective-permute-start(bf16[2,64,256]{2,1,0:T(8,128)(2,1)S(1)} %pad_maximum_fusion.6), channel_id=1, source_target_pairs={{0,32},{4,64},{8,96},{12,0},{16,112},{20,16},{24,48},{28,80},{32,3... | collective-permute-start | bytes 196616 | tf_op jit(solution)/shard_map/ppermute | solution.py:315
  12.5 9.6 %collective-permute-start.3 = (bf16[2,64,256]{2,1,0:T(8,128)(2,1)S(1)}, bf16[2,64,256]{2,1,0:T(8,128)(2,1)S(1)}, u32[]{:S(2)}, u32[]{:S(2)}) collective-permute-start(bf16[2,64,256]{2,1,0:T(8,128)(2,1)S(1)} %pad_maximum_fusion.6), channel_id=1, source_target_pairs={{0,0},{4,32},{8,64},{12,96},{16,80},{20,112},{24,16},{28,48},{32,4... | collective-permute-start | bytes 196616 | tf_op jit(solution)/shard_map/ppermute | solution.py:315
  22.1 4.7 %collective-permute-start.5 = (bf16[2,2,64,256]{3,2,1,0:T(8,128)(2,1)S(1)}, bf16[2,2,64,256]{3,2,1,0:T(8,128)(2,1)S(1)}, u32[]{:S(2)}, u32[]{:S(2)}) collective-permute-start(bf16[2,2,64,256]{3,2,1,0:T(8,128)(2,1)S(1)} %pad_maximum_fusion.refs_4_), channel_id=1, source_target_pairs={{0,16},{16,0},{1,17},{17,1},{2,18},{18,2},{3,19},{19,3},{4,20},{20... | collective-permute-start | bytes 393224 | tf_op jit(solution)/shard_map/ppermute | solution.py:317
  26.0 36.2 %slice-start = ((s8[6291456]{0:T(1024)(128)(4,1)}), s8[4194304]{0:T(1024)(128)(4,1)S(1)}, s32[]{:S(2)}) async-start(s8[6291456]{0:T(1024)(128)(4,1)} %bitcast.42), calls=%async_computation.6 | async-start | bytes 8388608
  26.2 36.0 %slice-start.1 = ((s8[6291456]{0:T(1024)(128)(4,1)}), s8[2097152]{0:T(1024)(128)(4,1)S(1)}, s32[]{:S(2)}) async-start(s8[6291456]{0:T(1024)(128)(4,1)} %bitcast.42), calls=%async_computation.7 | async-start | bytes 4194304
  52.0 1.3 collective-permute-start.6
  53.3 7.4 %collective-permute-start.8 = (f16[2,64,256]{2,1,0:T(8,128)(2,1)S(1)}, f16[2,64,256]{2,1,0:T(8,128)(2,1)S(1)}, u32[]{:S(2)}, u32[]{:S(2)}) collective-permute-start(f16[2,64,256]{2,1,0:T(8,128)(2,1)S(1)} %pad_maximum_fusion.7), channel_id=1, source_target_pairs={{0,32},{4,64},{8,96},{12,0},{16,112},{20,16},{24,48},{28,80},{32,3... | collective-permute-start | bytes 196616 | tf_op jit(solution)/shard_map/ppermute | solution.py:315
  53.4 7.3 %collective-permute-start.7 = (f16[2,64,256]{2,1,0:T(8,128)(2,1)S(1)}, f16[2,64,256]{2,1,0:T(8,128)(2,1)S(1)}, u32[]{:S(2)}, u32[]{:S(2)}) collective-permute-start(f16[2,64,256]{2,1,0:T(8,128)(2,1)S(1)} %pad_maximum_fusion.7), channel_id=1, source_target_pairs={{0,0},{4,32},{8,64},{12,96},{16,80},{20,112},{24,16},{28,48},{32,4... | collective-permute-start | bytes 196616 | tf_op jit(solution)/shard_map/ppermute | solution.py:315
  60.7 1.4 collective-permute-start.9
  86.7 1.3 collective-permute-start.10
  88.0 7.1 %collective-permute-start.12 = (f16[2,64,256]{2,1,0:T(8,128)(2,1)S(1)}, f16[2,64,256]{2,1,0:T(8,128)(2,1)S(1)}, u32[]{:S(2)}, u32[]{:S(2)}) collective-permute-start(f16[2,64,256]{2,1,0:T(8,128)(2,1)S(1)} %pad_maximum_fusion.8), channel_id=1, source_target_pairs={{0,32},{4,64},{8,96},{12,0},{16,112},{20,16},{24,48},{28,80},{32,3... | collective-permute-start | bytes 196616 | tf_op jit(solution)/shard_map/ppermute | solution.py:315
  89.5 5.5 %collective-permute-start.11 = (f16[2,64,256]{2,1,0:T(8,128)(2,1)S(1)}, f16[2,64,256]{2,1,0:T(8,128)(2,1)S(1)}, u32[]{:S(2)}, u32[]{:S(2)}) collective-permute-start(f16[2,64,256]{2,1,0:T(8,128)(2,1)S(1)} %pad_maximum_fusion.8), channel_id=1, source_target_pairs={{0,0},{4,32},{8,64},{12,96},{16,80},{20,112},{24,16},{28,48},{32,4... | collective-permute-start | bytes 196616 | tf_op jit(solution)/shard_map/ppermute | solution.py:315
  95.1 1.8 collective-permute-start.13
  122.2 1.3 collective-permute-start.14
  123.5 6.5 %collective-permute-start.16 = (f16[2,64,256]{2,1,0:T(8,128)(2,1)S(1)}, f16[2,64,256]{2,1,0:T(8,128)(2,1)S(1)}, u32[]{:S(2)}, u32[]{:S(2)}) collective-permute-start(f16[2,64,256]{2,1,0:T(8,128)(2,1)S(1)} %pad_maximum_fusion.9), channel_id=1, source_target_pairs={{0,32},{4,64},{8,96},{12,0},{16,112},{20,16},{24,48},{28,80},{32,3... | collective-permute-start | bytes 196616 | tf_op jit(solution)/shard_map/ppermute | solution.py:315
  125.0 5.0 %collective-permute-start.15 = (f16[2,64,256]{2,1,0:T(8,128)(2,1)S(1)}, f16[2,64,256]{2,1,0:T(8,128)(2,1)S(1)}, u32[]{:S(2)}, u32[]{:S(2)}) collective-permute-start(f16[2,64,256]{2,1,0:T(8,128)(2,1)S(1)} %pad_maximum_fusion.9), channel_id=1, source_target_pairs={{0,0},{4,32},{8,64},{12,96},{16,80},{20,112},{24,16},{28,48},{32,4... | collective-permute-start | bytes 196616 | tf_op jit(solution)/shard_map/ppermute | solution.py:315
  130.1 3.2 %collective-permute-start.17 = (f16[2,2,64,256]{3,2,1,0:T(8,128)(2,1)S(1)}, f16[2,2,64,256]{3,2,1,0:T(8,128)(2,1)S(1)}, u32[]{:S(2)}, u32[]{:S(2)}) collective-permute-start(f16[2,2,64,256]{3,2,1,0:T(8,128)(2,1)S(1)} %get-tuple-element.35), channel_id=1, source_target_pairs={{0,16},{16,0},{1,17},{17,1},{2,18},{18,2},{3,19},{19,3},{4,20},{20... | collective-permute-start | bytes 393224 | tf_op jit(solution)/shard_map/ppermute | solution.py:317
  160.1 1.3 collective-permute-start.18
  160.3 9.9 %copy-start.2 = (f16[1,64,256]{2,1,0:T(8,128)(2,1)}, f16[1,64,256]{2,1,0:T(8,128)(2,1)S(1)}, u32[]{:S(2)}) copy-start(f16[1,64,256]{2,1,0:T(8,128)(2,1)S(1)} %convert_bitcast_fusion) | copy-start | bytes 98308
  161.5 7.0 %collective-permute-start.20 = (f16[2,64,256]{2,1,0:T(8,128)(2,1)S(1)}, f16[2,64,256]{2,1,0:T(8,128)(2,1)S(1)}, u32[]{:S(2)}, u32[]{:S(2)}) collective-permute-start(f16[2,64,256]{2,1,0:T(8,128)(2,1)S(1)} %pad_maximum_fusion.10), channel_id=1, source_target_pairs={{0,32},{4,64},{8,96},{12,0},{16,112},{20,16},{24,48},{28,80},{32,3... | collective-permute-start | bytes 196616 | tf_op jit(solution)/shard_map/ppermute | solution.py:315
  161.5 6.9 %collective-permute-start.19 = (f16[2,64,256]{2,1,0:T(8,128)(2,1)S(1)}, f16[2,64,256]{2,1,0:T(8,128)(2,1)S(1)}, u32[]{:S(2)}, u32[]{:S(2)}) collective-permute-start(f16[2,64,256]{2,1,0:T(8,128)(2,1)S(1)} %pad_maximum_fusion.10), channel_id=1, source_target_pairs={{0,0},{4,32},{8,64},{12,96},{16,80},{20,112},{24,16},{28,48},{32,4... | collective-permute-start | bytes 196616 | tf_op jit(solution)/shard_map/ppermute | solution.py:315
  168.5 1.6 collective-permute-start.21
  175.6 21.9 %all-to-all-start.4 = ((f16[16,80,256]{2,1,0:T(8,128)(2,1)}), f16[16,80,256]{2,1,0:T(8,128)(2,1)S(1)}, u32[]{:S(2)}, u32[]{:S(2)}) async-start(f16[16,80,256]{2,1,0:T(8,128)(2,1)} %bitcast.30), calls=%async_computation.4 | async-start | bytes 1310720 | tf_op jit(solution)/shard_map/all_to_all | solution.py:300
  197.6 18.7 %copy-start.1 = (f32[64,256]{1,0:T(8,128)S(1)}, f32[64,256]{1,0:T(8,128)}, u32[]{:S(2)}) copy-start(f32[64,256]{1,0:T(8,128)} %p_ref.1) | copy-start | bytes 196612
  197.9 1.2 collective-permute-start.23
  199.8 16.5 %all-to-all-start.5 = ((f32[64,8,128]{2,1,0:T(8,128)}), f32[64,8,128]{2,1,0:T(8,128)S(1)}, u32[]{:S(2)}, u32[]{:S(2)}) async-start(f32[64,8,128]{2,1,0:T(8,128)} %shard_map.56), calls=%async_computation.5 | async-start | bytes 524288 | tf_op jit(solution)/shard_map/all_to_all | solution.py:300
  205.0 0.7 collective-permute-start.22
  (1 other events, 9.6 us)

commit v9 on v8

--- a/solution.py
+++ b/solution.py
@@ -38,7 +38,7 @@
 SWAP = [(0, 1), (1, 0)]
 SPREAD = [
     [
-        ((z * NK + k) * NX + x, (((x + 2 * k + t) % NZ) * NK + k) * NX + z)
+        ((z * NK + k) * NX + x, (((x + k + 2 - 2 * t) % NZ) * NK + k) * NX + z)
         for z in range(NZ)
         for k in range(NK)
         for x in range(NX)
@@ -118,7 +118,7 @@
     for ref, k in ((own_refs[-1], core), (other_refs[-1], 1 - core)):
         for i in range(NX):
             t, o = divmod(i, 2)
-            x, half = (place + 2 * NZ - 2 * k - t) % NX, (k + o + side) % 2
+            x, half = (place + 2 * NZ - k - 2 + 2 * t) % NX, (k + o + side) % 2
             value = ref[t, o]
             rows = pl.ds(pl.multiple_of(half * HALF + x * SUB, SUB), SUB)
             high = value.astype(jnp.bfloat16)
@@ -336,6 +336,7 @@
         fields.append(spread(both))
         if j == KRYLOV:
             inner = jnp.stack(pieces).astype(WIRE)
+            fields[-1], inner = lax.optimization_barrier((fields[-1], inner))
         partial = apply_rates(at, kept, got, weights, fields, False)
         met = reduce(partial)
         if j < KRYLOV:

time: 218 us -> 216 us (level)
  waiting for transfers between devices: 66 us -> 38.1 us
  starting transfers between devices: 36.3 us -> 51 us
  blocking collectives: 83.8 us -> 96 us
    ppermute x10, starting transfers between devices: 8.42 us -> 37.2 us  [spread(): own = [lax.ppermute(both, ('z', 'k', 'x'), pairs) for pairs in SPREAD]]
    ppermute x10, waiting for transfers between devices: 31.1 us -> 15.7 us  [spread(): own = [lax.ppermute(both, ('z', 'k', 'x'), pairs) for pairs in SPREAD]]
    all_to_all x2 -> x1, waiting for transfers between devices: 23.7 us -> 10.6 us  [body(): exchange = lambda v, axes: lax.all_to_all(v, axes, 0, 0, tiled=True)]
    all_to_all x4 -> x5, blocking collectives: 83.8 us -> 96 us  [body(): exchange = lambda v, axes: lax.all_to_all(v, axes, 0, 0, tiled=True)]
    all_to_all x2 -> x1, starting transfers between devices: 13.8 us -> 5.69 us  [body(): exchange = lambda v, axes: lax.all_to_all(v, axes, 0, 0, tiled=True)]
    ppermute x5, starting transfers between devices: 7.1 us -> 1.15 us  [spread(): other = lax.ppermute(own, 'k', SWAP)]
  transfers between devices with their start and end apart: 26 -> 25, of which waited for: 17 -> 16; matrix products, arithmetic and copies ran while one was open for 2% -> 2% of each run, Pallas kernels for 0% -> 0%
where the time goes in v9:
time: 216 us; the launch traced here: 215 us
  blocking collectives  96 us (44%)
  starting transfers between devices  51 us (24%)
  waiting for transfers between devices  38.1 us (18%)
  Pallas kernels  22.8 us (11%)
  local copies, waits for them, and re-layouts  3.83 us (2%)
  other arithmetic  2.45 us (1%)
    all_to_all x5, blocking collectives, body(): exchange = lambda v, axes: lax.all_to_all(v, axes, 0, 0, tiled=True)  96 us
    ppermute x10, starting transfers between devices, spread(): own = [lax.ppermute(both, ('z', 'k', 'x'), pairs) for pairs in SPREAD]  37.2 us
    pallas_call x12, Pallas kernels, call(): pl.pallas_call(kernel, out_shape=outs, in_specs=specs, out_specs=jax.tree...  22.8 us
    ppermute x10, waiting for transfers between devices, spread(): own = [lax.ppermute(both, ('z', 'k', 'x'), pairs) for pairs in SPREAD]  15.7 us
    all_to_all x1, waiting for transfers between devices, body(): exchange = lambda v, axes: lax.all_to_all(v, axes, 0, 0, tiled=True)  10.6 us
    ppermute x5, waiting for transfers between devices, spread(): other = lax.ppermute(own, 'k', SWAP)  5.95 us
    all_to_all x1, starting transfers between devices, body(): exchange = lambda v, axes: lax.all_to_all(v, axes, 0, 0, tiled=True)  5.69 us
    ppermute x5, starting transfers between devices, body(): both = jnp.stack([piece, lax.ppermute(piece, 'k', SWAP)])  5.44 us
  transfers between devices with their start and end apart: 25, of which 16 were waited for; matrix products, arithmetic and copies ran while one was open for 2% of the time, Pallas kernels for 0%

profile of v9, /device:TPU:0, one launch (start us, length us, event | category | flops | bytes accessed | tf_op | source)
XLA Modules:
  0.0 214.9 jit_solution(6852057318600694333)
XLA Ops:
  1.5 5.1 %collective-permute-start.1 = (bf16[64,256]{1,0:T(8,128)(2,1)S(1)}, bf16[64,256]{1,0:T(8,128)(2,1)S(1)}, u32[]{:S(2)}, u32[]{:S(2)}) collective-permute-start(bf16[64,256]{1,0:T(8,128)(2,1)S(1)} %collective-permute-done), channel_id=1, source_target_pairs={{0,16},{16,0},{1,17},{17,1},{2,18},{18,2},{3,19},{19,3},{4,20},{20... | collective-permute-start | bytes 98312 | tf_op jit(solution)/shard_map/ppermute | solution.py:324
  6.6 3.7 %slice_bitcast_fusion = bf16[6,2,256,512]{3,2,1,0:T(8,128)(2,1)} fusion(bf16[6,2,2,256,512]{4,3,2,1,0:T(8,128)(2,1)} %bitcast.40), kind=kLoop, calls=%fused_computation | loop fusion | bytes 6291456 | tf_op jit(solution)/shard_map/squeeze | solution.py:303
  11.2 11.8 %collective-permute-start.3 = (bf16[2,64,256]{2,1,0:T(8,128)(2,1)S(1)}, bf16[2,64,256]{2,1,0:T(8,128)(2,1)S(1)}, u32[]{:S(2)}, u32[]{:S(2)}) collective-permute-start(bf16[2,64,256]{2,1,0:T(8,128)(2,1)S(1)} %pad_maximum_fusion.6), channel_id=1, source_target_pairs={{0,64},{4,96},{8,0},{12,32},{16,112},{20,16},{24,48},{28,80},{32,6... | collective-permute-start | bytes 196616 | tf_op jit(solution)/shard_map/ppermute | solution.py:315
  23.0 2.0 collective-permute-done.3
  26.4 3.4 %shard_map.46 = f32[4,4,64,256]{3,2,1,0:T(8,128)S(1)} custom-call(s32[3]{0:T(128)S(1)} %pad_add_fusion.refs_0_, bf16[6,2,2,256,512]{4,3,2,1,0:T(8,128)(2,1)} %bitcast.41, bf16[6,2,256,512]{3,2,1,0:T(8,128)(2,1)S(1)} %collective-permute-done.2.refs_2_, f32[8,256]{1,0:T(8,128)S(1)} %pad.4.refs_3_, bf16[2,2,64,256]{3,2,1,0:T(8,128)(2,1)S(1)} %pad_maximum_fusion.refs_4_, ...), custom_call_target="tpu_custom_call" | custom-call | tf_op jit(solution)/shard_map/pallas_call | solution.py:90
  30.0 20.7 %all_to_all.30 = f16[16,64,256]{2,1,0:T(8,128)(2,1)S(1)} all-to-all(f16[16,64,256]{2,1,0:T(8,128)(2,1)S(1)} %bitcast.52), channel_id=1, replica_groups=mesh['z'=4,'k'=2,'x'=4,'y'=4] {'x','y'}, dimensions={0} | all-to-all | bytes 1048576 | tf_op jit(solution)/shard_map/all_to_all | solution.py:300
  50.9 1.2 collective-permute-done.6
  52.8 5.4 %collective-permute-start.7 = (f16[2,64,256]{2,1,0:T(8,128)(2,1)S(1)}, f16[2,64,256]{2,1,0:T(8,128)(2,1)S(1)}, u32[]{:S(2)}, u32[]{:S(2)}) collective-permute-start(f16[2,64,256]{2,1,0:T(8,128)(2,1)S(1)} %pad_maximum_fusion.7), channel_id=1, source_target_pairs={{0,64},{4,96},{8,0},{12,32},{16,112},{20,16},{24,48},{28,80},{32,6... | collective-permute-start | bytes 196616 | tf_op jit(solution)/shard_map/ppermute | solution.py:315
  58.3 3.1 %collective-permute-done.7 = f16[2,64,256]{2,1,0:T(8,128)(2,1)S(1)} collective-permute-done((f16[2,64,256]{2,1,0:T(8,128)(2,1)S(1)}, f16[2,64,256]{2,1,0:T(8,128)(2,1)S(1)}, u32[]{:S(2)}, u32[]{:S(2)}) %collective-permute-start.7) | collective-permute-done | bytes 65568 | tf_op jit(solution)/shard_map/ppermute | solution.py:315
  62.9 4.1 %shard_map.48 = f32[4,4,72,256]{3,2,1,0:T(8,128)S(1)} custom-call(s32[3]{0:T(128)S(1)} %pad_add_fusion.refs_0_, bf16[6,2,2,256,512]{4,3,2,1,0:T(8,128)(2,1)S(1)} %bitcast.44, bf16[6,2,256,512]{3,2,1,0:T(8,128)(2,1)S(1)} %collective-permute-done.2.refs_2_, f32[8,256]{1,0:T(8,128)S(1)} %pad.4.refs_3_, f32[2,2,64,256]{3,2,1,0:T(8,128)S(1)} %get-tuple-element.46.refs_4_, ...), custom_call_target="tpu_custom_call" | custom-call | tf_op jit(solution)/shard_map/pallas_call | solution.py:90
  67.1 18.3 %all_to_all.31 = f16[16,72,256]{2,1,0:T(8,128)(2,1)S(1)} all-to-all(f16[16,72,256]{2,1,0:T(8,128)(2,1)S(1)} %bitcast.50), channel_id=1, replica_groups=mesh['z'=4,'k'=2,'x'=4,'y'=4] {'x','y'}, dimensions={0} | all-to-all | bytes 1179648 | tf_op jit(solution)/shard_map/all_to_all | solution.py:300
  85.8 1.2 collective-permute-done.10
  87.7 5.5 %collective-permute-start.11 = (f16[2,64,256]{2,1,0:T(8,128)(2,1)S(1)}, f16[2,64,256]{2,1,0:T(8,128)(2,1)S(1)}, u32[]{:S(2)}, u32[]{:S(2)}) collective-permute-start(f16[2,64,256]{2,1,0:T(8,128)(2,1)S(1)} %pad_maximum_fusion.8), channel_id=1, source_target_pairs={{0,64},{4,96},{8,0},{12,32},{16,112},{20,16},{24,48},{28,80},{32,6... | collective-permute-start | bytes 196616 | tf_op jit(solution)/shard_map/ppermute | solution.py:315
  93.2 3.9 %collective-permute-done.11 = f16[2,64,256]{2,1,0:T(8,128)(2,1)S(1)} collective-permute-done((f16[2,64,256]{2,1,0:T(8,128)(2,1)S(1)}, f16[2,64,256]{2,1,0:T(8,128)(2,1)S(1)}, u32[]{:S(2)}, u32[]{:S(2)}) %collective-permute-start.11) | collective-permute-done | bytes 65568 | tf_op jit(solution)/shard_map/ppermute | solution.py:315
  97.4 1.3 collective-permute-done.13
  98.7 4.2 %shard_map.50 = f32[4,4,72,256]{3,2,1,0:T(8,128)S(1)} custom-call(s32[3]{0:T(128)S(1)} %pad_add_fusion.refs_0_, bf16[6,2,2,256,512]{4,3,2,1,0:T(8,128)(2,1)S(1)} %bitcast.45, bf16[6,2,256,512]{3,2,1,0:T(8,128)(2,1)S(1)} %collective-permute-done.2.refs_2_, f32[8,256]{1,0:T(8,128)S(1)} %pad.4.refs_3_, f32[2,2,64,256]{3,2,1,0:T(8,128)S(1)} %get-tuple-element.46.refs_4_, ...), custom_call_target="tpu_custom_call" | custom-call | tf_op jit(solution)/shard_map/pallas_call | solution.py:90
  103.1 18.6 %all_to_all.32 = f16[16,72,256]{2,1,0:T(8,128)(2,1)S(1)} all-to-all(f16[16,72,256]{2,1,0:T(8,128)(2,1)S(1)} %bitcast.51), channel_id=1, replica_groups=mesh['z'=4,'k'=2,'x'=4,'y'=4] {'x','y'}, dimensions={0} | all-to-all | bytes 1179648 | tf_op jit(solution)/shard_map/all_to_all | solution.py:300
  122.1 1.2 collective-permute-done.14
  124.0 5.5 %collective-permute-start.15 = (f16[2,64,256]{2,1,0:T(8,128)(2,1)S(1)}, f16[2,64,256]{2,1,0:T(8,128)(2,1)S(1)}, u32[]{:S(2)}, u32[]{:S(2)}) collective-permute-start(f16[2,64,256]{2,1,0:T(8,128)(2,1)S(1)} %pad_maximum_fusion.9), channel_id=1, source_target_pairs={{0,64},{4,96},{8,0},{12,32},{16,112},{20,16},{24,48},{28,80},{32,6... | collective-permute-start | bytes 196616 | tf_op jit(solution)/shard_map/ppermute | solution.py:315
  129.5 3.5 %collective-permute-done.15 = f16[2,64,256]{2,1,0:T(8,128)(2,1)S(1)} collective-permute-done((f16[2,64,256]{2,1,0:T(8,128)(2,1)S(1)}, f16[2,64,256]{2,1,0:T(8,128)(2,1)S(1)}, u32[]{:S(2)}, u32[]{:S(2)}) %collective-permute-start.15) | collective-permute-done | bytes 65568 | tf_op jit(solution)/shard_map/ppermute | solution.py:315
  133.2 1.2 collective-permute-done.17
  134.5 4.4 %shard_map.52 = f32[4,4,80,256]{3,2,1,0:T(8,128)S(1)} custom-call(s32[3]{0:T(128)S(1)} %pad_add_fusion.refs_0_, bf16[6,2,2,256,512]{4,3,2,1,0:T(8,128)(2,1)S(1)} %bitcast.46, bf16[6,2,256,512]{3,2,1,0:T(8,128)(2,1)S(1)} %collective-permute-done.2.refs_2_, f32[8,256]{1,0:T(8,128)S(1)} %pad.4.refs_3_, f32[2,2,64,256]{3,2,1,0:T(8,128)S(1)} %get-tuple-element.46.refs_4_, ...), custom_call_target="tpu_custom_call" | custom-call | tf_op jit(solution)/shard_map/pallas_call | solution.py:90
  139.0 19.0 %all_to_all.33 = f16[16,80,256]{2,1,0:T(8,128)(2,1)S(1)} all-to-all(f16[16,80,256]{2,1,0:T(8,128)(2,1)S(1)} %bitcast.48), channel_id=1, replica_groups=mesh['z'=4,'k'=2,'x'=4,'y'=4] {'x','y'}, dimensions={0} | all-to-all | bytes 1310720 | tf_op jit(solution)/shard_map/all_to_all | solution.py:300
  158.4 1.2 collective-permute-done.18
  160.3 5.6 %collective-permute-start.19 = (f16[2,64,256]{2,1,0:T(8,128)(2,1)S(1)}, f16[2,64,256]{2,1,0:T(8,128)(2,1)S(1)}, u32[]{:S(2)}, u32[]{:S(2)}) collective-permute-start(f16[2,64,256]{2,1,0:T(8,128)(2,1)S(1)} %pad_maximum_fusion.10), channel_id=1, source_target_pairs={{0,64},{4,96},{8,0},{12,32},{16,112},{20,16},{24,48},{28,80},{32,6... | collective-permute-start | bytes 196616 | tf_op jit(solution)/shard_map/ppermute | solution.py:315
  165.9 3.2 %collective-permute-done.19 = f16[2,64,256]{2,1,0:T(8,128)(2,1)S(1)} collective-permute-done((f16[2,64,256]{2,1,0:T(8,128)(2,1)S(1)}, f16[2,64,256]{2,1,0:T(8,128)(2,1)S(1)}, u32[]{:S(2)}, u32[]{:S(2)}) %collective-permute-start.19) | collective-permute-done | bytes 65568 | tf_op jit(solution)/shard_map/ppermute | solution.py:315
  169.5 1.3 collective-permute-done.21
  170.8 4.4 %shard_map.54 = f32[4,4,80,256]{3,2,1,0:T(8,128)S(1)} custom-call(s32[3]{0:T(128)S(1)} %pad_add_fusion.refs_0_, bf16[6,2,2,256,512]{4,3,2,1,0:T(8,128)(2,1)S(1)} %bitcast.47, bf16[6,2,256,512]{3,2,1,0:T(8,128)(2,1)S(1)} %collective-permute-done.2.refs_2_, f32[8,256]{1,0:T(8,128)S(1)} %pad.4.refs_3_, f32[2,2,64,256]{3,2,1,0:T(8,128)S(1)} %get-tuple-element.46.refs_4_, ...), custom_call_target="tpu_custom_call" | custom-call | tf_op jit(solution)/shard_map/pallas_call | solution.py:90
  175.4 19.4 %all_to_all.34 = f16[16,80,256]{2,1,0:T(8,128)(2,1)S(1)} all-to-all(f16[16,80,256]{2,1,0:T(8,128)(2,1)S(1)} %bitcast.49), channel_id=1, replica_groups=mesh['z'=4,'k'=2,'x'=4,'y'=4] {'x','y'}, dimensions={0} | all-to-all | bytes 1310720 | tf_op jit(solution)/shard_map/all_to_all | solution.py:300
  195.2 1.2 collective-permute-done.23.other_ref
  197.1 5.7 %all-to-all-start.5 = ((f32[64,8,128]{2,1,0:T(8,128)}), f32[64,8,128]{2,1,0:T(8,128)S(1)}, u32[]{:S(2)}, u32[]{:S(2)}) async-start(f32[64,8,128]{2,1,0:T(8,128)} %shard_map.56), calls=%async_computation.5 | async-start | bytes 524288 | tf_op jit(solution)/shard_map/all_to_all | solution.py:300
  203.5 10.6 %all-to-all-done.5.dots_ref = f32[64,8,128]{2,1,0:T(8,128)S(1)} async-done(((f32[64,8,128]{2,1,0:T(8,128)}), f32[64,8,128]{2,1,0:T(8,128)S(1)}, u32[]{:S(2)}, u32[]{:S(2)}) %all-to-all-start.5) | async-done | bytes 262176 | tf_op jit(solution)/shard_map/all_to_all | solution.py:300
  (86 shorter events, 13.4 us)
Async XLA Ops:
  0.0 25.1 %copy-start = (f32[64,6]{0,1:T(8,128)S(1)}, f32[64,6]{0,1:T(8,128)}, u32[]{:S(2)}) copy-start(f32[64,6]{0,1:T(8,128)} %param.7) | copy-start | bytes 4612
  0.9 0.7 collective-permute-start
  1.5 8.8 %collective-permute-start.1 = (bf16[64,256]{1,0:T(8,128)(2,1)S(1)}, bf16[64,256]{1,0:T(8,128)(2,1)S(1)}, u32[]{:S(2)}, u32[]{:S(2)}) collective-permute-start(bf16[64,256]{1,0:T(8,128)(2,1)S(1)} %collective-permute-done), channel_id=1, source_target_pairs={{0,16},{16,0},{1,17},{17,1},{2,18},{18,2},{3,19},{19,3},{4,20},{20... | collective-permute-start | bytes 98312 | tf_op jit(solution)/shard_map/ppermute | solution.py:324
  6.6 18.5 %copy-start.2 = (s32[256]{0:T(256)S(1)}, s32[256]{0:T(256)}, u32[]{:S(2)}) copy-start(s32[256]{0:T(256)} %param.6) | copy-start | bytes 3076
  10.4 16.1 %collective-permute-start.2 = (bf16[6,2,256,512]{3,2,1,0:T(8,128)(2,1)}, bf16[6,2,256,512]{3,2,1,0:T(8,128)(2,1)S(1)}, u32[]{:S(2)}, u32[]{:S(2)}) collective-permute-start(bf16[6,2,256,512]{3,2,1,0:T(8,128)(2,1)} %slice_bitcast_fusion), channel_id=1, source_target_pairs={{0,16},{16,0},{1,17},{17,1},{2,18},{18,2},{3,19},{19,3},{4,20},{20... | collective-permute-start | bytes 9437192 | tf_op jit(solution)/shard_map/ppermute | solution.py:326
  10.5 12.5 %collective-permute-start.4 = (bf16[2,64,256]{2,1,0:T(8,128)(2,1)S(1)}, bf16[2,64,256]{2,1,0:T(8,128)(2,1)S(1)}, u32[]{:S(2)}, u32[]{:S(2)}) collective-permute-start(bf16[2,64,256]{2,1,0:T(8,128)(2,1)S(1)} %pad_maximum_fusion.6), channel_id=1, source_target_pairs={{0,0},{4,32},{8,64},{12,96},{16,48},{20,80},{24,112},{28,16},{32,4... | collective-permute-start | bytes 196616 | tf_op jit(solution)/shard_map/ppermute | solution.py:315
  11.2 13.8 %collective-permute-start.3 = (bf16[2,64,256]{2,1,0:T(8,128)(2,1)S(1)}, bf16[2,64,256]{2,1,0:T(8,128)(2,1)S(1)}, u32[]{:S(2)}, u32[]{:S(2)}) collective-permute-start(bf16[2,64,256]{2,1,0:T(8,128)(2,1)S(1)} %pad_maximum_fusion.6), channel_id=1, source_target_pairs={{0,64},{4,96},{8,0},{12,32},{16,112},{20,16},{24,48},{28,80},{32,6... | collective-permute-start | bytes 196616 | tf_op jit(solution)/shard_map/ppermute | solution.py:315
  25.0 1.4 collective-permute-start.5
  25.3 37.5 %slice-start = ((s8[6291456]{0:T(1024)(128)(4,1)}), s8[4194304]{0:T(1024)(128)(4,1)S(1)}, s32[]{:S(2)}) async-start(s8[6291456]{0:T(1024)(128)(4,1)} %bitcast.42), calls=%async_computation.6 | async-start | bytes 8388608
  25.5 37.4 %slice-start.1 = ((s8[6291456]{0:T(1024)(128)(4,1)}), s8[2097152]{0:T(1024)(128)(4,1)S(1)}, s32[]{:S(2)}) async-start(s8[6291456]{0:T(1024)(128)(4,1)} %bitcast.42), calls=%async_computation.7 | async-start | bytes 4194304
  50.8 1.3 collective-permute-start.6
  52.2 6.1 %collective-permute-start.8 = (f16[2,64,256]{2,1,0:T(8,128)(2,1)S(1)}, f16[2,64,256]{2,1,0:T(8,128)(2,1)S(1)}, u32[]{:S(2)}, u32[]{:S(2)}) collective-permute-start(f16[2,64,256]{2,1,0:T(8,128)(2,1)S(1)} %pad_maximum_fusion.7), channel_id=1, source_target_pairs={{0,0},{4,32},{8,64},{12,96},{16,48},{20,80},{24,112},{28,16},{32,4... | collective-permute-start | bytes 196616 | tf_op jit(solution)/shard_map/ppermute | solution.py:315
  52.8 8.5 %collective-permute-start.7 = (f16[2,64,256]{2,1,0:T(8,128)(2,1)S(1)}, f16[2,64,256]{2,1,0:T(8,128)(2,1)S(1)}, u32[]{:S(2)}, u32[]{:S(2)}) collective-permute-start(f16[2,64,256]{2,1,0:T(8,128)(2,1)S(1)} %pad_maximum_fusion.7), channel_id=1, source_target_pairs={{0,64},{4,96},{8,0},{12,32},{16,112},{20,16},{24,48},{28,80},{32,6... | collective-permute-start | bytes 196616 | tf_op jit(solution)/shard_map/ppermute | solution.py:315
  61.4 1.4 collective-permute-start.9
  85.7 1.3 collective-permute-start.10
  87.0 6.2 %collective-permute-start.12 = (f16[2,64,256]{2,1,0:T(8,128)(2,1)S(1)}, f16[2,64,256]{2,1,0:T(8,128)(2,1)S(1)}, u32[]{:S(2)}, u32[]{:S(2)}) collective-permute-start(f16[2,64,256]{2,1,0:T(8,128)(2,1)S(1)} %pad_maximum_fusion.8), channel_id=1, source_target_pairs={{0,0},{4,32},{8,64},{12,96},{16,48},{20,80},{24,112},{28,16},{32,4... | collective-permute-start | bytes 196616 | tf_op jit(solution)/shard_map/ppermute | solution.py:315
  87.7 9.4 %collective-permute-start.11 = (f16[2,64,256]{2,1,0:T(8,128)(2,1)S(1)}, f16[2,64,256]{2,1,0:T(8,128)(2,1)S(1)}, u32[]{:S(2)}, u32[]{:S(2)}) collective-permute-start(f16[2,64,256]{2,1,0:T(8,128)(2,1)S(1)} %pad_maximum_fusion.8), channel_id=1, source_target_pairs={{0,64},{4,96},{8,0},{12,32},{16,112},{20,16},{24,48},{28,80},{32,6... | collective-permute-start | bytes 196616 | tf_op jit(solution)/shard_map/ppermute | solution.py:315
  97.1 1.6 collective-permute-start.13
  122.0 1.3 collective-permute-start.14
  123.3 6.2 %collective-permute-start.16 = (f16[2,64,256]{2,1,0:T(8,128)(2,1)S(1)}, f16[2,64,256]{2,1,0:T(8,128)(2,1)S(1)}, u32[]{:S(2)}, u32[]{:S(2)}) collective-permute-start(f16[2,64,256]{2,1,0:T(8,128)(2,1)S(1)} %pad_maximum_fusion.9), channel_id=1, source_target_pairs={{0,0},{4,32},{8,64},{12,96},{16,48},{20,80},{24,112},{28,16},{32,4... | collective-permute-start | bytes 196616 | tf_op jit(solution)/shard_map/ppermute | solution.py:315
  124.0 9.0 %collective-permute-start.15 = (f16[2,64,256]{2,1,0:T(8,128)(2,1)S(1)}, f16[2,64,256]{2,1,0:T(8,128)(2,1)S(1)}, u32[]{:S(2)}, u32[]{:S(2)}) collective-permute-start(f16[2,64,256]{2,1,0:T(8,128)(2,1)S(1)} %pad_maximum_fusion.9), channel_id=1, source_target_pairs={{0,64},{4,96},{8,0},{12,32},{16,112},{20,16},{24,48},{28,80},{32,6... | collective-permute-start | bytes 196616 | tf_op jit(solution)/shard_map/ppermute | solution.py:315
  133.0 1.4 collective-permute-start.17
  158.3 1.3 collective-permute-start.18
  159.6 6.3 %collective-permute-start.20 = (f16[2,64,256]{2,1,0:T(8,128)(2,1)S(1)}, f16[2,64,256]{2,1,0:T(8,128)(2,1)S(1)}, u32[]{:S(2)}, u32[]{:S(2)}) collective-permute-start(f16[2,64,256]{2,1,0:T(8,128)(2,1)S(1)} %pad_maximum_fusion.10), channel_id=1, source_target_pairs={{0,0},{4,32},{8,64},{12,96},{16,48},{20,80},{24,112},{28,16},{32,4... | collective-permute-start | bytes 196616 | tf_op jit(solution)/shard_map/ppermute | solution.py:315
  160.3 8.8 %collective-permute-start.19 = (f16[2,64,256]{2,1,0:T(8,128)(2,1)S(1)}, f16[2,64,256]{2,1,0:T(8,128)(2,1)S(1)}, u32[]{:S(2)}, u32[]{:S(2)}) collective-permute-start(f16[2,64,256]{2,1,0:T(8,128)(2,1)S(1)} %pad_maximum_fusion.10), channel_id=1, source_target_pairs={{0,64},{4,96},{8,0},{12,32},{16,112},{20,16},{24,48},{28,80},{32,6... | collective-permute-start | bytes 196616 | tf_op jit(solution)/shard_map/ppermute | solution.py:315
  169.1 1.6 collective-permute-start.21
  194.9 19.2 %copy-start.1 = (f32[64,256]{1,0:T(8,128)S(1)}, f32[64,256]{1,0:T(8,128)}, u32[]{:S(2)}) copy-start(f32[64,256]{1,0:T(8,128)} %p_ref.1) | copy-start | bytes 196612
  195.1 1.2 collective-permute-start.23
  197.1 17.0 %all-to-all-start.5 = ((f32[64,8,128]{2,1,0:T(8,128)}), f32[64,8,128]{2,1,0:T(8,128)S(1)}, u32[]{:S(2)}, u32[]{:S(2)}) async-start(f32[64,8,128]{2,1,0:T(8,128)} %shard_map.56), calls=%async_computation.5 | async-start | bytes 524288 | tf_op jit(solution)/shard_map/all_to_all | solution.py:300
  202.8 0.7 collective-permute-start.22

commit v10 on v9

--- a/solution.py
+++ b/solution.py
@@ -38,7 +38,7 @@
 SWAP = [(0, 1), (1, 0)]
 SPREAD = [
     [
-        ((z * NK + k) * NX + x, (((x + k + 2 - 2 * t) % NZ) * NK + k) * NX + z)
+        ((z * NK + k) * NX + x, (((x + k + 2 * t) % NZ) * NK + k) * NX + z)
         for z in range(NZ)
         for k in range(NK)
         for x in range(NX)
@@ -118,7 +118,7 @@
     for ref, k in ((own_refs[-1], core), (other_refs[-1], 1 - core)):
         for i in range(NX):
             t, o = divmod(i, 2)
-            x, half = (place + 2 * NZ - k - 2 + 2 * t) % NX, (k + o + side) % 2
+            x, half = (place + 2 * NZ - k - 2 * t) % NX, (k + o + side) % 2
             value = ref[t, o]
             rows = pl.ds(pl.multiple_of(half * HALF + x * SUB, SUB), SUB)
             high = value.astype(jnp.bfloat16)
@@ -144,11 +144,11 @@
         for x in range(NX):
             block = total[x * SUB : (x + 1) * SUB, :]
             if exact:
-                out_ref[x, y] = block
+                out_ref[y, x] = block
                 continue
             power = exponent(jnp.max(jnp.abs(block), axis=0, keepdims=True))
-            out_ref[x, y, pl.ds(0, SUB), :] = block * jnp.exp2(-power)
-            out_ref[x, y, pl.ds(SUB, 1), :] = power
+            out_ref[y, x, pl.ds(0, SUB), :] = block * jnp.exp2(-power)
+            out_ref[y, x, pl.ds(SUB, 1), :] = power
     if not exact:
         extra_ref = refs[-1]
         extra_ref[...] = jnp.zeros_like(extra_ref)
@@ -166,7 +166,7 @@
             extra_ref[pl.ds(3 * m + 3, 1), :] = (total - high) * 256.0
         for b in range(NX * NY):
             x, y = divmod(b, NY)
-            out_ref[x, y, pl.ds(SUB + 1, extra_ref.shape[0] - 1), :] = extra_ref[pl.ds(1, extra_ref.shape[0] - 1), :]
+            out_ref[y, x, pl.ds(SUB + 1, extra_ref.shape[0] - 1), :] = extra_ref[pl.ds(1, extra_ref.shape[0] - 1), :]
 
 
 def apply_rates(at, kept, got, weights, fields, exact):
@@ -185,7 +185,7 @@
 
     out = call(
         kernel,
-        jax.ShapeDtypeStruct((NX, NY, rows, cells), jnp.float32),
+        jax.ShapeDtypeStruct((NY, NX, rows, cells), jnp.float32),
         at,
         kept,
         got,
@@ -318,7 +318,7 @@
         return own.astype(wide), other.astype(wide)
 
     def reduce(partial):
-        return exchange(partial.astype(WIRE), ("x", "y")).astype(jnp.float32)
+        return exchange(partial.astype(WIRE), ("y", "x")).astype(jnp.float32)
 
     piece = lax.ppermute(populations.astype(jnp.bfloat16), ALL, TO_INNER)
     both = jnp.stack([piece, lax.ppermute(piece, "k", SWAP)])

time: 216 us -> 214 us (level)
  starting transfers between devices: 51 us -> 36.3 us
  blocking collectives: 96 us -> 103 us
  waiting for transfers between devices: 38.1 us -> 44 us
    ppermute x10, starting transfers between devices: 37.2 us -> 10.6 us  [spread(): own = [lax.ppermute(both, ('z', 'k', 'x'), pairs) for pairs in SPREAD]]
    ppermute x5, starting transfers between devices: 1.15 us -> 14.2 us  [spread(): other = lax.ppermute(own, 'k', SWAP)]
    ppermute x10, waiting for transfers between devices: 15.7 us -> 22.7 us  [spread(): own = [lax.ppermute(both, ('z', 'k', 'x'), pairs) for pairs in SPREAD]]
    all_to_all x5, blocking collectives: 96 us -> 103 us  [body(): exchange = lambda v, axes: lax.all_to_all(v, axes, 0, 0, tiled=True)]
where the time goes in v10:
time: 214 us; the launch traced here: 213 us
  blocking collectives  103 us (48%)
  waiting for transfers between devices  44 us (21%)
  starting transfers between devices  36.3 us (17%)
  Pallas kernels  23.1 us (11%)
  local copies, waits for them, and re-layouts  3.83 us (2%)
  other arithmetic  2.45 us (1%)
    all_to_all x5, blocking collectives, body(): exchange = lambda v, axes: lax.all_to_all(v, axes, 0, 0, tiled=True)  103 us
    pallas_call x12, Pallas kernels, call(): pl.pallas_call(kernel, out_shape=outs, in_specs=specs, out_specs=jax.tree...  23.1 us
    ppermute x10, waiting for transfers between devices, spread(): own = [lax.ppermute(both, ('z', 'k', 'x'), pairs) for pairs in SPREAD]  22.7 us
    ppermute x5, starting transfers between devices, spread(): other = lax.ppermute(own, 'k', SWAP)  14.2 us
    all_to_all x1, waiting for transfers between devices, body(): exchange = lambda v, axes: lax.all_to_all(v, axes, 0, 0, tiled=True)  10.9 us
    ppermute x10, starting transfers between devices, spread(): own = [lax.ppermute(both, ('z', 'k', 'x'), pairs) for pairs in SPREAD]  10.6 us
    ppermute x5, starting transfers between devices, body(): both = jnp.stack([piece, lax.ppermute(piece, 'k', SWAP)])  5.44 us
    ppermute x5, waiting for transfers between devices, body(): both = jnp.stack([piece, lax.ppermute(piece, 'k', SWAP)])  4.72 us
  transfers between devices with their start and end apart: 25, of which 16 were waited for; matrix products, arithmetic and copies ran while one was open for 2% of the time, Pallas kernels for 0%

profile of v10, /device:TPU:0, one launch (start us, length us, event | category | flops | bytes accessed | tf_op | source)
XLA Modules:
  0.0 213.3 jit_solution(11530766869862476136)
XLA Ops:
  1.5 5.1 %collective-permute-start.1 = (bf16[64,256]{1,0:T(8,128)(2,1)S(1)}, bf16[64,256]{1,0:T(8,128)(2,1)S(1)}, u32[]{:S(2)}, u32[]{:S(2)}) collective-permute-start(bf16[64,256]{1,0:T(8,128)(2,1)S(1)} %collective-permute-done), channel_id=1, source_target_pairs={{0,16},{16,0},{1,17},{17,1},{2,18},{18,2},{3,19},{19,3},{4,20},{20... | collective-permute-start | bytes 98312 | tf_op jit(solution)/shard_map/ppermute | solution.py:324
  6.6 3.7 %slice_bitcast_fusion = bf16[6,2,256,512]{3,2,1,0:T(8,128)(2,1)} fusion(bf16[6,2,2,256,512]{4,3,2,1,0:T(8,128)(2,1)} %bitcast.40), kind=kLoop, calls=%fused_computation | loop fusion | bytes 6291456 | tf_op jit(solution)/shard_map/squeeze | solution.py:303
  10.5 3.9 %collective-permute-start.4 = (bf16[2,64,256]{2,1,0:T(8,128)(2,1)S(1)}, bf16[2,64,256]{2,1,0:T(8,128)(2,1)S(1)}, u32[]{:S(2)}, u32[]{:S(2)}) collective-permute-start(bf16[2,64,256]{2,1,0:T(8,128)(2,1)S(1)} %pad_maximum_fusion.6), channel_id=1, source_target_pairs={{0,64},{4,96},{8,0},{12,32},{16,112},{20,16},{24,48},{28,80},{32,6... | collective-permute-start | bytes 196616 | tf_op jit(solution)/shard_map/ppermute | solution.py:315
  15.1 5.4 %collective-permute-done.4 = bf16[2,64,256]{2,1,0:T(8,128)(2,1)S(1)} collective-permute-done((bf16[2,64,256]{2,1,0:T(8,128)(2,1)S(1)}, bf16[2,64,256]{2,1,0:T(8,128)(2,1)S(1)}, u32[]{:S(2)}, u32[]{:S(2)}) %collective-permute-start.4) | collective-permute-done | bytes 65568 | tf_op jit(solution)/shard_map/ppermute | solution.py:315
  20.5 1.5 collective-permute-start.5
  23.0 3.7 %shard_map.46 = f32[4,4,64,256]{3,2,1,0:T(8,128)S(1)} custom-call(s32[3]{0:T(128)S(1)} %pad_add_fusion.refs_0_, bf16[6,2,2,256,512]{4,3,2,1,0:T(8,128)(2,1)} %bitcast.41, bf16[6,2,256,512]{3,2,1,0:T(8,128)(2,1)S(1)} %collective-permute-done.2.refs_2_, f32[8,256]{1,0:T(8,128)S(1)} %pad.4.refs_3_, bf16[2,2,64,256]{3,2,1,0:T(8,128)(2,1)S(1)} %pad_maximum_fusion.refs_4_, ...), custom_call_target="tpu_custom_call" | custom-call | tf_op jit(solution)/shard_map/pallas_call | solution.py:90
  26.8 22.1 %all_to_all.30 = f16[16,64,256]{2,1,0:T(8,128)(2,1)S(1)} all-to-all(f16[16,64,256]{2,1,0:T(8,128)(2,1)S(1)} %bitcast.52), channel_id=1, replica_groups=mesh['z'=4,'k'=2,'x'=4,'y'=4] {'y','x'}, dimensions={0} | all-to-all | bytes 1048576 | tf_op jit(solution)/shard_map/all_to_all | solution.py:300
  49.3 1.2 collective-permute-done.6
  50.5 3.1 %collective-permute-start.8 = (f16[2,64,256]{2,1,0:T(8,128)(2,1)S(1)}, f16[2,64,256]{2,1,0:T(8,128)(2,1)S(1)}, u32[]{:S(2)}, u32[]{:S(2)}) collective-permute-start(f16[2,64,256]{2,1,0:T(8,128)(2,1)S(1)} %pad_maximum_fusion.7), channel_id=1, source_target_pairs={{0,64},{4,96},{8,0},{12,32},{16,112},{20,16},{24,48},{28,80},{32,6... | collective-permute-start | bytes 196616 | tf_op jit(solution)/shard_map/ppermute | solution.py:315
  54.3 2.0 collective-permute-done.8
  56.3 4.0 %collective-permute-start.9 = (f16[2,2,64,256]{3,2,1,0:T(8,128)(2,1)S(1)}, f16[2,2,64,256]{3,2,1,0:T(8,128)(2,1)S(1)}, u32[]{:S(2)}, u32[]{:S(2)}) collective-permute-start(f16[2,2,64,256]{3,2,1,0:T(8,128)(2,1)S(1)} %get-tuple-element.45), channel_id=1, source_target_pairs={{0,16},{16,0},{1,17},{17,1},{2,18},{18,2},{3,19},{19,3},{4,20},{20... | collective-permute-start | bytes 393224 | tf_op jit(solution)/shard_map/ppermute | solution.py:317
  60.3 1.0 collective-permute-done.9
  61.4 4.1 %shard_map.48 = f32[4,4,72,256]{3,2,1,0:T(8,128)S(1)} custom-call(s32[3]{0:T(128)S(1)} %pad_add_fusion.refs_0_, bf16[6,2,2,256,512]{4,3,2,1,0:T(8,128)(2,1)S(1)} %bitcast.44, bf16[6,2,256,512]{3,2,1,0:T(8,128)(2,1)S(1)} %collective-permute-done.2.refs_2_, f32[8,256]{1,0:T(8,128)S(1)} %pad.4.refs_3_, f32[2,2,64,256]{3,2,1,0:T(8,128)S(1)} %get-tuple-element.46.refs_4_, ...), custom_call_target="tpu_custom_call" | custom-call | tf_op jit(solution)/shard_map/pallas_call | solution.py:90
  65.6 20.1 %all_to_all.31 = f16[16,72,256]{2,1,0:T(8,128)(2,1)S(1)} all-to-all(f16[16,72,256]{2,1,0:T(8,128)(2,1)S(1)} %bitcast.50), channel_id=1, replica_groups=mesh['z'=4,'k'=2,'x'=4,'y'=4] {'y','x'}, dimensions={0} | all-to-all | bytes 1179648 | tf_op jit(solution)/shard_map/all_to_all | solution.py:300
  86.0 1.2 collective-permute-done.10
  88.0 5.1 %collective-permute-done.12 = f16[2,64,256]{2,1,0:T(8,128)(2,1)S(1)} collective-permute-done((f16[2,64,256]{2,1,0:T(8,128)(2,1)S(1)}, f16[2,64,256]{2,1,0:T(8,128)(2,1)S(1)}, u32[]{:S(2)}, u32[]{:S(2)}) %collective-permute-start.12) | collective-permute-done | bytes 65568 | tf_op jit(solution)/shard_map/ppermute | solution.py:315
  93.1 3.0 %collective-permute-start.13 = (f16[2,2,64,256]{3,2,1,0:T(8,128)(2,1)S(1)}, f16[2,2,64,256]{3,2,1,0:T(8,128)(2,1)S(1)}, u32[]{:S(2)}, u32[]{:S(2)}) collective-permute-start(f16[2,2,64,256]{3,2,1,0:T(8,128)(2,1)S(1)} %get-tuple-element.43), channel_id=1, source_target_pairs={{0,16},{16,0},{1,17},{17,1},{2,18},{18,2},{3,19},{19,3},{4,20},{20... | collective-permute-start | bytes 393224 | tf_op jit(solution)/shard_map/ppermute | solution.py:317
  97.1 4.2 %shard_map.50 = f32[4,4,72,256]{3,2,1,0:T(8,128)S(1)} custom-call(s32[3]{0:T(128)S(1)} %pad_add_fusion.refs_0_, bf16[6,2,2,256,512]{4,3,2,1,0:T(8,128)(2,1)S(1)} %bitcast.45, bf16[6,2,256,512]{3,2,1,0:T(8,128)(2,1)S(1)} %collective-permute-done.2.refs_2_, f32[8,256]{1,0:T(8,128)S(1)} %pad.4.refs_3_, f32[2,2,64,256]{3,2,1,0:T(8,128)S(1)} %get-tuple-element.46.refs_4_, ...), custom_call_target="tpu_custom_call" | custom-call | tf_op jit(solution)/shard_map/pallas_call | solution.py:90
  101.5 19.8 %all_to_all.32 = f16[16,72,256]{2,1,0:T(8,128)(2,1)S(1)} all-to-all(f16[16,72,256]{2,1,0:T(8,128)(2,1)S(1)} %bitcast.51), channel_id=1, replica_groups=mesh['z'=4,'k'=2,'x'=4,'y'=4] {'y','x'}, dimensions={0} | all-to-all | bytes 1179648 | tf_op jit(solution)/shard_map/all_to_all | solution.py:300
  121.7 1.2 collective-permute-done.14
  123.6 5.1 %collective-permute-done.16 = f16[2,64,256]{2,1,0:T(8,128)(2,1)S(1)} collective-permute-done((f16[2,64,256]{2,1,0:T(8,128)(2,1)S(1)}, f16[2,64,256]{2,1,0:T(8,128)(2,1)S(1)}, u32[]{:S(2)}, u32[]{:S(2)}) %collective-permute-start.16) | collective-permute-done | bytes 65568 | tf_op jit(solution)/shard_map/ppermute | solution.py:315
  128.7 2.8 %collective-permute-start.17 = (f16[2,2,64,256]{3,2,1,0:T(8,128)(2,1)S(1)}, f16[2,2,64,256]{3,2,1,0:T(8,128)(2,1)S(1)}, u32[]{:S(2)}, u32[]{:S(2)}) collective-permute-start(f16[2,2,64,256]{3,2,1,0:T(8,128)(2,1)S(1)} %get-tuple-element.41), channel_id=1, source_target_pairs={{0,16},{16,0},{1,17},{17,1},{2,18},{18,2},{3,19},{19,3},{4,20},{20... | collective-permute-start | bytes 393224 | tf_op jit(solution)/shard_map/ppermute | solution.py:317
  132.6 4.3 %shard_map.52 = f32[4,4,80,256]{3,2,1,0:T(8,128)S(1)} custom-call(s32[3]{0:T(128)S(1)} %pad_add_fusion.refs_0_, bf16[6,2,2,256,512]{4,3,2,1,0:T(8,128)(2,1)S(1)} %bitcast.46, bf16[6,2,256,512]{3,2,1,0:T(8,128)(2,1)S(1)} %collective-permute-done.2.refs_2_, f32[8,256]{1,0:T(8,128)S(1)} %pad.4.refs_3_, f32[2,2,64,256]{3,2,1,0:T(8,128)S(1)} %get-tuple-element.46.refs_4_, ...), custom_call_target="tpu_custom_call" | custom-call | tf_op jit(solution)/shard_map/pallas_call | solution.py:90
  137.0 20.5 %all_to_all.33 = f16[16,80,256]{2,1,0:T(8,128)(2,1)S(1)} all-to-all(f16[16,80,256]{2,1,0:T(8,128)(2,1)S(1)} %bitcast.48), channel_id=1, replica_groups=mesh['z'=4,'k'=2,'x'=4,'y'=4] {'y','x'}, dimensions={0} | all-to-all | bytes 1310720 | tf_op jit(solution)/shard_map/all_to_all | solution.py:300
  158.0 1.2 collective-permute-done.18
  159.9 5.1 %collective-permute-done.20 = f16[2,64,256]{2,1,0:T(8,128)(2,1)S(1)} collective-permute-done((f16[2,64,256]{2,1,0:T(8,128)(2,1)S(1)}, f16[2,64,256]{2,1,0:T(8,128)(2,1)S(1)}, u32[]{:S(2)}, u32[]{:S(2)}) %collective-permute-start.20) | collective-permute-done | bytes 65568 | tf_op jit(solution)/shard_map/ppermute | solution.py:315
  165.1 2.9 %collective-permute-start.21 = (f16[2,2,64,256]{3,2,1,0:T(8,128)(2,1)S(1)}, f16[2,2,64,256]{3,2,1,0:T(8,128)(2,1)S(1)}, u32[]{:S(2)}, u32[]{:S(2)}) collective-permute-start(f16[2,2,64,256]{3,2,1,0:T(8,128)(2,1)S(1)} %get-tuple-element.39), channel_id=1, source_target_pairs={{0,16},{16,0},{1,17},{17,1},{2,18},{18,2},{3,19},{19,3},{4,20},{20... | collective-permute-start | bytes 393224 | tf_op jit(solution)/shard_map/ppermute | solution.py:317
  169.0 4.4 %shard_map.54 = f32[4,4,80,256]{3,2,1,0:T(8,128)S(1)} custom-call(s32[3]{0:T(128)S(1)} %pad_add_fusion.refs_0_, bf16[6,2,2,256,512]{4,3,2,1,0:T(8,128)(2,1)S(1)} %bitcast.47, bf16[6,2,256,512]{3,2,1,0:T(8,128)(2,1)S(1)} %collective-permute-done.2.refs_2_, f32[8,256]{1,0:T(8,128)S(1)} %pad.4.refs_3_, f32[2,2,64,256]{3,2,1,0:T(8,128)S(1)} %get-tuple-element.46.refs_4_, ...), custom_call_target="tpu_custom_call" | custom-call | tf_op jit(solution)/shard_map/pallas_call | solution.py:90
  173.6 20.4 %all_to_all.34 = f16[16,80,256]{2,1,0:T(8,128)(2,1)S(1)} all-to-all(f16[16,80,256]{2,1,0:T(8,128)(2,1)S(1)} %bitcast.49), channel_id=1, replica_groups=mesh['z'=4,'k'=2,'x'=4,'y'=4] {'y','x'}, dimensions={0} | all-to-all | bytes 1310720 | tf_op jit(solution)/shard_map/all_to_all | solution.py:300
  194.4 1.2 collective-permute-done.23.other_ref
  196.3 4.6 %all-to-all-start.5 = ((f32[64,8,128]{2,1,0:T(8,128)}), f32[64,8,128]{2,1,0:T(8,128)S(1)}, u32[]{:S(2)}, u32[]{:S(2)}) async-start(f32[64,8,128]{2,1,0:T(8,128)} %shard_map.56), calls=%async_computation.5 | async-start | bytes 524288 | tf_op jit(solution)/shard_map/all_to_all | solution.py:300
  201.6 10.9 %all-to-all-done.5.dots_ref = f32[64,8,128]{2,1,0:T(8,128)S(1)} async-done(((f32[64,8,128]{2,1,0:T(8,128)}), f32[64,8,128]{2,1,0:T(8,128)S(1)}, u32[]{:S(2)}, u32[]{:S(2)}) %all-to-all-start.5) | async-done | bytes 262176 | tf_op jit(solution)/shard_map/all_to_all | solution.py:300
  (86 shorter events, 13.9 us)
Async XLA Ops:
  0.0 22.0 %copy-start = (f32[64,6]{0,1:T(8,128)S(1)}, f32[64,6]{0,1:T(8,128)}, u32[]{:S(2)}) copy-start(f32[64,6]{0,1:T(8,128)} %param.7) | copy-start | bytes 4612
  0.9 0.7 collective-permute-start
  1.5 8.8 %collective-permute-start.1 = (bf16[64,256]{1,0:T(8,128)(2,1)S(1)}, bf16[64,256]{1,0:T(8,128)(2,1)S(1)}, u32[]{:S(2)}, u32[]{:S(2)}) collective-permute-start(bf16[64,256]{1,0:T(8,128)(2,1)S(1)} %collective-permute-done), channel_id=1, source_target_pairs={{0,16},{16,0},{1,17},{17,1},{2,18},{18,2},{3,19},{19,3},{4,20},{20... | collective-permute-start | bytes 98312 | tf_op jit(solution)/shard_map/ppermute | solution.py:324
  6.6 15.4 %copy-start.2 = (s32[256]{0:T(256)S(1)}, s32[256]{0:T(256)}, u32[]{:S(2)}) copy-start(s32[256]{0:T(256)} %param.6) | copy-start | bytes 3076
  10.4 12.6 %collective-permute-start.2 = (bf16[6,2,256,512]{3,2,1,0:T(8,128)(2,1)}, bf16[6,2,256,512]{3,2,1,0:T(8,128)(2,1)S(1)}, u32[]{:S(2)}, u32[]{:S(2)}) collective-permute-start(bf16[6,2,256,512]{3,2,1,0:T(8,128)(2,1)} %slice_bitcast_fusion), channel_id=1, source_target_pairs={{0,16},{16,0},{1,17},{17,1},{2,18},{18,2},{3,19},{19,3},{4,20},{20... | collective-permute-start | bytes 9437192 | tf_op jit(solution)/shard_map/ppermute | solution.py:326
  10.5 10.0 %collective-permute-start.4 = (bf16[2,64,256]{2,1,0:T(8,128)(2,1)S(1)}, bf16[2,64,256]{2,1,0:T(8,128)(2,1)S(1)}, u32[]{:S(2)}, u32[]{:S(2)}) collective-permute-start(bf16[2,64,256]{2,1,0:T(8,128)(2,1)S(1)} %pad_maximum_fusion.6), channel_id=1, source_target_pairs={{0,64},{4,96},{8,0},{12,32},{16,112},{20,16},{24,48},{28,80},{32,6... | collective-permute-start | bytes 196616 | tf_op jit(solution)/shard_map/ppermute | solution.py:315
  14.4 6.1 %collective-permute-start.3 = (bf16[2,64,256]{2,1,0:T(8,128)(2,1)S(1)}, bf16[2,64,256]{2,1,0:T(8,128)(2,1)S(1)}, u32[]{:S(2)}, u32[]{:S(2)}) collective-permute-start(bf16[2,64,256]{2,1,0:T(8,128)(2,1)S(1)} %pad_maximum_fusion.6), channel_id=1, source_target_pairs={{0,0},{4,32},{8,64},{12,96},{16,48},{20,80},{24,112},{28,16},{32,4... | collective-permute-start | bytes 196616 | tf_op jit(solution)/shard_map/ppermute | solution.py:315
  20.5 2.5 %collective-permute-start.5 = (bf16[2,2,64,256]{3,2,1,0:T(8,128)(2,1)S(1)}, bf16[2,2,64,256]{3,2,1,0:T(8,128)(2,1)S(1)}, u32[]{:S(2)}, u32[]{:S(2)}) collective-permute-start(bf16[2,2,64,256]{3,2,1,0:T(8,128)(2,1)S(1)} %pad_maximum_fusion.refs_4_), channel_id=1, source_target_pairs={{0,16},{16,0},{1,17},{17,1},{2,18},{18,2},{3,19},{19,3},{4,20},{20... | collective-permute-start | bytes 393224 | tf_op jit(solution)/shard_map/ppermute | solution.py:317
  22.2 39.2 %slice-start = ((s8[6291456]{0:T(1024)(128)(4,1)}), s8[4194304]{0:T(1024)(128)(4,1)S(1)}, s32[]{:S(2)}) async-start(s8[6291456]{0:T(1024)(128)(4,1)} %bitcast.42), calls=%async_computation.6 | async-start | bytes 8388608
  22.4 39.0 %slice-start.1 = ((s8[6291456]{0:T(1024)(128)(4,1)}), s8[2097152]{0:T(1024)(128)(4,1)S(1)}, s32[]{:S(2)}) async-start(s8[6291456]{0:T(1024)(128)(4,1)} %bitcast.42), calls=%async_computation.7 | async-start | bytes 4194304
  49.1 1.3 collective-permute-start.6
  50.5 5.8 %collective-permute-start.8 = (f16[2,64,256]{2,1,0:T(8,128)(2,1)S(1)}, f16[2,64,256]{2,1,0:T(8,128)(2,1)S(1)}, u32[]{:S(2)}, u32[]{:S(2)}) collective-permute-start(f16[2,64,256]{2,1,0:T(8,128)(2,1)S(1)} %pad_maximum_fusion.7), channel_id=1, source_target_pairs={{0,64},{4,96},{8,0},{12,32},{16,112},{20,16},{24,48},{28,80},{32,6... | collective-permute-start | bytes 196616 | tf_op jit(solution)/shard_map/ppermute | solution.py:315
  53.6 2.7 %collective-permute-start.7 = (f16[2,64,256]{2,1,0:T(8,128)(2,1)S(1)}, f16[2,64,256]{2,1,0:T(8,128)(2,1)S(1)}, u32[]{:S(2)}, u32[]{:S(2)}) collective-permute-start(f16[2,64,256]{2,1,0:T(8,128)(2,1)S(1)} %pad_maximum_fusion.7), channel_id=1, source_target_pairs={{0,0},{4,32},{8,64},{12,96},{16,48},{20,80},{24,112},{28,16},{32,4... | collective-permute-start | bytes 196616 | tf_op jit(solution)/shard_map/ppermute | solution.py:315
  56.3 5.0 %collective-permute-start.9 = (f16[2,2,64,256]{3,2,1,0:T(8,128)(2,1)S(1)}, f16[2,2,64,256]{3,2,1,0:T(8,128)(2,1)S(1)}, u32[]{:S(2)}, u32[]{:S(2)}) collective-permute-start(f16[2,2,64,256]{3,2,1,0:T(8,128)(2,1)S(1)} %get-tuple-element.45), channel_id=1, source_target_pairs={{0,16},{16,0},{1,17},{17,1},{2,18},{18,2},{3,19},{19,3},{4,20},{20... | collective-permute-start | bytes 393224 | tf_op jit(solution)/shard_map/ppermute | solution.py:317
  85.9 1.3 collective-permute-start.10
  87.3 5.8 %collective-permute-start.12 = (f16[2,64,256]{2,1,0:T(8,128)(2,1)S(1)}, f16[2,64,256]{2,1,0:T(8,128)(2,1)S(1)}, u32[]{:S(2)}, u32[]{:S(2)}) collective-permute-start(f16[2,64,256]{2,1,0:T(8,128)(2,1)S(1)} %pad_maximum_fusion.8), channel_id=1, source_target_pairs={{0,64},{4,96},{8,0},{12,32},{16,112},{20,16},{24,48},{28,80},{32,6... | collective-permute-start | bytes 196616 | tf_op jit(solution)/shard_map/ppermute | solution.py:315
  87.3 5.8 %collective-permute-start.11 = (f16[2,64,256]{2,1,0:T(8,128)(2,1)S(1)}, f16[2,64,256]{2,1,0:T(8,128)(2,1)S(1)}, u32[]{:S(2)}, u32[]{:S(2)}) collective-permute-start(f16[2,64,256]{2,1,0:T(8,128)(2,1)S(1)} %pad_maximum_fusion.8), channel_id=1, source_target_pairs={{0,0},{4,32},{8,64},{12,96},{16,48},{20,80},{24,112},{28,16},{32,4... | collective-permute-start | bytes 196616 | tf_op jit(solution)/shard_map/ppermute | solution.py:315
  93.1 4.0 %collective-permute-start.13 = (f16[2,2,64,256]{3,2,1,0:T(8,128)(2,1)S(1)}, f16[2,2,64,256]{3,2,1,0:T(8,128)(2,1)S(1)}, u32[]{:S(2)}, u32[]{:S(2)}) collective-permute-start(f16[2,2,64,256]{3,2,1,0:T(8,128)(2,1)S(1)} %get-tuple-element.43), channel_id=1, source_target_pairs={{0,16},{16,0},{1,17},{17,1},{2,18},{18,2},{3,19},{19,3},{4,20},{20... | collective-permute-start | bytes 393224 | tf_op jit(solution)/shard_map/ppermute | solution.py:317
  121.5 1.3 collective-permute-start.14
  122.9 5.8 %collective-permute-start.16 = (f16[2,64,256]{2,1,0:T(8,128)(2,1)S(1)}, f16[2,64,256]{2,1,0:T(8,128)(2,1)S(1)}, u32[]{:S(2)}, u32[]{:S(2)}) collective-permute-start(f16[2,64,256]{2,1,0:T(8,128)(2,1)S(1)} %pad_maximum_fusion.9), channel_id=1, source_target_pairs={{0,64},{4,96},{8,0},{12,32},{16,112},{20,16},{24,48},{28,80},{32,6... | collective-permute-start | bytes 196616 | tf_op jit(solution)/shard_map/ppermute | solution.py:315
  122.9 5.8 %collective-permute-start.15 = (f16[2,64,256]{2,1,0:T(8,128)(2,1)S(1)}, f16[2,64,256]{2,1,0:T(8,128)(2,1)S(1)}, u32[]{:S(2)}, u32[]{:S(2)}) collective-permute-start(f16[2,64,256]{2,1,0:T(8,128)(2,1)S(1)} %pad_maximum_fusion.9), channel_id=1, source_target_pairs={{0,0},{4,32},{8,64},{12,96},{16,48},{20,80},{24,112},{28,16},{32,4... | collective-permute-start | bytes 196616 | tf_op jit(solution)/shard_map/ppermute | solution.py:315
  128.7 3.8 %collective-permute-start.17 = (f16[2,2,64,256]{3,2,1,0:T(8,128)(2,1)S(1)}, f16[2,2,64,256]{3,2,1,0:T(8,128)(2,1)S(1)}, u32[]{:S(2)}, u32[]{:S(2)}) collective-permute-start(f16[2,2,64,256]{3,2,1,0:T(8,128)(2,1)S(1)} %get-tuple-element.41), channel_id=1, source_target_pairs={{0,16},{16,0},{1,17},{17,1},{2,18},{18,2},{3,19},{19,3},{4,20},{20... | collective-permute-start | bytes 393224 | tf_op jit(solution)/shard_map/ppermute | solution.py:317
  157.9 1.3 collective-permute-start.18
  159.2 5.8 %collective-permute-start.20 = (f16[2,64,256]{2,1,0:T(8,128)(2,1)S(1)}, f16[2,64,256]{2,1,0:T(8,128)(2,1)S(1)}, u32[]{:S(2)}, u32[]{:S(2)}) collective-permute-start(f16[2,64,256]{2,1,0:T(8,128)(2,1)S(1)} %pad_maximum_fusion.10), channel_id=1, source_target_pairs={{0,64},{4,96},{8,0},{12,32},{16,112},{20,16},{24,48},{28,80},{32,6... | collective-permute-start | bytes 196616 | tf_op jit(solution)/shard_map/ppermute | solution.py:315
  159.2 5.8 %collective-permute-start.19 = (f16[2,64,256]{2,1,0:T(8,128)(2,1)S(1)}, f16[2,64,256]{2,1,0:T(8,128)(2,1)S(1)}, u32[]{:S(2)}, u32[]{:S(2)}) collective-permute-start(f16[2,64,256]{2,1,0:T(8,128)(2,1)S(1)} %pad_maximum_fusion.10), channel_id=1, source_target_pairs={{0,0},{4,32},{8,64},{12,96},{16,48},{20,80},{24,112},{28,16},{32,4... | collective-permute-start | bytes 196616 | tf_op jit(solution)/shard_map/ppermute | solution.py:315
  165.1 3.9 %collective-permute-start.21 = (f16[2,2,64,256]{3,2,1,0:T(8,128)(2,1)S(1)}, f16[2,2,64,256]{3,2,1,0:T(8,128)(2,1)S(1)}, u32[]{:S(2)}, u32[]{:S(2)}) collective-permute-start(f16[2,2,64,256]{3,2,1,0:T(8,128)(2,1)S(1)} %get-tuple-element.39), channel_id=1, source_target_pairs={{0,16},{16,0},{1,17},{17,1},{2,18},{18,2},{3,19},{19,3},{4,20},{20... | collective-permute-start | bytes 393224 | tf_op jit(solution)/shard_map/ppermute | solution.py:317
  194.0 18.4 %copy-start.1 = (f32[64,256]{1,0:T(8,128)S(1)}, f32[64,256]{1,0:T(8,128)}, u32[]{:S(2)}) copy-start(f32[64,256]{1,0:T(8,128)} %p_ref.1) | copy-start | bytes 196612
  194.3 1.2 collective-permute-start.23
  196.3 16.2 %all-to-all-start.5 = ((f32[64,8,128]{2,1,0:T(8,128)}), f32[64,8,128]{2,1,0:T(8,128)S(1)}, u32[]{:S(2)}, u32[]{:S(2)}) async-start(f32[64,8,128]{2,1,0:T(8,128)} %shard_map.56), calls=%async_computation.5 | async-start | bytes 524288 | tf_op jit(solution)/shard_map/all_to_all | solution.py:300
  200.9 0.7 collective-permute-start.22
